TPU v7x, 512 devices: a whole 4x4x16 slice. The times are simulated.
512 devices in a mesh: gx: 32 (over x, y, core), gy: 16 (over z).
Axes of the slice: x: 4, y: 4, z: 16, core: 2. Of those that a mesh axis runs over, the one named last changes fastest.
Arguments:
- schur_blocks: float32 [32, 16, 768, 768], P('gx', 'gy'), may hold values from -32 to 32, as said below
- basis: float32 [32, 16, 32, 768], P('gx', 'gy'), may hold values from -0.21875 to 0.21875
- loads: float32 [32, 16, 16, 768], P('gx', 'gy'), may hold values from -64 to 64
- coarse_inverse: float32 [16384, 16384], P(('gx', 'gy')), may hold values from -0.09375 to 0.09375
- iface_map: int32 [32, 16, 768], P('gx', 'gy'), may hold values from 0 to 767, as said below
- coarse_slot: int32 [512], replicated, may hold values from 0 to 511, each once
Outputs:
- solution: float32 [32, 16, 16, 768], P('gx', 'gy')
Inputs may be any that keep to these rules, and one draw needn't show every extreme that they name: `schur_blocks`: each block is symmetric. `iface_map`: for every subdomain the map is a permutation of 0 to 767 that maps each aligned block of 128 cells onto itself. `coarse_slot`: every subdomain has its own coarse block number.
All inputs are finite; a program needn't handle non-finite values.
Results may differ from a plain program's by a relative error of at most 0.0001.
Values sent between devices are 32-bit elements; how exact they have to be, the bound alone decides.
No kernel may reach another device: no remote copies, remote signals or barrier semaphores. Data moves between devices by JAX's collectives and lax.ppermute only.
A program may use at most 128 MiB of HBM per device.

v0:
```python
import jax
import jax.numpy as jnp
from jax import lax
from jax.sharding import PartitionSpec as P

EW = 256
ES = 128
ITERS = 3


highest = lax.Precision.HIGHEST
epsilon = 1e-06


def padded(block, sides, width):
    for axis, dim in sides:
        count = lax.axis_size(axis)
        forward = [(i, i + 1) for i in range(count - 1)]
        backward = [(target, source) for source, target in forward]
        low = lax.ppermute(
            lax.slice_in_dim(block, block.shape[dim] - width, None, axis=dim), axis, forward
        )
        high = lax.ppermute(lax.slice_in_dim(block, 0, width, axis=dim), axis, backward)
        block = jnp.concatenate([low, block, high], axis=dim)
    return block


def edge_stacks(layout):
    column_edges = jnp.stack([layout[:, :EW], layout[:, EW : 2 * EW]])
    row_edges = jnp.stack([layout[:, 2 * EW : 2 * EW + ES], layout[:, 2 * EW + ES :]])
    return (column_edges, row_edges)


def add_edges(values, position, across, along):
    outside = jnp.concatenate([across[0], across[3], along[0], along[3]], axis=1)
    return values + jnp.take(outside, position, axis=1)


def assemble(values, position, inverse):
    column_edges, row_edges = edge_stacks(jnp.take(values, inverse, axis=1))
    across = padded(column_edges, (("gy", 0),), 1)
    along = padded(row_edges, (("gx", 0),), 1)
    return add_edges(values, position, across, along)


def per_device(schur_blocks, basis, loads, coarse_inverse, iface_map, coarse_slot):
    schur_block = schur_blocks[0, 0]
    local_basis = basis[0, 0]
    position = iface_map[0, 0]
    inverse = jnp.argsort(position)
    mode_count = local_basis.shape[0]
    domain_count = coarse_slot.shape[0]
    reordered = jnp.take(
        coarse_inverse.reshape(mode_count, domain_count, mode_count), coarse_slot, axis=1
    )
    reordered = reordered.reshape(mode_count, domain_count * mode_count)
    residual = assemble(loads[0, 0], position, inverse)
    solution = jnp.zeros_like(residual)
    for iteration in range(ITERS):
        lifted = lax.dot_general(
            lax.all_gather(
                lax.dot_general(
                    residual,
                    local_basis,
                    (((1,), (1,)), ((), ())),
                    precision=highest,
                    preferred_element_type=jnp.float32,
                ),
                ("gx", "gy"),
                axis=1,
                tiled=True,
            ),
            reordered,
            (((1,), (1,)), ((), ())),
            precision=highest,
            preferred_element_type=jnp.float32,
        )
        spread = jnp.dot(lifted, local_basis, precision=highest, preferred_element_type=jnp.float32)
        column_edges, row_edges = edge_stacks(jnp.take(spread, inverse, axis=1))
        across = padded(column_edges, (("gy", 0),), 1)
        along = padded(row_edges, (("gx", 0),), 1)
        search = residual + add_edges(spread, position, across, along)
        local_image = jnp.dot(
            search, schur_block, precision=highest, preferred_element_type=jnp.float32
        )
        applied = assemble(local_image, position, inverse)
        totals = lax.psum(
            (jnp.sum(residual * applied, axis=1), jnp.sum(applied * applied, axis=1)), ("gx", "gy")
        )
        stride = (totals[0] / (totals[1] + epsilon))[:, None]
        solution = solution + stride * search
        residual = residual - stride * applied
    return solution[None, None]


def solution(mesh):
    placed = (
        P("gx", "gy", None, None),
        P("gx", "gy", None, None),
        P("gx", "gy", None, None),
        P(("gx", "gy"), None),
        P("gx", "gy", None),
        P(),
    )
    return jax.shard_map(
        per_device, mesh=mesh, in_specs=placed, out_specs=P("gx", "gy", None, None), check_vma=False
    )
```

profile of v0, /device:TPU:1, one launch (start us, length us, event | category | flops | bytes accessed | tf_op | source)
XLA Modules:
  0.0 1102.6 jit_solution(14531170180641245100)
XLA Ops:
  7.4 4.4 sort.17
  14.6 4.4 collective-permute-start
  20.3 4.0 collective-permute-start.2
  24.3 2.9 collective-permute-start.3
  27.3 2.6 collective-permute-done.3
  32.6 6.4 reshape.19
  39.0 11.5 %copy.97 = f32[32,512,32]{2,0,1:T(8,128)} copy(f32[32,512,32]{2,1,0:T(8,128)} %reshape.19) | data formatting | bytes 4194304 | tf_op jit(solution)/shard_map/reshape | solution.py:54
  50.5 7.7 gather_fusion
  58.3 11.5 %copy.98 = f32[32,512,32]{2,1,0:T(8,128)} copy(f32[32,512,32]{2,0,1:T(8,128)} %bitcast.179) | data formatting | bytes 4194304 | tf_op jit(solution)/shard_map/jit(_take)/gather | solution.py:53
  69.8 7.5 gather.10
  78.2 160.2 %all-gather.7.cloned.1.call-done = f32[512,32,16]{1,2,0:T(8,128)} async-done(((f32[1,32,16]{1,2,0:T(8,128)}), f32[512,32,16]{1,2,0:T(8,128)}) %all-gather.7.cloned.1.call-update) | async-done | bytes 1048592 | tf_op jit(solution)/shard_map/all_gather | solution.py:61
  238.4 5.5 copy.96
  243.9 3.5 reshape.156
  247.4 3.3 fusion.10
  253.9 3.2 collective-permute-start.4
  258.4 3.4 collective-permute-start.6
  261.8 1.9 collective-permute-start.7
  263.7 3.6 collective-permute-done.7
  272.4 4.3 collective-permute-start.8
  278.0 2.1 collective-permute-start.10
  280.2 2.2 collective-permute-start.11
  282.4 3.4 collective-permute-done.11
  287.6 106.4 %all-reduce.2 = (f32[16]{0:T(128)S(1)}, f32[16]{0:T(128)S(1)}) all-reduce(f32[16]{0:T(128)S(1)} %get-tuple-element.13, f32[16]{0:T(128)S(1)} %get-tuple-element.12), channel_id=1, replica_groups=mesh['gx'=32,'gy'=16] {'gx','gy'}, use_global_device_ids=true, to_apply=%region_2.4 | all-reduce | flops 32 | bytes 256 | tf_op jit(solution)/shard_map/psum | solution.py:87
  395.6 193.8 %all-gather.9.cloned.1.call-done = f32[512,32,16]{1,2,0:T(8,128)} async-done(((f32[1,32,16]{1,2,0:T(8,128)}), f32[512,32,16]{1,2,0:T(8,128)}) %all-gather.9.cloned.1.call-update) | async-done | bytes 1048592 | tf_op jit(solution)/shard_map/all_gather | solution.py:61
  589.5 5.6 copy.103
  595.0 3.7 reshape.158
  598.7 3.3 fusion.8
  604.2 3.0 collective-permute-start.12
  608.6 3.6 collective-permute-start.14
  612.1 1.9 collective-permute-start.15
  614.1 3.6 collective-permute-done.15
  622.7 4.3 collective-permute-start.16
  628.3 2.1 collective-permute-start.18
  630.5 2.2 collective-permute-start.19
  632.7 3.4 collective-permute-done.19
  637.9 106.4 %all-reduce.1 = (f32[16]{0:T(128)S(1)}, f32[16]{0:T(128)S(1)}) all-reduce(f32[16]{0:T(128)S(1)} %get-tuple-element.11, f32[16]{0:T(128)S(1)} %get-tuple-element.10), channel_id=1, replica_groups=mesh['gx'=32,'gy'=16] {'gx','gy'}, use_global_device_ids=true, to_apply=%region_6.8 | all-reduce | flops 32 | bytes 256 | tf_op jit(solution)/shard_map/psum | solution.py:87
  745.3 193.9 %all-gather.11.cloned.1.call-done = f32[512,32,16]{1,2,0:T(8,128)} async-done(((f32[1,32,16]{1,2,0:T(8,128)}), f32[512,32,16]{1,2,0:T(8,128)}) %all-gather.11.cloned.1.call-update) | async-done | bytes 1048592 | tf_op jit(solution)/shard_map/all_gather | solution.py:61
  939.2 5.6 copy.108
  944.7 3.5 reshape.160
  948.2 3.3 fusion.6
  954.7 3.0 collective-permute-start.20
  959.3 3.6 collective-permute-start.22
  964.8 3.6 collective-permute-done.23
  973.4 4.3 collective-permute-start.24
  979.0 2.1 collective-permute-start.26
  981.2 2.2 collective-permute-start.27
  983.4 3.4 collective-permute-done.27
  988.6 106.4 %all-reduce = (f32[16]{0:T(128)S(1)}, f32[16]{0:T(128)S(1)}) all-reduce(f32[16]{0:T(128)S(1)} %get-tuple-element.9, f32[16]{0:T(128)S(1)} %get-tuple-element.8), channel_id=1, replica_groups=mesh['gx'=32,'gy'=16] {'gx','gy'}, use_global_device_ids=true, to_apply=%region_10.12 | all-reduce | flops 32 | bytes 256 | tf_op jit(solution)/shard_map/psum | solution.py:87
  (188 shorter events, 50.2 us)
Async XLA Ops:
  6.5 262.7 %copy-start = (f32[1,1,768,768]{3,2,1,0:T(8,128)S(1)}, f32[1,1,768,768]{3,2,1,0:T(8,128)}, u32[]{:S(2)}) copy-start(f32[1,1,768,768]{3,2,1,0:T(8,128)} %param.8) | copy-start | bytes 7077892
  6.5 25.1 %copy-start.17 = (f32[1,1,16,768]{3,2,1,0:T(8,128)S(1)}, f32[1,1,16,768]{3,2,1,0:T(8,128)}, u32[]{:S(2)}) copy-start(f32[1,1,16,768]{3,2,1,0:T(8,128)} %param.10) | copy-start | bytes 147460
  6.5 25.2 %copy-start.1 = (f32[1,1,32,768]{3,2,1,0:T(8,128)S(1)}, f32[1,1,32,768]{3,2,1,0:T(8,128)}, u32[]{:S(2)}) copy-start(f32[1,1,32,768]{3,2,1,0:T(8,128)} %param.9) | copy-start | bytes 294916
  6.5 231.9 %all-gather.7.cloned.1.call-start = ((), (), s32[]{:S(2)}) async-start(), calls=%async_computation | async-start | bytes 4202496 | tf_op jit(solution)/shard_map/all_gather | solution.py:61
  11.8 15.5 %copy-start.12 = (s32[1024]{0:T(1024)}, s32[1024]{0:T(1024)S(1)}, u32[]{:S(2)}) copy-start(s32[1024]{0:T(1024)S(1)} %pad_clamp_fusion.2) | copy-start | bytes 12292
  14.6 15.3 %collective-permute-start = (f32[1,16,256]{1,2,0:T(8,128)S(1)}, f32[1,16,256]{1,2,0:T(8,128)S(1)}, u32[]{:S(2)}, u32[]{:S(2)}) collective-permute-start(f32[1,16,256]{1,2,0:T(8,128)S(1)} %get-tuple-element.46), channel_id=1, source_target_pairs={{0,1},{1,2},{2,3},{3,4},{4,5},{5,6},{6,7},{7,8},{8,9},{9,10},{10,1... | collective-permute-start | bytes 49160 | tf_op jit(solution)/shard_map/ppermute | solution.py:20
  19.0 11.0 collective-permute-start.1
  20.3 7.1 collective-permute-start.2
  24.3 5.6 collective-permute-start.3
  32.5 556.9 %all-gather.9.cloned.1.call-start = ((), (), s32[]{:S(2)}) async-start(), calls=%async_computation.1 | async-start | bytes 4202496 | tf_op jit(solution)/shard_map/all_gather | solution.py:61
  250.8 16.7 %copy-start.9 = (s32[1024]{0:T(1024)S(1)}, s32[1024]{0:T(1024)}, u32[]{:S(2)}) copy-start(s32[1024]{0:T(1024)} %copy-done.8) | copy-start | bytes 12292
  250.8 18.4 %copy-start.19 = (pred[768]{0:T(1024)(128)(4,1)S(1)}, pred[768]{0:T(1024)(128)(4,1)}, u32[]{:S(2)}) copy-start(pred[768]{0:T(1024)(128)(4,1)} %copy-done.18) | copy-start | bytes 2308
  253.9 13.5 %collective-permute-start.4 = (f32[1,16,256]{1,2,0:T(8,128)S(1)}, f32[1,16,256]{1,2,0:T(8,128)S(1)}, u32[]{:S(2)}, u32[]{:S(2)}) collective-permute-start(f32[1,16,256]{1,2,0:T(8,128)S(1)} %get-tuple-element.42), channel_id=1, source_target_pairs={{0,1},{1,2},{2,3},{3,4},{4,5},{5,6},{6,7},{7,8},{8,9},{9,10},{10,1... | collective-permute-start | bytes 49160 | tf_op jit(solution)/shard_map/ppermute | solution.py:20
  257.0 10.3 collective-permute-start.5
  258.4 5.4 collective-permute-start.6
  261.8 5.6 collective-permute-start.7
  272.4 13.3 %collective-permute-start.8 = (f32[1,16,256]{1,2,0:T(8,128)S(1)}, f32[1,16,256]{1,2,0:T(8,128)S(1)}, u32[]{:S(2)}, u32[]{:S(2)}) collective-permute-start(f32[1,16,256]{1,2,0:T(8,128)S(1)} %get-tuple-element.38), channel_id=1, source_target_pairs={{0,1},{1,2},{2,3},{3,4},{4,5},{5,6},{6,7},{7,8},{8,9},{9,10},{10,1... | collective-permute-start | bytes 49160 | tf_op jit(solution)/shard_map/ppermute | solution.py:20
  276.7 9.1 collective-permute-start.9
  278.0 4.3 collective-permute-start.10
  280.2 5.6 collective-permute-start.11
  394.1 195.4 %copy-start.27 = (f32[16]{0:T(128)}, f32[16]{0:T(128)S(1)}, u32[]{:S(2)}) copy-start(f32[16]{0:T(128)S(1)} %add_divide_fusion.2) | copy-start | bytes 196
  395.6 543.6 %all-gather.11.cloned.1.call-start = ((), (), s32[]{:S(2)}) async-start(), calls=%async_computation.2 | async-start | bytes 4202496 | tf_op jit(solution)/shard_map/all_gather | solution.py:61
  602.0 15.7 %copy-start.10 = (s32[1024]{0:T(1024)S(1)}, s32[1024]{0:T(1024)}, u32[]{:S(2)}) copy-start(s32[1024]{0:T(1024)} %copy-done.8) | copy-start | bytes 12292
  602.0 17.5 %copy-start.3 = (f32[16,768]{1,0:T(8,128)S(1)}, f32[16,768]{1,0:T(8,128)}, u32[]{:S(2)}) copy-start(f32[16,768]{1,0:T(8,128)} %copy-done.2) | copy-start | bytes 147460
  602.1 17.4 %copy-start.20 = (pred[768]{0:T(1024)(128)(4,1)S(1)}, pred[768]{0:T(1024)(128)(4,1)}, u32[]{:S(2)}) copy-start(pred[768]{0:T(1024)(128)(4,1)} %copy-done.18) | copy-start | bytes 2308
  604.2 13.5 %collective-permute-start.12 = (f32[1,16,256]{1,2,0:T(8,128)S(1)}, f32[1,16,256]{1,2,0:T(8,128)S(1)}, u32[]{:S(2)}, u32[]{:S(2)}) collective-permute-start(f32[1,16,256]{1,2,0:T(8,128)S(1)} %get-tuple-element.34), channel_id=1, source_target_pairs={{0,1},{1,2},{2,3},{3,4},{4,5},{5,6},{6,7},{7,8},{8,9},{9,10},{10,1... | collective-permute-start | bytes 49160 | tf_op jit(solution)/shard_map/ppermute | solution.py:20
  607.3 10.5 collective-permute-start.13
  608.6 5.5 collective-permute-start.14
  612.1 5.6 collective-permute-start.15
  622.7 13.4 %collective-permute-start.16 = (f32[1,16,256]{1,2,0:T(8,128)S(1)}, f32[1,16,256]{1,2,0:T(8,128)S(1)}, u32[]{:S(2)}, u32[]{:S(2)}) collective-permute-start(f32[1,16,256]{1,2,0:T(8,128)S(1)} %get-tuple-element.30), channel_id=1, source_target_pairs={{0,1},{1,2},{2,3},{3,4},{4,5},{5,6},{6,7},{7,8},{8,9},{9,10},{10,1... | collective-permute-start | bytes 49160 | tf_op jit(solution)/shard_map/ppermute | solution.py:20
  627.0 9.1 collective-permute-start.17
  628.3 4.3 collective-permute-start.18
  630.5 5.6 collective-permute-start.19
  744.4 194.8 %copy-start.29 = (f32[16]{0:T(128)}, f32[16]{0:T(128)S(1)}, u32[]{:S(2)}) copy-start(f32[16]{0:T(128)S(1)} %add_divide_fusion.1) | copy-start | bytes 196
  951.6 16.9 %copy-start.11 = (s32[1024]{0:T(1024)S(1)}, s32[1024]{0:T(1024)}, u32[]{:S(2)}) copy-start(s32[1024]{0:T(1024)} %copy-done.8) | copy-start | bytes 12292
  951.8 18.4 %copy-start.21 = (pred[768]{0:T(1024)(128)(4,1)S(1)}, pred[768]{0:T(1024)(128)(4,1)}, u32[]{:S(2)}) copy-start(pred[768]{0:T(1024)(128)(4,1)} %copy-done.18) | copy-start | bytes 2308
  954.7 13.7 %collective-permute-start.20 = (f32[1,16,256]{1,2,0:T(8,128)S(1)}, f32[1,16,256]{1,2,0:T(8,128)S(1)}, u32[]{:S(2)}, u32[]{:S(2)}) collective-permute-start(f32[1,16,256]{1,2,0:T(8,128)S(1)} %get-tuple-element.26), channel_id=1, source_target_pairs={{0,1},{1,2},{2,3},{3,4},{4,5},{5,6},{6,7},{7,8},{8,9},{9,10},{10,1... | collective-permute-start | bytes 49160 | tf_op jit(solution)/shard_map/ppermute | solution.py:20
  957.7 10.7 collective-permute-start.21
  959.3 5.5 collective-permute-start.22
  962.8 5.6 collective-permute-start.23
  971.4 123.7 %copy-start.5 = (f32[16,768]{1,0:T(8,128)S(1)}, f32[16,768]{1,0:T(8,128)}, u32[]{:S(2)}) copy-start(f32[16,768]{1,0:T(8,128)} %copy-done.4) | copy-start | bytes 147460
  971.4 123.7 %copy-start.7 = (f32[16,768]{1,0:T(8,128)S(1)}, f32[16,768]{1,0:T(8,128)}, u32[]{:S(2)}) copy-start(f32[16,768]{1,0:T(8,128)} %copy-done.6) | copy-start | bytes 147460
  971.4 123.7 %copy-start.28 = (f32[16]{0:T(128)S(1)}, f32[16]{0:T(128)}, u32[]{:S(2)}) copy-start(f32[16]{0:T(128)} %copy-done.27) | copy-start | bytes 196
  971.5 123.7 %copy-start.30 = (f32[16]{0:T(128)S(1)}, f32[16]{0:T(128)}, u32[]{:S(2)}) copy-start(f32[16]{0:T(128)} %copy-done.29) | copy-start | bytes 196
  973.4 13.3 %collective-permute-start.24 = (f32[1,16,256]{1,2,0:T(8,128)S(1)}, f32[1,16,256]{1,2,0:T(8,128)S(1)}, u32[]{:S(2)}, u32[]{:S(2)}) collective-permute-start(f32[1,16,256]{1,2,0:T(8,128)S(1)} %get-tuple-element.22), channel_id=1, source_target_pairs={{0,1},{1,2},{2,3},{3,4},{4,5},{5,6},{6,7},{7,8},{8,9},{9,10},{10,1... | collective-permute-start | bytes 49160 | tf_op jit(solution)/shard_map/ppermute | solution.py:20
  977.7 9.1 collective-permute-start.25
  979.0 4.3 collective-permute-start.26
  981.2 5.6 collective-permute-start.27
  (14 other events, 84.6 us)
Sparse Core Ops, SparseCore 0:
  32.7 205.7 all-gather.6
  395.7 193.6 all-gather.8
  745.4 193.7 all-gather.10
where the time goes:
time: 1110 us; the launch traced here: 1100 us
  waiting for transfers between devices  572 us (52%)
  blocking collectives  319 us (29%)
  local copies, waits for them, and re-layouts  99.3 us (9%)
  starting transfers between devices  72 us (6%)
  matrix products  16.6 us (1%)
  between operations  14.5 us (1%)
    all_gather x3, waiting for transfers between devices, per_device(): lax.all_gather(lax.dot_general(residual, local_basis, (((1,), (1,)), ((),...  548 us
    psum x3, blocking collectives, per_device(): lax.psum((jnp.sum(residual * applied, axis=1), jnp.sum(applied * applied,...  319 us
    ppermute x14, starting transfers between devices, padded(): lax.ppermute(lax.slice_in_dim(block, block.shape[dim] - width, None, axis...  47.4 us
    gather x3, local copies, waits for them, and re-layouts, per_device(): jnp.take(coarse_inverse.reshape(mode_count, domain_count, mode_count), co...  26.8 us
    ppermute x14, starting transfers between devices, padded(): lax.ppermute(lax.slice_in_dim(block, 0, width, axis=dim), axis, backward)  24.5 us
    ppermute x14, waiting for transfers between devices, padded(): lax.ppermute(lax.slice_in_dim(block, 0, width, axis=dim), axis, backward)  23.7 us
  transfers between devices with their start and end apart: 31, of which 10 were waited for; matrix products, arithmetic and copies ran while one was open for 4% of the time, Pallas kernels for 0%

commit v1 on v0

v1 whole, which is shorter than its diff:
```python
import functools
import jax
import jax.numpy as jnp
from jax import lax
from jax.experimental import pallas as pl
from jax.experimental.pallas import tpu as pltpu
from jax.sharding import PartitionSpec as P

EW = 256
ES = 128
MB = 128
ITERS = 3
LANES = 128
ROWS = 8

highest = lax.Precision.HIGHEST
epsilon = 1e-06
VMEM = pl.BlockSpec(memory_space=pltpu.VMEM)
SMEM = pl.BlockSpec(memory_space=pltpu.SMEM)


def dot(a, b, dims=((1,), (0,))):
    return lax.dot_general(
        a, b, (dims, ((), ())), precision=highest, preferred_element_type=jnp.float32
    )


def call(kernel, outs, args, flops=1 << 20, specs=None):
    outs = [jax.ShapeDtypeStruct(shape, dtype) for shape, dtype in outs]
    moved = sum(a.size * a.dtype.itemsize for a in args) + sum(
        o.size * o.dtype.itemsize for o in outs
    )
    return pl.pallas_call(
        kernel,
        out_shape=outs,
        in_specs=specs or [VMEM] * len(args),
        out_specs=[VMEM] * len(outs),
        cost_estimate=pl.CostEstimate(flops=flops, bytes_accessed=moved, transcendentals=0),
    )(*args)


def sides(cells):
    return ((0, EW), (EW, 2 * EW), (2 * EW, 2 * EW + ES), (2 * EW + ES, cells))


def sublane_mask(rows, loads):
    row = lax.broadcasted_iota(jnp.int32, (rows, LANES), 0)
    lane = lax.broadcasted_iota(jnp.int32, (rows, LANES), 1)
    return lax.rem(row, ROWS) == lax.div(lane, loads)


def pack(rows, loads):
    kept = jnp.where(sublane_mask(rows.shape[0], loads), rows, 0.0)
    return jnp.sum(kept.reshape(rows.shape[0] // ROWS, ROWS, LANES), axis=1)


def column_of(row, loads):
    a = lax.broadcasted_iota(jnp.int32, (loads, LANES), 0)
    b = lax.broadcasted_iota(jnp.int32, (loads, LANES), 1)
    return jnp.sum(jnp.where(a == b, row, 0.0), axis=1, keepdims=True)


def row_of(column, loads):
    a = lax.broadcasted_iota(jnp.int32, (loads, LANES), 0)
    b = lax.broadcasted_iota(jnp.int32, (loads, LANES), 1)
    return jnp.sum(jnp.where(a == lax.rem(b, loads), column, 0.0), axis=0, keepdims=True)


def one_hot(map_row, block):
    inside = map_row[:, block * MB : (block + 1) * MB] - block * MB
    spot = lax.broadcasted_iota(jnp.int32, (MB, MB), 0)
    return jnp.where(spot == inside, 1.0, 0.0)


def route_kernel(slot_ref, rows_ref, out_ref):
    groups, modes, width = out_ref.shape
    per_tile = LANES // modes
    tiles = width // LANES
    lane = lax.broadcasted_iota(jnp.int32, (modes, LANES), 1)

    def step(group, carry):
        for tile in range(tiles):
            block = jnp.zeros((modes, LANES), jnp.float32)
            for part in range(per_tile):
                slot = slot_ref[(group * tiles + tile) * per_tile + part]
                home = lax.div(slot, per_tile)
                offset = lax.rem(slot, per_tile)
                source = rows_ref[:, pl.ds(pl.multiple_of(home * LANES, LANES), LANES)]
                shift = lax.rem(part - offset + per_tile, per_tile) * modes
                moved = pltpu.roll(source, shift, 1)
                block = jnp.where(lax.div(lane, modes) == part, moved, block)
            out_ref[group, :, tile * LANES : (tile + 1) * LANES] = block
        return carry

    lax.fori_loop(0, groups, step, 0)


def prepare_kernel(map_ref, schur_ref, basis_ref, loads_ref, s_ref, b_ref, *edge_refs):
    cells = schur_ref.shape[0]
    map_row = map_ref[...]
    hots = [one_hot(map_row, block) for block in range(cells // MB)]
    for block, hot in enumerate(hots):
        span = slice(block * MB, (block + 1) * MB)
        b_ref[:, span] = dot(basis_ref[:, span], hot, ((1,), (1,)))
        moved = dot(loads_ref[:, span], hot, ((1,), (1,)))
        for edge_ref, (low, high) in zip(edge_refs, sides(cells)):
            if low <= block * MB < high:
                edge_ref[:, block * MB - low : (block + 1) * MB - low] = moved
    for i, left in enumerate(hots):
        rows = dot(left, schur_ref[i * MB : (i + 1) * MB, :])
        for j, right in enumerate(hots):
            span = slice(j * MB, (j + 1) * MB)
            s_ref[i * MB : (i + 1) * MB, span] = dot(rows[:, span], right, ((1,), (1,)))


def joined(own, other):
    return jnp.concatenate([a[...] + b[...] for a, b in zip(own, other)], axis=1)


def gather_kernel(has_dots, has_coeffs, *refs):
    refs = list(refs)
    own, other = refs[:4], refs[4:8]
    refs = refs[8:]
    residual_ref = refs.pop(0) if has_dots else None
    basis_ref = refs.pop(0) if has_coeffs else None
    field_ref, out_ref = refs
    field = joined(own, other)
    loads = field.shape[0]
    field_ref[...] = field
    parts = []
    if has_coeffs:
        copies = jnp.concatenate([field] * (LANES // loads), axis=0)
        parts.append(pack(dot(basis_ref[...], copies, ((1,), (1,))), loads))
    else:
        parts.append(jnp.zeros((4, LANES), jnp.float32))
    if has_dots:
        for other_field in (residual_ref[...], field):
            total = jnp.sum(other_field * field, axis=1, keepdims=True)
            parts.append(row_of(total, loads))
    else:
        parts.append(jnp.zeros((2, LANES), jnp.float32))
    parts.append(jnp.zeros((2, LANES), jnp.float32))
    payload = jnp.concatenate(parts, axis=0)
    out_ref[...] = jnp.broadcast_to(payload[None], out_ref.shape)


def coarse_kernel(loads, gathered_ref, matrix_ref, out_ref, wide_ref):
    columns = gathered_ref.shape[0]
    groups = out_ref.shape[0]
    modes = matrix_ref.shape[0] // groups
    quads = modes // ROWS
    keep = sublane_mask(ROWS, loads)
    for column in range(columns):
        for quad in range(quads):
            row = gathered_ref[column, quad : quad + 1, :]
            start = (column * quads + quad) * ROWS
            wide_ref[start : start + ROWS, :] = jnp.where(keep, row, 0.0)
    product = dot(matrix_ref[...], wide_ref[...])
    a = lax.broadcasted_iota(jnp.int32, (LANES, LANES), 0)
    b = lax.broadcasted_iota(jnp.int32, (LANES, LANES), 1)
    fold = jnp.where(lax.rem(a, loads) == lax.rem(b, loads), 1.0, 0.0)
    packed = pack(dot(product, fold), loads)
    tail = jnp.sum(gathered_ref[...], axis=0)[quads:, :]
    for group in range(groups):
        out_ref[group, :quads, :] = packed[group * quads : (group + 1) * quads, :]
        out_ref[group, quads:, :] = tail


def lift_kernel(first, *refs):
    refs = list(refs)
    reduced_ref, basis_ref, residual_ref = refs[:3]
    refs = refs[3:]
    if not first:
        image_ref, solution_ref, search_ref, lifted_ref = refs[:4]
        refs = refs[4:]
        residual_out, solution_out = refs[:2]
        refs = refs[2:]
    lifted_out, edges = refs[0], refs[1:]
    loads, cells = residual_ref.shape
    modes = basis_ref.shape[0]
    quads = modes // ROWS
    sums = jnp.sum(reduced_ref[...], axis=0)
    lifted = sums[:quads, :]
    if not first:
        stride_row = sums[quads : quads + 1, :] / (sums[quads + 1 : quads + 2, :] + epsilon)
        stride = column_of(stride_row, loads)
        residual_out[...] = residual_ref[...] - stride * image_ref[...]
        solution_out[...] = solution_ref[...] + stride * search_ref[...]
        lifted = lifted_ref[...] - stride_row * lifted
    lifted_out[...] = lifted
    keep = sublane_mask(ROWS, loads)
    wide = jnp.concatenate(
        [jnp.where(keep, lifted[quad : quad + 1, :], 0.0) for quad in range(quads)], axis=0
    )
    a = lax.broadcasted_iota(jnp.int32, (loads, LANES), 0)
    b = lax.broadcasted_iota(jnp.int32, (loads, LANES), 1)
    fold = jnp.where(a == lax.rem(b, loads), 1.0, 0.0)
    narrow = dot(fold, wide, ((1,), (1,)))
    spread = dot(narrow, basis_ref[...])
    for edge, (low, high) in zip(edges, sides(cells)):
        edge[...] = spread[:, low:high]


def schur_kernel(*refs):
    own, other = refs[:4], refs[4:8]
    residual_ref, schur_ref, search_ref = refs[8:11]
    edges = refs[11:]
    search = residual_ref[...] + joined(own, other)
    search_ref[...] = search
    image = dot(search, schur_ref[...])
    for edge, (low, high) in zip(edges, sides(search.shape[1])):
        edge[...] = image[:, low:high]


def total_kernel(gathered_ref, out_ref):
    out_ref[...] = jnp.broadcast_to(jnp.sum(gathered_ref[...], axis=0)[None], out_ref.shape)


def finish_kernel(reduced_ref, solution_ref, search_ref, map_ref, out_ref):
    loads, cells = solution_ref.shape
    sums = jnp.sum(reduced_ref[...], axis=0)
    stride = column_of(sums[4:5, :] / (sums[5:6, :] + epsilon), loads)
    result = solution_ref[...] + stride * search_ref[...]
    map_row = map_ref[...]
    for block in range(cells // MB):
        span = slice(block * MB, (block + 1) * MB)
        out_ref[:, span] = dot(result[:, span], one_hot(map_row, block))


def exchange(edges):
    west, east, south, north = edges
    found = []
    for axis, low, high in (("gy", west, east), ("gx", south, north)):
        count = lax.axis_size(axis)
        forward = [(i, i + 1) for i in range(count - 1)]
        backward = [(i + 1, i) for i in range(count - 1)]
        found.append(lax.ppermute(high, axis, forward))
        found.append(lax.ppermute(low, axis, backward))
    return found


def per_device(schur_blocks, basis, loads, coarse_inverse, iface_map, coarse_slot):
    f32 = jnp.float32
    columns = lax.axis_size("gy")
    groups = lax.axis_size("gx")
    count, cells = loads.shape[2:]
    modes = basis.shape[2]
    field = ((count, cells), f32)
    edge_shapes = [((count, high - low), f32) for low, high in sides(cells)]
    packed = ((modes // ROWS, LANES), f32)
    along = ((columns, ROWS, LANES), f32)
    across = ((groups, ROWS, LANES), f32)

    (routed,) = call(
        route_kernel,
        [((groups, modes, columns * modes), f32)],
        [coarse_slot, coarse_inverse],
        specs=[SMEM, VMEM],
    )
    matrix = lax.all_to_all(routed, "gx", 0, 0, tiled=True)
    matrix = matrix.reshape(groups * modes, columns * modes)

    schur, modes_here, *edges = call(
        prepare_kernel,
        [((cells, cells), f32), ((modes, cells), f32), *edge_shapes],
        [iface_map[0], schur_blocks[0, 0], basis[0, 0], loads[0, 0]],
        flops=1 << 28,
    )
    residual, payload = call(
        functools.partial(gather_kernel, False, True),
        [field, along],
        [*edges, *exchange(edges), modes_here],
    )
    solution = image = search = lifted = None
    for iteration in range(ITERS):
        gathered = lax.all_to_all(payload, "gy", 0, 0, tiled=True)
        (partial,) = pl.pallas_call(
            functools.partial(coarse_kernel, count),
            out_shape=[jax.ShapeDtypeStruct(*across)],
            in_specs=[VMEM] * 2,
            out_specs=[VMEM],
            scratch_shapes=[pltpu.VMEM((columns * modes, LANES), f32)],
            cost_estimate=pl.CostEstimate(
                flops=1 << 29, bytes_accessed=1 << 22, transcendentals=0
            ),
        )(gathered, matrix)
        reduced = lax.all_to_all(partial, "gx", 0, 0, tiled=True)
        if iteration == 0:
            lifted, *edges = call(
                functools.partial(lift_kernel, True),
                [packed, *edge_shapes],
                [reduced, modes_here, residual],
            )
            solution = jnp.zeros((count, cells), f32)
        else:
            residual, solution, lifted, *edges = call(
                functools.partial(lift_kernel, False),
                [field, field, packed, *edge_shapes],
                [reduced, modes_here, residual, image, solution, search, lifted],
            )
        search, *images = call(
            schur_kernel,
            [field, *edge_shapes],
            [*edges, *exchange(edges), residual, schur],
            flops=1 << 27,
        )
        more = iteration < ITERS - 1
        image, payload = call(
            functools.partial(gather_kernel, True, more),
            [field, along],
            [*images, *exchange(images), residual] + ([modes_here] if more else []),
        )
    gathered = lax.all_to_all(payload, "gy", 0, 0, tiled=True)
    (partial,) = call(total_kernel, [across], [gathered])
    reduced = lax.all_to_all(partial, "gx", 0, 0, tiled=True)
    (result,) = call(finish_kernel, [field], [reduced, solution, search, iface_map[0]])
    return result[None, None]


def solution(mesh):
    placed = (
        P("gx", "gy", None, None),
        P("gx", "gy", None, None),
        P("gx", "gy", None, None),
        P(("gx", "gy"), None),
        P("gx", "gy", None),
        P(),
    )
    return jax.shard_map(
        per_device, mesh=mesh, in_specs=placed, out_specs=P("gx", "gy", None, None), check_vma=False
    )
```

time: 1110 us -> 338 us (0.30)
  waiting for transfers between devices: 572 us -> 11.6 us
  blocking collectives: 319 us -> 160 us
  local copies, waits for them, and re-layouts: 99.3 us -> 6.57 us
  Pallas kernels: 0 us -> 62.4 us
  starting transfers between devices: 72 us -> 95.4 us
  matrix products: 16.6 us -> 0 us
  between operations: 14.5 us -> 0.49 us
    all_gather x3 -> x0, waiting for transfers between devices: 548 us -> none  [per_device(): lax.all_gather(lax.dot_general(residual, local_basis, (((1,), (1,)), ((),...]
    psum x3 -> x0, blocking collectives: 319 us -> none  [per_device(): lax.psum((jnp.sum(residual * applied, axis=1), jnp.sum(applied * applied,...]
    all_to_all x0 -> x8, blocking collectives: none -> 160 us  [the longest x4 68.6 us: per_device(): reduced = lax.all_to_all(partial, 'gx', 0, 0, tiled=True)]
    pallas_call x0 -> x17, Pallas kernels: none -> 62.4 us  [the longest x14 46.4 us: call(): pl.pallas_call(kernel, out_shape=outs, in_specs=specs or [VMEM] * len(arg...]
    gather x24 -> x0, local copies, waits for them, and re-layouts: 50.3 us -> none  [the longest x3 26.8 us: per_device(): jnp.take(coarse_inverse.reshape(mode_count, domain_count, mode_count), co...]
    reshape x2 -> x0, local copies, waits for them, and re-layouts: 17.9 us -> none  [per_device(): coarse_inverse.reshape(mode_count, domain_count, mode_count)]
    dot_general x12 -> x0, matrix products: 16.6 us -> none  [the longest x3 9.99 us: per_device(): lax.dot_general(lax.all_gather(lax.dot_general(residual, local_basis, (((...]
    all_gather x3 -> x0, local copies, waits for them, and re-layouts: 16.6 us -> none  [per_device(): lax.all_gather(lax.dot_general(residual, local_basis, (((1,), (1,)), ((),...]
  transfers between devices with their start and end apart: 31 -> 29, of which waited for: 10 -> 8; matrix products, arithmetic and copies ran while one was open for 4% -> 0% of each run, Pallas kernels for 0% -> 2%
where the time goes in v1:
time: 338 us; the launch traced here: 336 us
  blocking collectives  160 us (47%)
  starting transfers between devices  95.4 us (28%)
  Pallas kernels  62.4 us (18%)
  waiting for transfers between devices  11.6 us (3%)
  local copies, waits for them, and re-layouts  6.57 us (2%)
    all_to_all x4, blocking collectives, per_device(): reduced = lax.all_to_all(partial, 'gx', 0, 0, tiled=True)  68.6 us
    all_to_all x3, blocking collectives, per_device(): gathered = lax.all_to_all(payload, 'gy', 0, 0, tiled=True)  52.6 us
    ppermute x14, starting transfers between devices, exchange(): found.append(lax.ppermute(high, axis, forward))  52.4 us
    pallas_call x14, Pallas kernels, call(): pl.pallas_call(kernel, out_shape=outs, in_specs=specs or [VMEM] * len(arg...  46.4 us
    all_to_all x1, blocking collectives, per_device(): matrix = lax.all_to_all(routed, 'gx', 0, 0, tiled=True)  38.6 us
    ppermute x14, starting transfers between devices, exchange(): found.append(lax.ppermute(low, axis, backward))  32.5 us
    pallas_call x3, Pallas kernels, per_device(): pl.pallas_call(functools.partial(coarse_kernel, count), out_shape=[jax.Sh...  16 us
    all_to_all x1, starting transfers between devices, per_device(): gathered = lax.all_to_all(payload, 'gy', 0, 0, tiled=True)  10.4 us
  transfers between devices with their start and end apart: 29, of which 8 were waited for; matrix products, arithmetic and copies ran while one was open for 0% of the time, Pallas kernels for 2%

profile of v1, /device:TPU:1, one launch (start us, length us, event | category | flops | bytes accessed | tf_op | source)
XLA Modules:
  0.0 336.2 jit_solution(11849348005200028381)
XLA Ops:
  0.0 10.0 %shard_map.64 = (f32[768,768]{1,0:T(8,128)}, f32[32,768]{1,0:T(8,128)}, f32[16,256]{1,0:T(8,128)}, f32[16,256]{1,0:T(8,128)}, f32[16,128]{1,0:T(8,128)}, /*index=5*/f32[16,128]{1,0:T(8,128)}) custom-call(s32[1,768]{1,0:T(1,128)} %bitcast.12, f32[768,768]{1,0:T(8,128)} %bitcast.9, f32[32,768]{1,0:T(8,128)} %bitcast.10, f32[16,768]{1,0:T(8,128)} %bitcast.11), custom_call_target="tpu_custom_call" | custom-call | flops 268435456 | bytes 5016576 | tf_op jit(solution)/shard_map/pallas_call | solution.py:33
  11.3 5.0 %collective-permute-start = (f32[16,256]{1,0:T(8,128)}, f32[16,256]{1,0:T(8,128)S(1)}, u32[]{:S(2)}, u32[]{:S(2)}) collective-permute-start(f32[16,256]{1,0:T(8,128)} %get-tuple-element.52.refs_1_), channel_id=1, source_target_pairs={{0,1},{1,2},{2,3},{3,4},{4,5},{5,6},{6,7},{7,8},{8,9},{9,10},{10,1... | collective-permute-start | bytes 49160 | tf_op jit(solution)/shard_map/ppermute | solution.py:237
  16.3 8.3 %collective-permute-start.3 = (f32[16,128]{1,0:T(8,128)}, f32[16,128]{1,0:T(8,128)S(1)}, u32[]{:S(2)}, u32[]{:S(2)}) collective-permute-start(f32[16,128]{1,0:T(8,128)} %get-tuple-element.53.refs_2_), channel_id=1, source_target_pairs={{16,0},{32,16},{48,32},{64,48},{80,64},{96,80},{112,96},{128,112},... | collective-permute-start | bytes 24584 | tf_op jit(solution)/shard_map/ppermute | solution.py:238
  24.6 1.9 collective-permute-start.2
  28.5 2.1 shard_map.65
  30.7 10.4 %all-to-all-start = ((f32[16,8,128]{2,1,0:T(8,128)}), f32[16,8,128]{2,1,0:T(8,128)S(1)}, u32[]{:S(2)}, u32[]{:S(2)}) async-start(f32[16,8,128]{2,1,0:T(8,128)} %get-tuple-element.56), calls=%async_computation | async-start | bytes 131072 | tf_op jit(solution)/shard_map/all_to_all | solution.py:276
  41.1 7.9 %shard_map.66 = f32[32,32,512]{2,1,0:T(8,128)} custom-call(s32[512]{0:T(512)} %slot_ref.1, f32[32,16384]{1,0:T(8,128)} %rows_ref.1), custom_call_target="tpu_custom_call" | custom-call | flops 1048576 | bytes 4196352 | tf_op jit(solution)/shard_map/pallas_call | solution.py:33
  48.9 4.4 %all-to-all-done.gathered_ref = f32[16,8,128]{2,1,0:T(8,128)S(1)} async-done(((f32[16,8,128]{2,1,0:T(8,128)}), f32[16,8,128]{2,1,0:T(8,128)S(1)}, u32[]{:S(2)}, u32[]{:S(2)}) %all-to-all-start) | async-done | bytes 65568 | tf_op jit(solution)/shard_map/all_to_all | solution.py:276
  53.4 38.6 %all_to_all.45 = f32[32,32,512]{2,1,0:T(8,128)} all-to-all(f32[32,32,512]{2,1,0:T(8,128)} %shard_map.66), channel_id=1, replica_groups=mesh['gx'=32,'gy'=16] {'gx'}, dimensions={0} | all-to-all | bytes 4194304 | tf_op jit(solution)/shard_map/all_to_all | solution.py:260
  92.0 5.3 %shard_map.67 = f32[32,8,128]{2,1,0:T(8,128)} custom-call(f32[16,8,128]{2,1,0:T(8,128)} %copy-done, f32[1024,512]{1,0:T(8,128)} %bitcast.6), custom_call_target="tpu_custom_call" | custom-call | flops 536870912 | bytes 4194304 | tf_op jit(solution)/shard_map/pallas_call | solution.py:277
  97.3 12.1 %all_to_all.46.refs_0_ = f32[32,8,128]{2,1,0:T(8,128)} all-to-all(f32[32,8,128]{2,1,0:T(8,128)} %shard_map.67), channel_id=1, replica_groups=mesh['gx'=32,'gy'=16] {'gx'}, dimensions={0} | all-to-all | bytes 262144 | tf_op jit(solution)/shard_map/all_to_all | solution.py:287
  109.4 2.0 shard_map.68
  112.7 4.0 %collective-permute-start.4 = (f32[16,256]{1,0:T(8,128)}, f32[16,256]{1,0:T(8,128)S(1)}, u32[]{:S(2)}, u32[]{:S(2)}) collective-permute-start(f32[16,256]{1,0:T(8,128)} %get-tuple-element.59.refs_1_), channel_id=1, source_target_pairs={{0,1},{1,2},{2,3},{3,4},{4,5},{5,6},{6,7},{7,8},{8,9},{9,10},{10,1... | collective-permute-start | bytes 49160 | tf_op jit(solution)/shard_map/ppermute | solution.py:237
  116.7 2.9 collective-permute-start.7
  119.6 2.7 collective-permute-start.6
  123.9 3.6 %shard_map.69 = (f32[16,768]{1,0:T(8,128)}, f32[16,256]{1,0:T(8,128)}, f32[16,256]{1,0:T(8,128)}, f32[16,128]{1,0:T(8,128)}, f32[16,128]{1,0:T(8,128)}) custom-call(f32[16,256]{1,0:T(8,128)} %get-tuple-element.58.refs_0_, f32[16,256]{1,0:T(8,128)} %get-tuple-element.59.refs_1_, f32[16,128]{1,0:T(8,128)} %get-tuple-element.60.refs_2_, ...), custom_call_target="tpu_custom_call" | custom-call | flops 134217728 | bytes 2605056 | tf_op jit(solution)/shard_map/pallas_call | solution.py:33
  128.7 4.0 %collective-permute-start.8 = (f32[16,256]{1,0:T(8,128)}, f32[16,256]{1,0:T(8,128)S(1)}, u32[]{:S(2)}, u32[]{:S(2)}) collective-permute-start(f32[16,256]{1,0:T(8,128)} %get-tuple-element.64.refs_1_), channel_id=1, source_target_pairs={{0,1},{1,2},{2,3},{3,4},{4,5},{5,6},{6,7},{7,8},{8,9},{9,10},{10,1... | collective-permute-start | bytes 49160 | tf_op jit(solution)/shard_map/ppermute | solution.py:237
  132.7 2.2 collective-permute-start.11
  134.9 4.6 %collective-permute-start.10 = (f32[16,128]{1,0:T(8,128)}, f32[16,128]{1,0:T(8,128)S(1)}, u32[]{:S(2)}, u32[]{:S(2)}) collective-permute-start(f32[16,128]{1,0:T(8,128)} %get-tuple-element.66.refs_3_), channel_id=1, source_target_pairs={{0,16},{16,32},{32,48},{48,64},{64,80},{80,96},{96,112},{112,128},... | collective-permute-start | bytes 24584 | tf_op jit(solution)/shard_map/ppermute | solution.py:237
  141.8 2.2 shard_map.70
  143.9 18.8 %all_to_all.47.gathered_ref = f32[16,8,128]{2,1,0:T(8,128)} all-to-all(f32[16,8,128]{2,1,0:T(8,128)} %get-tuple-element.67), channel_id=1, replica_groups=mesh['gx'=32,'gy'=16] {'gy'}, dimensions={0} | all-to-all | bytes 131072 | tf_op jit(solution)/shard_map/all_to_all | solution.py:276
  162.7 5.3 %shard_map.71 = f32[32,8,128]{2,1,0:T(8,128)} custom-call(f32[16,8,128]{2,1,0:T(8,128)} %all_to_all.47.gathered_ref, f32[1024,512]{1,0:T(8,128)} %bitcast.7), custom_call_target="tpu_custom_call" | custom-call | flops 536870912 | bytes 4194304 | tf_op jit(solution)/shard_map/pallas_call | solution.py:277
  168.1 19.0 %all_to_all.48.refs_0_ = f32[32,8,128]{2,1,0:T(8,128)} all-to-all(f32[32,8,128]{2,1,0:T(8,128)} %shard_map.71), channel_id=1, replica_groups=mesh['gx'=32,'gy'=16] {'gx'}, dimensions={0} | all-to-all | bytes 262144 | tf_op jit(solution)/shard_map/all_to_all | solution.py:287
  187.7 2.0 shard_map.72
  191.0 4.0 %collective-permute-start.12 = (f32[16,256]{1,0:T(8,128)}, f32[16,256]{1,0:T(8,128)S(1)}, u32[]{:S(2)}, u32[]{:S(2)}) collective-permute-start(f32[16,256]{1,0:T(8,128)} %get-tuple-element.72.refs_1_), channel_id=1, source_target_pairs={{0,1},{1,2},{2,3},{3,4},{4,5},{5,6},{6,7},{7,8},{8,9},{9,10},{10,1... | collective-permute-start | bytes 49160 | tf_op jit(solution)/shard_map/ppermute | solution.py:237
  195.0 2.9 collective-permute-start.15
  197.8 2.7 collective-permute-start.14
  202.1 3.6 %shard_map.73 = (f32[16,768]{1,0:T(8,128)}, f32[16,256]{1,0:T(8,128)}, f32[16,256]{1,0:T(8,128)}, f32[16,128]{1,0:T(8,128)}, f32[16,128]{1,0:T(8,128)}) custom-call(f32[16,256]{1,0:T(8,128)} %get-tuple-element.71.refs_0_, f32[16,256]{1,0:T(8,128)} %get-tuple-element.72.refs_1_, f32[16,128]{1,0:T(8,128)} %get-tuple-element.73.refs_2_, ...), custom_call_target="tpu_custom_call" | custom-call | flops 134217728 | bytes 2605056 | tf_op jit(solution)/shard_map/pallas_call | solution.py:33
  207.0 4.0 %collective-permute-start.16 = (f32[16,256]{1,0:T(8,128)}, f32[16,256]{1,0:T(8,128)S(1)}, u32[]{:S(2)}, u32[]{:S(2)}) collective-permute-start(f32[16,256]{1,0:T(8,128)} %get-tuple-element.77.refs_1_), channel_id=1, source_target_pairs={{0,1},{1,2},{2,3},{3,4},{4,5},{5,6},{6,7},{7,8},{8,9},{9,10},{10,1... | collective-permute-start | bytes 49160 | tf_op jit(solution)/shard_map/ppermute | solution.py:237
  211.0 2.2 collective-permute-start.19
  213.2 4.4 %collective-permute-start.18 = (f32[16,128]{1,0:T(8,128)}, f32[16,128]{1,0:T(8,128)S(1)}, u32[]{:S(2)}, u32[]{:S(2)}) collective-permute-start(f32[16,128]{1,0:T(8,128)} %get-tuple-element.79.refs_3_), channel_id=1, source_target_pairs={{0,16},{16,32},{32,48},{48,64},{64,80},{80,96},{96,112},{112,128},... | collective-permute-start | bytes 24584 | tf_op jit(solution)/shard_map/ppermute | solution.py:237
  219.9 2.2 shard_map.74
  222.0 16.9 %all_to_all.49.gathered_ref = f32[16,8,128]{2,1,0:T(8,128)} all-to-all(f32[16,8,128]{2,1,0:T(8,128)} %get-tuple-element.80), channel_id=1, replica_groups=mesh['gx'=32,'gy'=16] {'gy'}, dimensions={0} | all-to-all | bytes 131072 | tf_op jit(solution)/shard_map/all_to_all | solution.py:276
  238.9 5.3 %shard_map.75 = f32[32,8,128]{2,1,0:T(8,128)} custom-call(f32[16,8,128]{2,1,0:T(8,128)} %all_to_all.49.gathered_ref, f32[1024,512]{1,0:T(8,128)} %bitcast.8), custom_call_target="tpu_custom_call" | custom-call | flops 536870912 | bytes 4194304 | tf_op jit(solution)/shard_map/pallas_call | solution.py:277
  244.3 18.8 %all_to_all.50.refs_0_ = f32[32,8,128]{2,1,0:T(8,128)} all-to-all(f32[32,8,128]{2,1,0:T(8,128)} %shard_map.75), channel_id=1, replica_groups=mesh['gx'=32,'gy'=16] {'gx'}, dimensions={0} | all-to-all | bytes 262144 | tf_op jit(solution)/shard_map/all_to_all | solution.py:287
  263.1 2.0 shard_map.76
  266.4 4.0 %collective-permute-start.20 = (f32[16,256]{1,0:T(8,128)}, f32[16,256]{1,0:T(8,128)S(1)}, u32[]{:S(2)}, u32[]{:S(2)}) collective-permute-start(f32[16,256]{1,0:T(8,128)} %get-tuple-element.86.refs_1_), channel_id=1, source_target_pairs={{0,1},{1,2},{2,3},{3,4},{4,5},{5,6},{6,7},{7,8},{8,9},{9,10},{10,1... | collective-permute-start | bytes 49160 | tf_op jit(solution)/shard_map/ppermute | solution.py:237
  270.4 2.9 collective-permute-start.23
  273.2 2.7 collective-permute-start.22
  277.5 3.6 %shard_map.77 = (f32[16,768]{1,0:T(8,128)}, f32[16,256]{1,0:T(8,128)}, f32[16,256]{1,0:T(8,128)}, f32[16,128]{1,0:T(8,128)}, f32[16,128]{1,0:T(8,128)}) custom-call(f32[16,256]{1,0:T(8,128)} %get-tuple-element.85.refs_0_, f32[16,256]{1,0:T(8,128)} %get-tuple-element.86.refs_1_, f32[16,128]{1,0:T(8,128)} %get-tuple-element.87.refs_2_, ...), custom_call_target="tpu_custom_call" | custom-call | flops 134217728 | bytes 2605056 | tf_op jit(solution)/shard_map/pallas_call | solution.py:33
  282.4 4.0 %collective-permute-start.24 = (f32[16,256]{1,0:T(8,128)}, f32[16,256]{1,0:T(8,128)S(1)}, u32[]{:S(2)}, u32[]{:S(2)}) collective-permute-start(f32[16,256]{1,0:T(8,128)} %get-tuple-element.91.refs_1_), channel_id=1, source_target_pairs={{0,1},{1,2},{2,3},{3,4},{4,5},{5,6},{6,7},{7,8},{8,9},{9,10},{10,1... | collective-permute-start | bytes 49160 | tf_op jit(solution)/shard_map/ppermute | solution.py:237
  286.4 2.2 collective-permute-start.27
  288.6 4.4 %collective-permute-start.26 = (f32[16,128]{1,0:T(8,128)}, f32[16,128]{1,0:T(8,128)S(1)}, u32[]{:S(2)}, u32[]{:S(2)}) collective-permute-start(f32[16,128]{1,0:T(8,128)} %get-tuple-element.93.refs_3_), channel_id=1, source_target_pairs={{0,16},{16,32},{32,48},{48,64},{64,80},{80,96},{96,112},{112,128},... | collective-permute-start | bytes 24584 | tf_op jit(solution)/shard_map/ppermute | solution.py:237
  295.3 1.7 shard_map.78
  296.9 16.9 %all_to_all.51.gathered_ref = f32[16,8,128]{2,1,0:T(8,128)} all-to-all(f32[16,8,128]{2,1,0:T(8,128)} %get-tuple-element.94), channel_id=1, replica_groups=mesh['gx'=32,'gy'=16] {'gy'}, dimensions={0} | all-to-all | bytes 131072 | tf_op jit(solution)/shard_map/all_to_all | solution.py:313
  313.8 1.5 shard_map.79
  315.3 18.8 %all_to_all.52.reduced_ref = f32[32,8,128]{2,1,0:T(8,128)} all-to-all(f32[32,8,128]{2,1,0:T(8,128)} %shard_map.79), channel_id=1, replica_groups=mesh['gx'=32,'gy'=16] {'gx'}, dimensions={0} | all-to-all | bytes 262144 | tf_op jit(solution)/shard_map/all_to_all | solution.py:315
  334.1 2.1 shard_map.80
  (94 shorter events, 22.7 us)
Async XLA Ops:
  10.0 17.9 %collective-permute-start.1 = (f32[16,256]{1,0:T(8,128)}, f32[16,256]{1,0:T(8,128)S(1)}, u32[]{:S(2)}, u32[]{:S(2)}) collective-permute-start(f32[16,256]{1,0:T(8,128)} %get-tuple-element.51.refs_0_), channel_id=1, source_target_pairs={{1,0},{2,1},{3,2},{4,3},{5,4},{6,5},{7,6},{8,7},{9,8},{10,9},{11,1... | collective-permute-start | bytes 49160 | tf_op jit(solution)/shard_map/ppermute | solution.py:238
  11.3 16.6 %collective-permute-start = (f32[16,256]{1,0:T(8,128)}, f32[16,256]{1,0:T(8,128)S(1)}, u32[]{:S(2)}, u32[]{:S(2)}) collective-permute-start(f32[16,256]{1,0:T(8,128)} %get-tuple-element.52.refs_1_), channel_id=1, source_target_pairs={{0,1},{1,2},{2,3},{3,4},{4,5},{5,6},{6,7},{7,8},{8,9},{9,10},{10,1... | collective-permute-start | bytes 49160 | tf_op jit(solution)/shard_map/ppermute | solution.py:237
  16.3 10.2 %collective-permute-start.3 = (f32[16,128]{1,0:T(8,128)}, f32[16,128]{1,0:T(8,128)S(1)}, u32[]{:S(2)}, u32[]{:S(2)}) collective-permute-start(f32[16,128]{1,0:T(8,128)} %get-tuple-element.53.refs_2_), channel_id=1, source_target_pairs={{16,0},{32,16},{48,32},{64,48},{80,64},{96,80},{112,96},{128,112},... | collective-permute-start | bytes 24584 | tf_op jit(solution)/shard_map/ppermute | solution.py:238
  24.6 3.3 collective-permute-start.2
  26.6 1.4 copy-start.22
  27.9 0.6 copy-start.8
  27.9 0.6 copy-start.10
  30.7 22.7 %all-to-all-start = ((f32[16,8,128]{2,1,0:T(8,128)}), f32[16,8,128]{2,1,0:T(8,128)S(1)}, u32[]{:S(2)}, u32[]{:S(2)}) async-start(f32[16,8,128]{2,1,0:T(8,128)} %get-tuple-element.56), calls=%async_computation | async-start | bytes 131072 | tf_op jit(solution)/shard_map/all_to_all | solution.py:276
  53.4 38.6 %copy-start = (f32[16,8,128]{2,1,0:T(8,128)}, f32[16,8,128]{2,1,0:T(8,128)S(1)}, u32[]{:S(2)}) copy-start(f32[16,8,128]{2,1,0:T(8,128)S(1)} %all-to-all-done.gathered_ref) | copy-start | bytes 196612
  111.4 11.8 %collective-permute-start.5 = (f32[16,256]{1,0:T(8,128)}, f32[16,256]{1,0:T(8,128)S(1)}, u32[]{:S(2)}, u32[]{:S(2)}) collective-permute-start(f32[16,256]{1,0:T(8,128)} %get-tuple-element.58.refs_0_), channel_id=1, source_target_pairs={{1,0},{2,1},{3,2},{4,3},{5,4},{6,5},{7,6},{8,7},{9,8},{10,9},{11,1... | collective-permute-start | bytes 49160 | tf_op jit(solution)/shard_map/ppermute | solution.py:238
  112.7 10.6 %collective-permute-start.4 = (f32[16,256]{1,0:T(8,128)}, f32[16,256]{1,0:T(8,128)S(1)}, u32[]{:S(2)}, u32[]{:S(2)}) collective-permute-start(f32[16,256]{1,0:T(8,128)} %get-tuple-element.59.refs_1_), channel_id=1, source_target_pairs={{0,1},{1,2},{2,3},{3,4},{4,5},{5,6},{6,7},{7,8},{8,9},{9,10},{10,1... | collective-permute-start | bytes 49160 | tf_op jit(solution)/shard_map/ppermute | solution.py:237
  116.7 5.6 %collective-permute-start.7 = (f32[16,128]{1,0:T(8,128)}, f32[16,128]{1,0:T(8,128)S(1)}, u32[]{:S(2)}, u32[]{:S(2)}) collective-permute-start(f32[16,128]{1,0:T(8,128)} %get-tuple-element.60.refs_2_), channel_id=1, source_target_pairs={{16,0},{32,16},{48,32},{64,48},{80,64},{96,80},{112,96},{128,112},... | collective-permute-start | bytes 24584 | tf_op jit(solution)/shard_map/ppermute | solution.py:238
  119.6 3.7 %collective-permute-start.6 = (f32[16,128]{1,0:T(8,128)}, f32[16,128]{1,0:T(8,128)S(1)}, u32[]{:S(2)}, u32[]{:S(2)}) collective-permute-start(f32[16,128]{1,0:T(8,128)} %get-tuple-element.61.refs_3_), channel_id=1, source_target_pairs={{0,16},{16,32},{32,48},{48,64},{64,80},{80,96},{96,112},{112,128},... | collective-permute-start | bytes 24584 | tf_op jit(solution)/shard_map/ppermute | solution.py:237
  122.3 1.0 copy-start.15
  123.2 0.6 copy-start.1
  123.3 0.6 copy-start.4
  127.4 13.1 %collective-permute-start.9 = (f32[16,256]{1,0:T(8,128)}, f32[16,256]{1,0:T(8,128)S(1)}, u32[]{:S(2)}, u32[]{:S(2)}) collective-permute-start(f32[16,256]{1,0:T(8,128)} %get-tuple-element.63.refs_0_), channel_id=1, source_target_pairs={{1,0},{2,1},{3,2},{4,3},{5,4},{6,5},{7,6},{8,7},{9,8},{10,9},{11,1... | collective-permute-start | bytes 49160 | tf_op jit(solution)/shard_map/ppermute | solution.py:238
  128.7 11.9 %collective-permute-start.8 = (f32[16,256]{1,0:T(8,128)}, f32[16,256]{1,0:T(8,128)S(1)}, u32[]{:S(2)}, u32[]{:S(2)}) collective-permute-start(f32[16,256]{1,0:T(8,128)} %get-tuple-element.64.refs_1_), channel_id=1, source_target_pairs={{0,1},{1,2},{2,3},{3,4},{4,5},{5,6},{6,7},{7,8},{8,9},{9,10},{10,1... | collective-permute-start | bytes 49160 | tf_op jit(solution)/shard_map/ppermute | solution.py:237
  132.7 6.9 %collective-permute-start.11 = (f32[16,128]{1,0:T(8,128)}, f32[16,128]{1,0:T(8,128)S(1)}, u32[]{:S(2)}, u32[]{:S(2)}) collective-permute-start(f32[16,128]{1,0:T(8,128)} %get-tuple-element.65.refs_2_), channel_id=1, source_target_pairs={{16,0},{32,16},{48,32},{64,48},{80,64},{96,80},{112,96},{128,112},... | collective-permute-start | bytes 24584 | tf_op jit(solution)/shard_map/ppermute | solution.py:238
  134.9 5.6 %collective-permute-start.10 = (f32[16,128]{1,0:T(8,128)}, f32[16,128]{1,0:T(8,128)S(1)}, u32[]{:S(2)}, u32[]{:S(2)}) collective-permute-start(f32[16,128]{1,0:T(8,128)} %get-tuple-element.66.refs_3_), channel_id=1, source_target_pairs={{0,16},{16,32},{32,48},{48,64},{64,80},{80,96},{96,112},{112,128},... | collective-permute-start | bytes 24584 | tf_op jit(solution)/shard_map/ppermute | solution.py:237
  139.6 1.0 copy-start.23
  140.6 0.6 copy-start.11
  189.7 11.8 %collective-permute-start.13 = (f32[16,256]{1,0:T(8,128)}, f32[16,256]{1,0:T(8,128)S(1)}, u32[]{:S(2)}, u32[]{:S(2)}) collective-permute-start(f32[16,256]{1,0:T(8,128)} %get-tuple-element.71.refs_0_), channel_id=1, source_target_pairs={{1,0},{2,1},{3,2},{4,3},{5,4},{6,5},{7,6},{8,7},{9,8},{10,9},{11,1... | collective-permute-start | bytes 49160 | tf_op jit(solution)/shard_map/ppermute | solution.py:238
  191.0 10.6 %collective-permute-start.12 = (f32[16,256]{1,0:T(8,128)}, f32[16,256]{1,0:T(8,128)S(1)}, u32[]{:S(2)}, u32[]{:S(2)}) collective-permute-start(f32[16,256]{1,0:T(8,128)} %get-tuple-element.72.refs_1_), channel_id=1, source_target_pairs={{0,1},{1,2},{2,3},{3,4},{4,5},{5,6},{6,7},{7,8},{8,9},{9,10},{10,1... | collective-permute-start | bytes 49160 | tf_op jit(solution)/shard_map/ppermute | solution.py:237
  195.0 5.6 %collective-permute-start.15 = (f32[16,128]{1,0:T(8,128)}, f32[16,128]{1,0:T(8,128)S(1)}, u32[]{:S(2)}, u32[]{:S(2)}) collective-permute-start(f32[16,128]{1,0:T(8,128)} %get-tuple-element.73.refs_2_), channel_id=1, source_target_pairs={{16,0},{32,16},{48,32},{64,48},{80,64},{96,80},{112,96},{128,112},... | collective-permute-start | bytes 24584 | tf_op jit(solution)/shard_map/ppermute | solution.py:238
  197.8 3.7 %collective-permute-start.14 = (f32[16,128]{1,0:T(8,128)}, f32[16,128]{1,0:T(8,128)S(1)}, u32[]{:S(2)}, u32[]{:S(2)}) collective-permute-start(f32[16,128]{1,0:T(8,128)} %get-tuple-element.74.refs_3_), channel_id=1, source_target_pairs={{0,16},{16,32},{32,48},{48,64},{64,80},{80,96},{96,112},{112,128},... | collective-permute-start | bytes 24584 | tf_op jit(solution)/shard_map/ppermute | solution.py:237
  200.5 1.0 copy-start.17
  201.5 0.6 copy-start.6
  205.7 13.0 %collective-permute-start.17 = (f32[16,256]{1,0:T(8,128)}, f32[16,256]{1,0:T(8,128)S(1)}, u32[]{:S(2)}, u32[]{:S(2)}) collective-permute-start(f32[16,256]{1,0:T(8,128)} %get-tuple-element.76.refs_0_), channel_id=1, source_target_pairs={{1,0},{2,1},{3,2},{4,3},{5,4},{6,5},{7,6},{8,7},{9,8},{10,9},{11,1... | collective-permute-start | bytes 49160 | tf_op jit(solution)/shard_map/ppermute | solution.py:238
  207.0 11.7 %collective-permute-start.16 = (f32[16,256]{1,0:T(8,128)}, f32[16,256]{1,0:T(8,128)S(1)}, u32[]{:S(2)}, u32[]{:S(2)}) collective-permute-start(f32[16,256]{1,0:T(8,128)} %get-tuple-element.77.refs_1_), channel_id=1, source_target_pairs={{0,1},{1,2},{2,3},{3,4},{4,5},{5,6},{6,7},{7,8},{8,9},{9,10},{10,1... | collective-permute-start | bytes 49160 | tf_op jit(solution)/shard_map/ppermute | solution.py:237
  211.0 6.7 %collective-permute-start.19 = (f32[16,128]{1,0:T(8,128)}, f32[16,128]{1,0:T(8,128)S(1)}, u32[]{:S(2)}, u32[]{:S(2)}) collective-permute-start(f32[16,128]{1,0:T(8,128)} %get-tuple-element.78.refs_2_), channel_id=1, source_target_pairs={{16,0},{32,16},{48,32},{64,48},{80,64},{96,80},{112,96},{128,112},... | collective-permute-start | bytes 24584 | tf_op jit(solution)/shard_map/ppermute | solution.py:238
  213.2 5.4 %collective-permute-start.18 = (f32[16,128]{1,0:T(8,128)}, f32[16,128]{1,0:T(8,128)S(1)}, u32[]{:S(2)}, u32[]{:S(2)}) collective-permute-start(f32[16,128]{1,0:T(8,128)} %get-tuple-element.79.refs_3_), channel_id=1, source_target_pairs={{0,16},{16,32},{32,48},{48,64},{64,80},{80,96},{96,112},{112,128},... | collective-permute-start | bytes 24584 | tf_op jit(solution)/shard_map/ppermute | solution.py:237
  217.7 1.0 copy-start.24
  218.7 0.6 copy-start.12
  219.3 0.6 copy-start.14
  265.1 11.8 %collective-permute-start.21 = (f32[16,256]{1,0:T(8,128)}, f32[16,256]{1,0:T(8,128)S(1)}, u32[]{:S(2)}, u32[]{:S(2)}) collective-permute-start(f32[16,256]{1,0:T(8,128)} %get-tuple-element.85.refs_0_), channel_id=1, source_target_pairs={{1,0},{2,1},{3,2},{4,3},{5,4},{6,5},{7,6},{8,7},{9,8},{10,9},{11,1... | collective-permute-start | bytes 49160 | tf_op jit(solution)/shard_map/ppermute | solution.py:238
  266.4 10.6 %collective-permute-start.20 = (f32[16,256]{1,0:T(8,128)}, f32[16,256]{1,0:T(8,128)S(1)}, u32[]{:S(2)}, u32[]{:S(2)}) collective-permute-start(f32[16,256]{1,0:T(8,128)} %get-tuple-element.86.refs_1_), channel_id=1, source_target_pairs={{0,1},{1,2},{2,3},{3,4},{4,5},{5,6},{6,7},{7,8},{8,9},{9,10},{10,1... | collective-permute-start | bytes 49160 | tf_op jit(solution)/shard_map/ppermute | solution.py:237
  270.4 5.6 %collective-permute-start.23 = (f32[16,128]{1,0:T(8,128)}, f32[16,128]{1,0:T(8,128)S(1)}, u32[]{:S(2)}, u32[]{:S(2)}) collective-permute-start(f32[16,128]{1,0:T(8,128)} %get-tuple-element.87.refs_2_), channel_id=1, source_target_pairs={{16,0},{32,16},{48,32},{64,48},{80,64},{96,80},{112,96},{128,112},... | collective-permute-start | bytes 24584 | tf_op jit(solution)/shard_map/ppermute | solution.py:238
  273.2 3.7 %collective-permute-start.22 = (f32[16,128]{1,0:T(8,128)}, f32[16,128]{1,0:T(8,128)S(1)}, u32[]{:S(2)}, u32[]{:S(2)}) collective-permute-start(f32[16,128]{1,0:T(8,128)} %get-tuple-element.88.refs_3_), channel_id=1, source_target_pairs={{0,16},{16,32},{32,48},{48,64},{64,80},{80,96},{96,112},{112,128},... | collective-permute-start | bytes 24584 | tf_op jit(solution)/shard_map/ppermute | solution.py:237
  276.0 1.0 copy-start.16
  276.9 0.6 copy-start.2
  276.9 0.6 copy-start.5
  281.1 13.0 %collective-permute-start.25 = (f32[16,256]{1,0:T(8,128)}, f32[16,256]{1,0:T(8,128)S(1)}, u32[]{:S(2)}, u32[]{:S(2)}) collective-permute-start(f32[16,256]{1,0:T(8,128)} %get-tuple-element.90.refs_0_), channel_id=1, source_target_pairs={{1,0},{2,1},{3,2},{4,3},{5,4},{6,5},{7,6},{8,7},{9,8},{10,9},{11,1... | collective-permute-start | bytes 49160 | tf_op jit(solution)/shard_map/ppermute | solution.py:238
  282.4 11.7 %collective-permute-start.24 = (f32[16,256]{1,0:T(8,128)}, f32[16,256]{1,0:T(8,128)S(1)}, u32[]{:S(2)}, u32[]{:S(2)}) collective-permute-start(f32[16,256]{1,0:T(8,128)} %get-tuple-element.91.refs_1_), channel_id=1, source_target_pairs={{0,1},{1,2},{2,3},{3,4},{4,5},{5,6},{6,7},{7,8},{8,9},{9,10},{10,1... | collective-permute-start | bytes 49160 | tf_op jit(solution)/shard_map/ppermute | solution.py:237
  286.4 6.7 %collective-permute-start.27 = (f32[16,128]{1,0:T(8,128)}, f32[16,128]{1,0:T(8,128)S(1)}, u32[]{:S(2)}, u32[]{:S(2)}) collective-permute-start(f32[16,128]{1,0:T(8,128)} %get-tuple-element.92.refs_2_), channel_id=1, source_target_pairs={{16,0},{32,16},{48,32},{64,48},{80,64},{96,80},{112,96},{128,112},... | collective-permute-start | bytes 24584 | tf_op jit(solution)/shard_map/ppermute | solution.py:238
  288.6 5.4 %collective-permute-start.26 = (f32[16,128]{1,0:T(8,128)}, f32[16,128]{1,0:T(8,128)S(1)}, u32[]{:S(2)}, u32[]{:S(2)}) collective-permute-start(f32[16,128]{1,0:T(8,128)} %get-tuple-element.93.refs_3_), channel_id=1, source_target_pairs={{0,16},{16,32},{32,48},{48,64},{64,80},{80,96},{96,112},{112,128},... | collective-permute-start | bytes 24584 | tf_op jit(solution)/shard_map/ppermute | solution.py:237
  293.1 1.0 copy-start.21
  294.1 0.6 copy-start.7
  (10 other events, 5.9 us)

commit v2 on v1

--- a/solution.py
+++ b/solution.py
@@ -12,6 +12,7 @@
 ITERS = 3
 LANES = 128
 ROWS = 8
+LIMIT = 20 << 20
 
 highest = lax.Precision.HIGHEST
 epsilon = 1e-06
@@ -25,7 +26,16 @@
     )
 
 
-def call(kernel, outs, args, flops=1 << 20, specs=None):
+def split(value):
+    high = value.astype(jnp.bfloat16)
+    return high, (value - high.astype(jnp.float32)).astype(jnp.bfloat16)
+
+
+def narrow_dot(a, b, dims=((1,), (0,))):
+    return lax.dot_general(a, b, (dims, ((), ())), preferred_element_type=jnp.float32)
+
+
+def call(kernel, outs, args, flops=1 << 20, specs=None, scratch=()):
     outs = [jax.ShapeDtypeStruct(shape, dtype) for shape, dtype in outs]
     moved = sum(a.size * a.dtype.itemsize for a in args) + sum(
         o.size * o.dtype.itemsize for o in outs
@@ -35,6 +45,8 @@
         out_shape=outs,
         in_specs=specs or [VMEM] * len(args),
         out_specs=[VMEM] * len(outs),
+        scratch_shapes=scratch,
+        compiler_params=pltpu.CompilerParams(vmem_limit_bytes=LIMIT),
         cost_estimate=pl.CostEstimate(flops=flops, bytes_accessed=moved, transcendentals=0),
     )(*args)
 
@@ -72,7 +84,7 @@
     return jnp.where(spot == inside, 1.0, 0.0)
 
 
-def route_kernel(slot_ref, rows_ref, out_ref):
+def route_kernel(slot_ref, rows_ref, out_ref, token_ref):
     groups, modes, width = out_ref.shape
     per_tile = LANES // modes
     tiles = width // LANES
@@ -93,24 +105,37 @@
         return carry
 
     lax.fori_loop(0, groups, step, 0)
-
-
-def prepare_kernel(map_ref, schur_ref, basis_ref, loads_ref, s_ref, b_ref, *edge_refs):
+    token_ref[...] = jnp.zeros_like(token_ref)
+
+
+def prepare_kernel(map_ref, basis_ref, loads_ref, token_ref, b_ref, *edge_refs):
+    modes, cells = basis_ref.shape
+    map_row = map_ref[...]
+    for block in range(cells // MB):
+        hot = one_hot(map_row, block)
+        span = slice(block * MB, (block + 1) * MB)
+        high, low = split(dot(basis_ref[:, span], hot, ((1,), (1,))))
+        b_ref[:modes, span] = high
+        b_ref[modes:, span] = low
+        moved = dot(loads_ref[:, span], hot, ((1,), (1,)))
+        for edge_ref, (start, stop) in zip(edge_refs, sides(cells)):
+            if start <= block * MB < stop:
+                edge_ref[:, block * MB - start : (block + 1) * MB - start] = moved
+
+
+def reorder_kernel(map_ref, schur_ref, token_ref, high_ref, low_ref):
     cells = schur_ref.shape[0]
     map_row = map_ref[...]
-    hots = [one_hot(map_row, block) for block in range(cells // MB)]
-    for block, hot in enumerate(hots):
-        span = slice(block * MB, (block + 1) * MB)
-        b_ref[:, span] = dot(basis_ref[:, span], hot, ((1,), (1,)))
-        moved = dot(loads_ref[:, span], hot, ((1,), (1,)))
-        for edge_ref, (low, high) in zip(edge_refs, sides(cells)):
-            if low <= block * MB < high:
-                edge_ref[:, block * MB - low : (block + 1) * MB - low] = moved
+    hots = [one_hot(map_row, block).astype(jnp.bfloat16) for block in range(cells // MB)]
     for i, left in enumerate(hots):
-        rows = dot(left, schur_ref[i * MB : (i + 1) * MB, :])
-        for j, right in enumerate(hots):
-            span = slice(j * MB, (j + 1) * MB)
-            s_ref[i * MB : (i + 1) * MB, span] = dot(rows[:, span], right, ((1,), (1,)))
+        span_i = slice(i * MB, (i + 1) * MB)
+        for part, out_ref in zip(split(schur_ref[span_i, :]), (high_ref, low_ref)):
+            rows = narrow_dot(left, part).astype(jnp.bfloat16)
+            for j, right in enumerate(hots):
+                span = slice(j * MB, (j + 1) * MB)
+                out_ref[span_i, span] = narrow_dot(rows[:, span], right, ((1,), (1,))).astype(
+                    jnp.bfloat16
+                )
 
 
 def joined(own, other):
@@ -129,8 +154,11 @@
     field_ref[...] = field
     parts = []
     if has_coeffs:
-        copies = jnp.concatenate([field] * (LANES // loads), axis=0)
-        parts.append(pack(dot(basis_ref[...], copies, ((1,), (1,))), loads))
+        modes = basis_ref.shape[0] // 2
+        copies = [jnp.concatenate([part] * (LANES // loads), axis=0) for part in split(field)]
+        both = narrow_dot(basis_ref[...], jnp.concatenate(copies, axis=0), ((1,), (1,)))
+        both = both[:, :LANES] + both[:, LANES:]
+        parts.append(pack(both[:modes] + both[modes:], loads))
     else:
         parts.append(jnp.zeros((4, LANES), jnp.float32))
     if has_dots:
@@ -144,10 +172,18 @@
     out_ref[...] = jnp.broadcast_to(payload[None], out_ref.shape)
 
 
-def coarse_kernel(loads, gathered_ref, matrix_ref, out_ref, wide_ref):
+def coarse_kernel(loads, first, *refs):
+    if first:
+        gathered_ref, matrix_ref, out_ref, high_ref, low_ref, wide_ref = refs
+        high, low = split(matrix_ref[...])
+        high_ref[...] = high
+        low_ref[...] = low
+    else:
+        gathered_ref, high_ref, low_ref, out_ref, wide_ref = refs
+        high, low = high_ref[...], low_ref[...]
     columns = gathered_ref.shape[0]
     groups = out_ref.shape[0]
-    modes = matrix_ref.shape[0] // groups
+    modes = high_ref.shape[0] // groups
     quads = modes // ROWS
     keep = sublane_mask(ROWS, loads)
     for column in range(columns):
@@ -155,37 +191,42 @@
             row = gathered_ref[column, quad : quad + 1, :]
             start = (column * quads + quad) * ROWS
             wide_ref[start : start + ROWS, :] = jnp.where(keep, row, 0.0)
-    product = dot(matrix_ref[...], wide_ref[...])
-    a = lax.broadcasted_iota(jnp.int32, (LANES, LANES), 0)
-    b = lax.broadcasted_iota(jnp.int32, (LANES, LANES), 1)
-    fold = jnp.where(lax.rem(a, loads) == lax.rem(b, loads), 1.0, 0.0)
-    packed = pack(dot(product, fold), loads)
+    wide = wide_ref[...]
+    shift = LANES // 2
+    while shift >= loads:
+        wide = wide + pltpu.roll(wide, shift, 1)
+        shift //= 2
+    right = jnp.concatenate(split(wide), axis=1)
+    product = narrow_dot(high, right) + narrow_dot(low, right)
+    packed = pack(product[:, :LANES] + product[:, LANES:], loads)
     tail = jnp.sum(gathered_ref[...], axis=0)[quads:, :]
     for group in range(groups):
         out_ref[group, :quads, :] = packed[group * quads : (group + 1) * quads, :]
         out_ref[group, quads:, :] = tail
 
 
-def lift_kernel(first, *refs):
+def lift_kernel(iteration, *refs):
     refs = list(refs)
-    reduced_ref, basis_ref, residual_ref = refs[:3]
-    refs = refs[3:]
-    if not first:
-        image_ref, solution_ref, search_ref, lifted_ref = refs[:4]
+    reduced_ref, basis_ref = refs[:2]
+    refs = refs[2:]
+    if iteration:
+        residual_ref, image_ref, search_ref, lifted_ref = refs[:4]
         refs = refs[4:]
+        solution_ref = refs.pop(0) if iteration > 1 else None
         residual_out, solution_out = refs[:2]
         refs = refs[2:]
     lifted_out, edges = refs[0], refs[1:]
-    loads, cells = residual_ref.shape
-    modes = basis_ref.shape[0]
+    loads = edges[0].shape[0]
+    modes, cells = basis_ref.shape[0] // 2, basis_ref.shape[1]
     quads = modes // ROWS
     sums = jnp.sum(reduced_ref[...], axis=0)
     lifted = sums[:quads, :]
-    if not first:
+    if iteration:
         stride_row = sums[quads : quads + 1, :] / (sums[quads + 1 : quads + 2, :] + epsilon)
         stride = column_of(stride_row, loads)
         residual_out[...] = residual_ref[...] - stride * image_ref[...]
-        solution_out[...] = solution_ref[...] + stride * search_ref[...]
+        step = stride * search_ref[...]
+        solution_out[...] = step if solution_ref is None else solution_ref[...] + step
         lifted = lifted_ref[...] - stride_row * lifted
     lifted_out[...] = lifted
     keep = sublane_mask(ROWS, loads)
@@ -195,21 +236,27 @@
     a = lax.broadcasted_iota(jnp.int32, (loads, LANES), 0)
     b = lax.broadcasted_iota(jnp.int32, (loads, LANES), 1)
     fold = jnp.where(a == lax.rem(b, loads), 1.0, 0.0)
-    narrow = dot(fold, wide, ((1,), (1,)))
-    spread = dot(narrow, basis_ref[...])
-    for edge, (low, high) in zip(edges, sides(cells)):
-        edge[...] = spread[:, low:high]
+    high, low = split(dot(fold, wide, ((1,), (1,))))
+    left = jnp.concatenate(
+        [jnp.concatenate([high, high], axis=1), jnp.concatenate([low, low], axis=1)], axis=0
+    )
+    both = narrow_dot(left, basis_ref[...])
+    spread = both[:loads] + both[loads:]
+    for edge, (start, stop) in zip(edges, sides(cells)):
+        edge[...] = spread[:, start:stop]
 
 
 def schur_kernel(*refs):
     own, other = refs[:4], refs[4:8]
-    residual_ref, schur_ref, search_ref = refs[8:11]
-    edges = refs[11:]
+    residual_ref, high_ref, low_ref, search_ref = refs[8:12]
+    edges = refs[12:]
     search = residual_ref[...] + joined(own, other)
     search_ref[...] = search
-    image = dot(search, schur_ref[...])
-    for edge, (low, high) in zip(edges, sides(search.shape[1])):
-        edge[...] = image[:, low:high]
+    loads, cells = search.shape
+    left = jnp.concatenate(split(search), axis=0)
+    for edge, (start, stop) in zip(edges, sides(cells)):
+        both = narrow_dot(left, high_ref[:, start:stop]) + narrow_dot(left, low_ref[:, start:stop])
+        edge[...] = both[:loads] + both[loads:]
 
 
 def total_kernel(gathered_ref, out_ref):
@@ -251,64 +298,68 @@
     along = ((columns, ROWS, LANES), f32)
     across = ((groups, ROWS, LANES), f32)
 
-    (routed,) = call(
+    routed, token = call(
         route_kernel,
-        [((groups, modes, columns * modes), f32)],
+        [((groups, modes, columns * modes), f32), ((ROWS, LANES), f32)],
         [coarse_slot, coarse_inverse],
         specs=[SMEM, VMEM],
     )
     matrix = lax.all_to_all(routed, "gx", 0, 0, tiled=True)
     matrix = matrix.reshape(groups * modes, columns * modes)
 
-    schur, modes_here, *edges = call(
+    frame, *edges = call(
         prepare_kernel,
-        [((cells, cells), f32), ((modes, cells), f32), *edge_shapes],
-        [iface_map[0], schur_blocks[0, 0], basis[0, 0], loads[0, 0]],
-        flops=1 << 28,
+        [((2 * modes, cells), jnp.bfloat16), *edge_shapes],
+        [iface_map[0], basis[0, 0], loads[0, 0], token],
     )
     residual, payload = call(
         functools.partial(gather_kernel, False, True),
         [field, along],
-        [*edges, *exchange(edges), modes_here],
-    )
+        [*edges, *exchange(edges), frame],
+    )
+    schur = call(
+        reorder_kernel,
+        [((cells, cells), jnp.bfloat16)] * 2,
+        [iface_map[0], schur_blocks[0, 0], token],
+        flops=1 << 28,
+    )
+    split_shape = (matrix.shape, jnp.bfloat16)
+    wide = [pltpu.VMEM((columns * modes, LANES), f32)]
     solution = image = search = lifted = None
     for iteration in range(ITERS):
+        first = iteration == 0
+        if first:
+            payload, matrix, *schur = lax.optimization_barrier((payload, matrix, *schur))
         gathered = lax.all_to_all(payload, "gy", 0, 0, tiled=True)
-        (partial,) = pl.pallas_call(
-            functools.partial(coarse_kernel, count),
-            out_shape=[jax.ShapeDtypeStruct(*across)],
-            in_specs=[VMEM] * 2,
-            out_specs=[VMEM],
-            scratch_shapes=[pltpu.VMEM((columns * modes, LANES), f32)],
-            cost_estimate=pl.CostEstimate(
-                flops=1 << 29, bytes_accessed=1 << 22, transcendentals=0
-            ),
-        )(gathered, matrix)
+        partial, *parts = call(
+            functools.partial(coarse_kernel, count, first),
+            [across] + [split_shape] * (2 * first),
+            [gathered, matrix] if first else [gathered, *halves],
+            flops=1 << 29,
+            scratch=wide,
+        )
+        halves = parts if first else halves
         reduced = lax.all_to_all(partial, "gx", 0, 0, tiled=True)
-        if iteration == 0:
-            lifted, *edges = call(
-                functools.partial(lift_kernel, True),
-                [packed, *edge_shapes],
-                [reduced, modes_here, residual],
-            )
-            solution = jnp.zeros((count, cells), f32)
-        else:
-            residual, solution, lifted, *edges = call(
-                functools.partial(lift_kernel, False),
-                [field, field, packed, *edge_shapes],
-                [reduced, modes_here, residual, image, solution, search, lifted],
-            )
+        known = [residual, image, search, lifted] if iteration else []
+        found = call(
+            functools.partial(lift_kernel, iteration),
+            [field] * (2 if iteration else 0) + [packed, *edge_shapes],
+            [reduced, frame, *known] + ([solution] if iteration > 1 else []),
+        )
+        if iteration:
+            residual, solution, *found = found
+        lifted, *edges = found
         search, *images = call(
             schur_kernel,
             [field, *edge_shapes],
-            [*edges, *exchange(edges), residual, schur],
+            [*edges, *exchange(edges), residual, *schur],
             flops=1 << 27,
         )
         more = iteration < ITERS - 1
         image, payload = call(
             functools.partial(gather_kernel, True, more),
             [field, along],
-            [*images, *exchange(images), residual] + ([modes_here] if more else []),
+            [*images, *exchange(images), residual] + ([frame] if more else []),
         )
     gathered = lax.all_to_all(payload, "gy", 0, 0, tiled=True)
     (partial,) = call(total_kernel, [across], [gathered])

time: 338 us -> 275 us (0.81)
  Pallas kernels: 62.4 us -> 21 us
  blocking collectives: 160 us -> 142 us
  starting transfers between devices: 95.4 us -> 90.5 us
  waiting for transfers between devices: 11.6 us -> 16 us
    all_to_all x1 -> x0, blocking collectives: 38.6 us -> none  [per_device(): matrix = lax.all_to_all(routed, 'gx', 0, 0, tiled=True)]
    pallas_call x14 -> x18, Pallas kernels: 46.4 us -> 21 us  [call(): pl.pallas_call(kernel, out_shape=outs, in_specs=specs or [VMEM] * len(arg...]
    all_to_all x3 -> x4, blocking collectives: 52.6 us -> 73.5 us  [per_device(): gathered = lax.all_to_all(payload, 'gy', 0, 0, tiled=True)]
    pallas_call x3 -> x0, Pallas kernels: 16 us -> none  [per_device(): pl.pallas_call(functools.partial(coarse_kernel, count), out_shape=[jax.Sh...]
    ppermute x14, waiting for transfers between devices: 0.04 us -> 6.42 us  [exchange(): found.append(lax.ppermute(low, axis, backward))]
    ppermute x14, starting transfers between devices: 32.5 us -> 26.6 us  [exchange(): found.append(lax.ppermute(low, axis, backward))]
where the time goes in v2:
time: 275 us; the launch traced here: 274 us
  blocking collectives  142 us (52%)
  starting transfers between devices  90.5 us (33%)
  Pallas kernels  21 us (8%)
  waiting for transfers between devices  16 us (6%)
  local copies, waits for them, and re-layouts  3.94 us (1%)
    all_to_all x4, blocking collectives, per_device(): gathered = lax.all_to_all(payload, 'gy', 0, 0, tiled=True)  73.5 us
    all_to_all x4, blocking collectives, per_device(): reduced = lax.all_to_all(partial, 'gx', 0, 0, tiled=True)  68.6 us
    ppermute x14, starting transfers between devices, exchange(): found.append(lax.ppermute(high, axis, forward))  52.6 us
    ppermute x14, starting transfers between devices, exchange(): found.append(lax.ppermute(low, axis, backward))  26.6 us
    pallas_call x18, Pallas kernels, call(): pl.pallas_call(kernel, out_shape=outs, in_specs=specs or [VMEM] * len(arg...  21 us
    all_to_all x1, starting transfers between devices, per_device(): matrix = lax.all_to_all(routed, 'gx', 0, 0, tiled=True)  11.3 us
    ppermute x14, waiting for transfers between devices, exchange(): found.append(lax.ppermute(low, axis, backward))  6.42 us
  transfers between devices with their start and end apart: 29, of which 8 were waited for; matrix products, arithmetic and copies ran while one was open for 0% of the time, Pallas kernels for 2%

profile of v2, /device:TPU:1, one launch (start us, length us, event | category | flops | bytes accessed | tf_op | source)
XLA Modules:
  0.0 274.0 jit_solution(16921123325657036907)
XLA Ops:
  0.0 1.6 copy-done.1
  2.3 6.8 %shard_map.64 = (f32[32,32,512]{2,1,0:T(8,128)}, f32[8,128]{1,0:T(8,128)S(1)}) custom-call(s32[512]{0:T(512)S(1)} %copy-done.5, f32[32,16384]{1,0:T(8,128)S(1)} %copy-done.1), custom_call_target="tpu_custom_call" | custom-call | flops 1048576 | bytes 4200448 | tf_op jit(solution)/shard_map/pallas_call | solution.py:43
  9.1 11.3 %all-to-all-start = ((f32[32,32,512]{2,1,0:T(8,128)}), f32[32,32,512]{2,1,0:T(8,128)}, u32[]{:S(2)}, u32[]{:S(2)}) async-start(f32[32,32,512]{2,1,0:T(8,128)} %get-tuple-element.68), calls=%async_computation | async-start | bytes 4194304 | tf_op jit(solution)/shard_map/all_to_all | solution.py:307
  20.5 1.3 shard_map.65
  21.8 2.3 collective-permute-start.3
  24.1 3.2 %collective-permute-start.2 = (f32[16,128]{1,0:T(8,128)S(1)}, f32[16,128]{1,0:T(8,128)S(1)}, u32[]{:S(2)}, u32[]{:S(2)}) collective-permute-start(f32[16,128]{1,0:T(8,128)S(1)} %get-tuple-element.65.refs_3_), channel_id=1, source_target_pairs={{0,16},{16,32},{32,48},{48,64},{64,80},{80,96},{96,112},{112,128},... | collective-permute-start | bytes 24584 | tf_op jit(solution)/shard_map/ppermute | solution.py:284
  27.4 1.3 collective-permute-start.1
  28.7 4.0 %collective-permute-start = (f32[16,256]{1,0:T(8,128)S(1)}, f32[16,256]{1,0:T(8,128)S(1)}, u32[]{:S(2)}, u32[]{:S(2)}) collective-permute-start(f32[16,256]{1,0:T(8,128)S(1)} %get-tuple-element.63.refs_1_), channel_id=1, source_target_pairs={{0,1},{1,2},{2,3},{3,4},{4,5},{5,6},{6,7},{7,8},{8,9},{9,10},{10,1... | collective-permute-start | bytes 49160 | tf_op jit(solution)/shard_map/ppermute | solution.py:284
  32.7 1.7 copy-done
  34.3 2.9 %shard_map.67 = (bf16[768,768]{1,0:T(8,128)(2,1)S(1)}, bf16[768,768]{1,0:T(8,128)(2,1)S(1)}) custom-call(s32[1,768]{1,0:T(1,128)S(1)} %bitcast.10, f32[768,768]{1,0:T(8,128)S(1)} %bitcast.6, f32[8,128]{1,0:T(8,128)S(1)} %get-tuple-element.61.token_ref), custom_call_target="tpu_custom_call" | custom-call | flops 268435456 | bytes 4725760 | tf_op jit(solution)/shard_map/pallas_call | solution.py:43
  37.2 6.4 %collective-permute-done.3.refs_7_ = f32[16,128]{1,0:T(8,128)S(1)} collective-permute-done((f32[16,128]{1,0:T(8,128)S(1)}, f32[16,128]{1,0:T(8,128)S(1)}, u32[]{:S(2)}, u32[]{:S(2)}) %collective-permute-start.3) | collective-permute-done | bytes 8224 | tf_op jit(solution)/shard_map/ppermute | solution.py:285
  43.9 5.0 %all-to-all-done = f32[32,32,512]{2,1,0:T(8,128)} async-done(((f32[32,32,512]{2,1,0:T(8,128)}), f32[32,32,512]{2,1,0:T(8,128)}, u32[]{:S(2)}, u32[]{:S(2)}) %all-to-all-start) | async-done | bytes 2097184 | tf_op jit(solution)/shard_map/all_to_all | solution.py:307
  48.9 23.7 %all_to_all.45.refs_0_ = f32[16,8,128]{2,1,0:T(8,128)S(1)} all-to-all(f32[16,8,128]{2,1,0:T(8,128)S(1)} %get-tuple-element.71), channel_id=1, replica_groups=mesh['gx'=32,'gy'=16] {'gy'}, dimensions={0} | all-to-all | bytes 131072 | tf_op jit(solution)/shard_map/all_to_all | solution.py:333
  72.6 2.6 shard_map.68
  75.1 13.2 %all_to_all.46.refs_0_ = f32[32,8,128]{2,1,0:T(8,128)S(1)} all-to-all(f32[32,8,128]{2,1,0:T(8,128)S(1)} %get-tuple-element.73), channel_id=1, replica_groups=mesh['gx'=32,'gy'=16] {'gx'}, dimensions={0} | all-to-all | bytes 262144 | tf_op jit(solution)/shard_map/all_to_all | solution.py:342
  88.7 1.3 collective-permute-start.5
  90.0 4.0 %collective-permute-start.4 = (f32[16,256]{1,0:T(8,128)S(1)}, f32[16,256]{1,0:T(8,128)S(1)}, u32[]{:S(2)}, u32[]{:S(2)}) collective-permute-start(f32[16,256]{1,0:T(8,128)S(1)} %get-tuple-element.75.refs_1_), channel_id=1, source_target_pairs={{0,1},{1,2},{2,3},{3,4},{4,5},{5,6},{6,7},{7,8},{8,9},{9,10},{10,1... | collective-permute-start | bytes 49160 | tf_op jit(solution)/shard_map/ppermute | solution.py:284
  94.0 2.9 %collective-permute-start.7 = (f32[16,128]{1,0:T(8,128)S(1)}, f32[16,128]{1,0:T(8,128)S(1)}, u32[]{:S(2)}, u32[]{:S(2)}) collective-permute-start(f32[16,128]{1,0:T(8,128)S(1)} %get-tuple-element.76.refs_2_), channel_id=1, source_target_pairs={{16,0},{32,16},{48,32},{64,48},{80,64},{96,80},{112,96},{128,112},... | collective-permute-start | bytes 24584 | tf_op jit(solution)/shard_map/ppermute | solution.py:285
  96.9 2.7 collective-permute-start.6
  100.9 1.3 collective-permute-start.9
  102.2 4.0 %collective-permute-start.8 = (f32[16,256]{1,0:T(8,128)S(1)}, f32[16,256]{1,0:T(8,128)S(1)}, u32[]{:S(2)}, u32[]{:S(2)}) collective-permute-start(f32[16,256]{1,0:T(8,128)S(1)} %get-tuple-element.82.refs_1_), channel_id=1, source_target_pairs={{0,1},{1,2},{2,3},{3,4},{4,5},{5,6},{6,7},{7,8},{8,9},{9,10},{10,1... | collective-permute-start | bytes 49160 | tf_op jit(solution)/shard_map/ppermute | solution.py:284
  106.2 2.2 collective-permute-start.11
  108.4 4.5 %collective-permute-start.10 = (f32[16,128]{1,0:T(8,128)S(1)}, f32[16,128]{1,0:T(8,128)S(1)}, u32[]{:S(2)}, u32[]{:S(2)}) collective-permute-start(f32[16,128]{1,0:T(8,128)S(1)} %get-tuple-element.84.refs_3_), channel_id=1, source_target_pairs={{0,16},{16,32},{32,48},{48,64},{64,80},{80,96},{96,112},{112,128},... | collective-permute-start | bytes 24584 | tf_op jit(solution)/shard_map/ppermute | solution.py:284
  113.9 16.7 %all_to_all.47.refs_0_ = f32[16,8,128]{2,1,0:T(8,128)S(1)} all-to-all(f32[16,8,128]{2,1,0:T(8,128)S(1)} %get-tuple-element.85), channel_id=1, replica_groups=mesh['gx'=32,'gy'=16] {'gy'}, dimensions={0} | all-to-all | bytes 131072 | tf_op jit(solution)/shard_map/all_to_all | solution.py:333
  130.6 0.9 shard_map.72
  131.5 18.5 %all_to_all.48.refs_0_ = f32[32,8,128]{2,1,0:T(8,128)S(1)} all-to-all(f32[32,8,128]{2,1,0:T(8,128)S(1)} %shard_map.72), channel_id=1, replica_groups=mesh['gx'=32,'gy'=16] {'gx'}, dimensions={0} | all-to-all | bytes 262144 | tf_op jit(solution)/shard_map/all_to_all | solution.py:342
  150.4 1.3 collective-permute-start.13
  151.7 4.0 %collective-permute-start.12 = (f32[16,256]{1,0:T(8,128)S(1)}, f32[16,256]{1,0:T(8,128)S(1)}, u32[]{:S(2)}, u32[]{:S(2)}) collective-permute-start(f32[16,256]{1,0:T(8,128)S(1)} %get-tuple-element.92.refs_1_), channel_id=1, source_target_pairs={{0,1},{1,2},{2,3},{3,4},{4,5},{5,6},{6,7},{7,8},{8,9},{9,10},{10,1... | collective-permute-start | bytes 49160 | tf_op jit(solution)/shard_map/ppermute | solution.py:284
  155.7 2.9 %collective-permute-start.15 = (f32[16,128]{1,0:T(8,128)S(1)}, f32[16,128]{1,0:T(8,128)S(1)}, u32[]{:S(2)}, u32[]{:S(2)}) collective-permute-start(f32[16,128]{1,0:T(8,128)S(1)} %get-tuple-element.93.refs_2_), channel_id=1, source_target_pairs={{16,0},{32,16},{48,32},{64,48},{80,64},{96,80},{112,96},{128,112},... | collective-permute-start | bytes 24584 | tf_op jit(solution)/shard_map/ppermute | solution.py:285
  158.6 2.7 collective-permute-start.14
  162.6 1.3 collective-permute-start.17
  163.9 4.0 %collective-permute-start.16 = (f32[16,256]{1,0:T(8,128)S(1)}, f32[16,256]{1,0:T(8,128)S(1)}, u32[]{:S(2)}, u32[]{:S(2)}) collective-permute-start(f32[16,256]{1,0:T(8,128)S(1)} %get-tuple-element.97.refs_1_), channel_id=1, source_target_pairs={{0,1},{1,2},{2,3},{3,4},{4,5},{5,6},{6,7},{7,8},{8,9},{9,10},{10,1... | collective-permute-start | bytes 49160 | tf_op jit(solution)/shard_map/ppermute | solution.py:284
  167.9 2.2 collective-permute-start.19
  170.1 4.5 %collective-permute-start.18 = (f32[16,128]{1,0:T(8,128)S(1)}, f32[16,128]{1,0:T(8,128)S(1)}, u32[]{:S(2)}, u32[]{:S(2)}) collective-permute-start(f32[16,128]{1,0:T(8,128)S(1)} %get-tuple-element.99.refs_3_), channel_id=1, source_target_pairs={{0,16},{16,32},{32,48},{48,64},{64,80},{80,96},{96,112},{112,128},... | collective-permute-start | bytes 24584 | tf_op jit(solution)/shard_map/ppermute | solution.py:284
  175.6 16.6 %all_to_all.49.refs_0_ = f32[16,8,128]{2,1,0:T(8,128)S(1)} all-to-all(f32[16,8,128]{2,1,0:T(8,128)S(1)} %get-tuple-element.100), channel_id=1, replica_groups=mesh['gx'=32,'gy'=16] {'gy'}, dimensions={0} | all-to-all | bytes 131072 | tf_op jit(solution)/shard_map/all_to_all | solution.py:333
  192.2 0.9 shard_map.76
  193.1 18.5 %all_to_all.50.refs_0_ = f32[32,8,128]{2,1,0:T(8,128)S(1)} all-to-all(f32[32,8,128]{2,1,0:T(8,128)S(1)} %shard_map.76), channel_id=1, replica_groups=mesh['gx'=32,'gy'=16] {'gx'}, dimensions={0} | all-to-all | bytes 262144 | tf_op jit(solution)/shard_map/all_to_all | solution.py:342
  212.2 1.3 collective-permute-start.21
  213.5 4.0 %collective-permute-start.20 = (f32[16,256]{1,0:T(8,128)S(1)}, f32[16,256]{1,0:T(8,128)S(1)}, u32[]{:S(2)}, u32[]{:S(2)}) collective-permute-start(f32[16,256]{1,0:T(8,128)S(1)} %get-tuple-element.106.refs_1_), channel_id=1, source_target_pairs={{0,1},{1,2},{2,3},{3,4},{4,5},{5,6},{6,7},{7,8},{8,9},{9,10},{10,1... | collective-permute-start | bytes 49160 | tf_op jit(solution)/shard_map/ppermute | solution.py:284
  217.5 2.9 %collective-permute-start.23 = (f32[16,128]{1,0:T(8,128)S(1)}, f32[16,128]{1,0:T(8,128)S(1)}, u32[]{:S(2)}, u32[]{:S(2)}) collective-permute-start(f32[16,128]{1,0:T(8,128)S(1)} %get-tuple-element.107.refs_2_), channel_id=1, source_target_pairs={{16,0},{32,16},{48,32},{64,48},{80,64},{96,80},{112,96},{128,112},... | collective-permute-start | bytes 24584 | tf_op jit(solution)/shard_map/ppermute | solution.py:285
  220.4 2.7 collective-permute-start.22
  224.3 1.3 collective-permute-start.25
  225.6 4.0 %collective-permute-start.24 = (f32[16,256]{1,0:T(8,128)S(1)}, f32[16,256]{1,0:T(8,128)S(1)}, u32[]{:S(2)}, u32[]{:S(2)}) collective-permute-start(f32[16,256]{1,0:T(8,128)S(1)} %get-tuple-element.111.refs_1_), channel_id=1, source_target_pairs={{0,1},{1,2},{2,3},{3,4},{4,5},{5,6},{6,7},{7,8},{8,9},{9,10},{10,1... | collective-permute-start | bytes 49160 | tf_op jit(solution)/shard_map/ppermute | solution.py:284
  229.6 2.2 collective-permute-start.27
  231.9 4.5 %collective-permute-start.26 = (f32[16,128]{1,0:T(8,128)S(1)}, f32[16,128]{1,0:T(8,128)S(1)}, u32[]{:S(2)}, u32[]{:S(2)}) collective-permute-start(f32[16,128]{1,0:T(8,128)S(1)} %get-tuple-element.113.refs_3_), channel_id=1, source_target_pairs={{0,16},{16,32},{32,48},{48,64},{64,80},{80,96},{96,112},{112,128},... | collective-permute-start | bytes 24584 | tf_op jit(solution)/shard_map/ppermute | solution.py:284
  237.7 16.6 %all_to_all.51.gathered_ref = f32[16,8,128]{2,1,0:T(8,128)S(1)} all-to-all(f32[16,8,128]{2,1,0:T(8,128)S(1)} %get-tuple-element.114), channel_id=1, replica_groups=mesh['gx'=32,'gy'=16] {'gy'}, dimensions={0} | all-to-all | bytes 131072 | tf_op jit(solution)/shard_map/all_to_all | solution.py:364
  254.4 18.5 %all_to_all.52.reduced_ref = f32[32,8,128]{2,1,0:T(8,128)S(1)} all-to-all(f32[32,8,128]{2,1,0:T(8,128)S(1)} %shard_map.80), channel_id=1, replica_groups=mesh['gx'=32,'gy'=16] {'gx'}, dimensions={0} | all-to-all | bytes 262144 | tf_op jit(solution)/shard_map/all_to_all | solution.py:366
  272.8 1.2 shard_map.81
  (48 shorter events, 9.7 us)
Async XLA Ops:
  0.0 1.6 copy-start.1
  1.6 0.7 copy-start.5
  9.1 11.3 %copy-start.2 = (f32[1,1,32,768]{3,2,1,0:T(8,128)S(1)}, f32[1,1,32,768]{3,2,1,0:T(8,128)}, u32[]{:S(2)}) copy-start(f32[1,1,32,768]{3,2,1,0:T(8,128)} %param.7) | copy-start | bytes 294916
  9.1 11.3 %copy-start.3 = (f32[1,1,16,768]{3,2,1,0:T(8,128)S(1)}, f32[1,1,16,768]{3,2,1,0:T(8,128)}, u32[]{:S(2)}) copy-start(f32[1,1,16,768]{3,2,1,0:T(8,128)} %param.8) | copy-start | bytes 147460
  9.1 11.3 %copy-start.4 = (s32[1,1,768]{2,1,0:T(1,128)S(1)}, s32[1,1,768]{2,1,0:T(1,128)}, u32[]{:S(2)}) copy-start(s32[1,1,768]{2,1,0:T(1,128)} %param.10) | copy-start | bytes 9220
  9.1 39.8 %all-to-all-start = ((f32[32,32,512]{2,1,0:T(8,128)}), f32[32,32,512]{2,1,0:T(8,128)}, u32[]{:S(2)}, u32[]{:S(2)}) async-start(f32[32,32,512]{2,1,0:T(8,128)} %get-tuple-element.68), calls=%async_computation | async-start | bytes 4194304 | tf_op jit(solution)/shard_map/all_to_all | solution.py:307
  21.8 21.8 %collective-permute-start.3 = (f32[16,128]{1,0:T(8,128)S(1)}, f32[16,128]{1,0:T(8,128)S(1)}, u32[]{:S(2)}, u32[]{:S(2)}) collective-permute-start(f32[16,128]{1,0:T(8,128)S(1)} %get-tuple-element.64.refs_2_), channel_id=1, source_target_pairs={{16,0},{32,16},{48,32},{64,48},{80,64},{96,80},{112,96},{128,112},... | collective-permute-start | bytes 24584 | tf_op jit(solution)/shard_map/ppermute | solution.py:285
  24.1 19.5 %collective-permute-start.2 = (f32[16,128]{1,0:T(8,128)S(1)}, f32[16,128]{1,0:T(8,128)S(1)}, u32[]{:S(2)}, u32[]{:S(2)}) collective-permute-start(f32[16,128]{1,0:T(8,128)S(1)} %get-tuple-element.65.refs_3_), channel_id=1, source_target_pairs={{0,16},{16,32},{32,48},{48,64},{64,80},{80,96},{96,112},{112,128},... | collective-permute-start | bytes 24584 | tf_op jit(solution)/shard_map/ppermute | solution.py:284
  27.4 16.3 %collective-permute-start.1 = (f32[16,256]{1,0:T(8,128)S(1)}, f32[16,256]{1,0:T(8,128)S(1)}, u32[]{:S(2)}, u32[]{:S(2)}) collective-permute-start(f32[16,256]{1,0:T(8,128)S(1)} %get-tuple-element.62.refs_0_), channel_id=1, source_target_pairs={{1,0},{2,1},{3,2},{4,3},{5,4},{6,5},{7,6},{8,7},{9,8},{10,9},{11,1... | collective-permute-start | bytes 49160 | tf_op jit(solution)/shard_map/ppermute | solution.py:285
  28.7 15.0 %collective-permute-start = (f32[16,256]{1,0:T(8,128)S(1)}, f32[16,256]{1,0:T(8,128)S(1)}, u32[]{:S(2)}, u32[]{:S(2)}) collective-permute-start(f32[16,256]{1,0:T(8,128)S(1)} %get-tuple-element.63.refs_1_), channel_id=1, source_target_pairs={{0,1},{1,2},{2,3},{3,4},{4,5},{5,6},{6,7},{7,8},{8,9},{9,10},{10,1... | collective-permute-start | bytes 49160 | tf_op jit(solution)/shard_map/ppermute | solution.py:284
  32.7 1.7 copy-start
  88.7 11.7 %collective-permute-start.5 = (f32[16,256]{1,0:T(8,128)S(1)}, f32[16,256]{1,0:T(8,128)S(1)}, u32[]{:S(2)}, u32[]{:S(2)}) collective-permute-start(f32[16,256]{1,0:T(8,128)S(1)} %get-tuple-element.74.refs_0_), channel_id=1, source_target_pairs={{1,0},{2,1},{3,2},{4,3},{5,4},{6,5},{7,6},{8,7},{9,8},{10,9},{11,1... | collective-permute-start | bytes 49160 | tf_op jit(solution)/shard_map/ppermute | solution.py:285
  90.0 10.4 %collective-permute-start.4 = (f32[16,256]{1,0:T(8,128)S(1)}, f32[16,256]{1,0:T(8,128)S(1)}, u32[]{:S(2)}, u32[]{:S(2)}) collective-permute-start(f32[16,256]{1,0:T(8,128)S(1)} %get-tuple-element.75.refs_1_), channel_id=1, source_target_pairs={{0,1},{1,2},{2,3},{3,4},{4,5},{5,6},{6,7},{7,8},{8,9},{9,10},{10,1... | collective-permute-start | bytes 49160 | tf_op jit(solution)/shard_map/ppermute | solution.py:284
  94.0 5.6 %collective-permute-start.7 = (f32[16,128]{1,0:T(8,128)S(1)}, f32[16,128]{1,0:T(8,128)S(1)}, u32[]{:S(2)}, u32[]{:S(2)}) collective-permute-start(f32[16,128]{1,0:T(8,128)S(1)} %get-tuple-element.76.refs_2_), channel_id=1, source_target_pairs={{16,0},{32,16},{48,32},{64,48},{80,64},{96,80},{112,96},{128,112},... | collective-permute-start | bytes 24584 | tf_op jit(solution)/shard_map/ppermute | solution.py:285
  96.9 3.5 %collective-permute-start.6 = (f32[16,128]{1,0:T(8,128)S(1)}, f32[16,128]{1,0:T(8,128)S(1)}, u32[]{:S(2)}, u32[]{:S(2)}) collective-permute-start(f32[16,128]{1,0:T(8,128)S(1)} %get-tuple-element.77.refs_3_), channel_id=1, source_target_pairs={{0,16},{16,32},{32,48},{48,64},{64,80},{80,96},{96,112},{112,128},... | collective-permute-start | bytes 24584 | tf_op jit(solution)/shard_map/ppermute | solution.py:284
  100.9 12.8 %collective-permute-start.9 = (f32[16,256]{1,0:T(8,128)S(1)}, f32[16,256]{1,0:T(8,128)S(1)}, u32[]{:S(2)}, u32[]{:S(2)}) collective-permute-start(f32[16,256]{1,0:T(8,128)S(1)} %get-tuple-element.81.refs_0_), channel_id=1, source_target_pairs={{1,0},{2,1},{3,2},{4,3},{5,4},{6,5},{7,6},{8,7},{9,8},{10,9},{11,1... | collective-permute-start | bytes 49160 | tf_op jit(solution)/shard_map/ppermute | solution.py:285
  102.2 11.5 %collective-permute-start.8 = (f32[16,256]{1,0:T(8,128)S(1)}, f32[16,256]{1,0:T(8,128)S(1)}, u32[]{:S(2)}, u32[]{:S(2)}) collective-permute-start(f32[16,256]{1,0:T(8,128)S(1)} %get-tuple-element.82.refs_1_), channel_id=1, source_target_pairs={{0,1},{1,2},{2,3},{3,4},{4,5},{5,6},{6,7},{7,8},{8,9},{9,10},{10,1... | collective-permute-start | bytes 49160 | tf_op jit(solution)/shard_map/ppermute | solution.py:284
  106.2 6.7 %collective-permute-start.11 = (f32[16,128]{1,0:T(8,128)S(1)}, f32[16,128]{1,0:T(8,128)S(1)}, u32[]{:S(2)}, u32[]{:S(2)}) collective-permute-start(f32[16,128]{1,0:T(8,128)S(1)} %get-tuple-element.83.refs_2_), channel_id=1, source_target_pairs={{16,0},{32,16},{48,32},{64,48},{80,64},{96,80},{112,96},{128,112},... | collective-permute-start | bytes 24584 | tf_op jit(solution)/shard_map/ppermute | solution.py:285
  108.4 5.2 %collective-permute-start.10 = (f32[16,128]{1,0:T(8,128)S(1)}, f32[16,128]{1,0:T(8,128)S(1)}, u32[]{:S(2)}, u32[]{:S(2)}) collective-permute-start(f32[16,128]{1,0:T(8,128)S(1)} %get-tuple-element.84.refs_3_), channel_id=1, source_target_pairs={{0,16},{16,32},{32,48},{48,64},{64,80},{80,96},{96,112},{112,128},... | collective-permute-start | bytes 24584 | tf_op jit(solution)/shard_map/ppermute | solution.py:284
  150.4 11.6 %collective-permute-start.13 = (f32[16,256]{1,0:T(8,128)S(1)}, f32[16,256]{1,0:T(8,128)S(1)}, u32[]{:S(2)}, u32[]{:S(2)}) collective-permute-start(f32[16,256]{1,0:T(8,128)S(1)} %get-tuple-element.91.refs_0_), channel_id=1, source_target_pairs={{1,0},{2,1},{3,2},{4,3},{5,4},{6,5},{7,6},{8,7},{9,8},{10,9},{11,1... | collective-permute-start | bytes 49160 | tf_op jit(solution)/shard_map/ppermute | solution.py:285
  151.7 10.4 %collective-permute-start.12 = (f32[16,256]{1,0:T(8,128)S(1)}, f32[16,256]{1,0:T(8,128)S(1)}, u32[]{:S(2)}, u32[]{:S(2)}) collective-permute-start(f32[16,256]{1,0:T(8,128)S(1)} %get-tuple-element.92.refs_1_), channel_id=1, source_target_pairs={{0,1},{1,2},{2,3},{3,4},{4,5},{5,6},{6,7},{7,8},{8,9},{9,10},{10,1... | collective-permute-start | bytes 49160 | tf_op jit(solution)/shard_map/ppermute | solution.py:284
  155.7 5.6 %collective-permute-start.15 = (f32[16,128]{1,0:T(8,128)S(1)}, f32[16,128]{1,0:T(8,128)S(1)}, u32[]{:S(2)}, u32[]{:S(2)}) collective-permute-start(f32[16,128]{1,0:T(8,128)S(1)} %get-tuple-element.93.refs_2_), channel_id=1, source_target_pairs={{16,0},{32,16},{48,32},{64,48},{80,64},{96,80},{112,96},{128,112},... | collective-permute-start | bytes 24584 | tf_op jit(solution)/shard_map/ppermute | solution.py:285
  158.6 3.5 %collective-permute-start.14 = (f32[16,128]{1,0:T(8,128)S(1)}, f32[16,128]{1,0:T(8,128)S(1)}, u32[]{:S(2)}, u32[]{:S(2)}) collective-permute-start(f32[16,128]{1,0:T(8,128)S(1)} %get-tuple-element.94.refs_3_), channel_id=1, source_target_pairs={{0,16},{16,32},{32,48},{48,64},{64,80},{80,96},{96,112},{112,128},... | collective-permute-start | bytes 24584 | tf_op jit(solution)/shard_map/ppermute | solution.py:284
  162.6 12.8 %collective-permute-start.17 = (f32[16,256]{1,0:T(8,128)S(1)}, f32[16,256]{1,0:T(8,128)S(1)}, u32[]{:S(2)}, u32[]{:S(2)}) collective-permute-start(f32[16,256]{1,0:T(8,128)S(1)} %get-tuple-element.96.refs_0_), channel_id=1, source_target_pairs={{1,0},{2,1},{3,2},{4,3},{5,4},{6,5},{7,6},{8,7},{9,8},{10,9},{11,1... | collective-permute-start | bytes 49160 | tf_op jit(solution)/shard_map/ppermute | solution.py:285
  163.9 11.5 %collective-permute-start.16 = (f32[16,256]{1,0:T(8,128)S(1)}, f32[16,256]{1,0:T(8,128)S(1)}, u32[]{:S(2)}, u32[]{:S(2)}) collective-permute-start(f32[16,256]{1,0:T(8,128)S(1)} %get-tuple-element.97.refs_1_), channel_id=1, source_target_pairs={{0,1},{1,2},{2,3},{3,4},{4,5},{5,6},{6,7},{7,8},{8,9},{9,10},{10,1... | collective-permute-start | bytes 49160 | tf_op jit(solution)/shard_map/ppermute | solution.py:284
  167.9 6.7 %collective-permute-start.19 = (f32[16,128]{1,0:T(8,128)S(1)}, f32[16,128]{1,0:T(8,128)S(1)}, u32[]{:S(2)}, u32[]{:S(2)}) collective-permute-start(f32[16,128]{1,0:T(8,128)S(1)} %get-tuple-element.98.refs_2_), channel_id=1, source_target_pairs={{16,0},{32,16},{48,32},{64,48},{80,64},{96,80},{112,96},{128,112},... | collective-permute-start | bytes 24584 | tf_op jit(solution)/shard_map/ppermute | solution.py:285
  170.1 5.2 %collective-permute-start.18 = (f32[16,128]{1,0:T(8,128)S(1)}, f32[16,128]{1,0:T(8,128)S(1)}, u32[]{:S(2)}, u32[]{:S(2)}) collective-permute-start(f32[16,128]{1,0:T(8,128)S(1)} %get-tuple-element.99.refs_3_), channel_id=1, source_target_pairs={{0,16},{16,32},{32,48},{48,64},{64,80},{80,96},{96,112},{112,128},... | collective-permute-start | bytes 24584 | tf_op jit(solution)/shard_map/ppermute | solution.py:284
  212.2 11.6 %collective-permute-start.21 = (f32[16,256]{1,0:T(8,128)S(1)}, f32[16,256]{1,0:T(8,128)S(1)}, u32[]{:S(2)}, u32[]{:S(2)}) collective-permute-start(f32[16,256]{1,0:T(8,128)S(1)} %get-tuple-element.105.refs_0_), channel_id=1, source_target_pairs={{1,0},{2,1},{3,2},{4,3},{5,4},{6,5},{7,6},{8,7},{9,8},{10,9},{11,1... | collective-permute-start | bytes 49160 | tf_op jit(solution)/shard_map/ppermute | solution.py:285
  213.5 10.4 %collective-permute-start.20 = (f32[16,256]{1,0:T(8,128)S(1)}, f32[16,256]{1,0:T(8,128)S(1)}, u32[]{:S(2)}, u32[]{:S(2)}) collective-permute-start(f32[16,256]{1,0:T(8,128)S(1)} %get-tuple-element.106.refs_1_), channel_id=1, source_target_pairs={{0,1},{1,2},{2,3},{3,4},{4,5},{5,6},{6,7},{7,8},{8,9},{9,10},{10,1... | collective-permute-start | bytes 49160 | tf_op jit(solution)/shard_map/ppermute | solution.py:284
  217.5 5.6 %collective-permute-start.23 = (f32[16,128]{1,0:T(8,128)S(1)}, f32[16,128]{1,0:T(8,128)S(1)}, u32[]{:S(2)}, u32[]{:S(2)}) collective-permute-start(f32[16,128]{1,0:T(8,128)S(1)} %get-tuple-element.107.refs_2_), channel_id=1, source_target_pairs={{16,0},{32,16},{48,32},{64,48},{80,64},{96,80},{112,96},{128,112},... | collective-permute-start | bytes 24584 | tf_op jit(solution)/shard_map/ppermute | solution.py:285
  220.4 3.5 %collective-permute-start.22 = (f32[16,128]{1,0:T(8,128)S(1)}, f32[16,128]{1,0:T(8,128)S(1)}, u32[]{:S(2)}, u32[]{:S(2)}) collective-permute-start(f32[16,128]{1,0:T(8,128)S(1)} %get-tuple-element.108.refs_3_), channel_id=1, source_target_pairs={{0,16},{16,32},{32,48},{48,64},{64,80},{80,96},{96,112},{112,128},... | collective-permute-start | bytes 24584 | tf_op jit(solution)/shard_map/ppermute | solution.py:284
  224.3 12.8 %collective-permute-start.25 = (f32[16,256]{1,0:T(8,128)S(1)}, f32[16,256]{1,0:T(8,128)S(1)}, u32[]{:S(2)}, u32[]{:S(2)}) collective-permute-start(f32[16,256]{1,0:T(8,128)S(1)} %get-tuple-element.110.refs_0_), channel_id=1, source_target_pairs={{1,0},{2,1},{3,2},{4,3},{5,4},{6,5},{7,6},{8,7},{9,8},{10,9},{11,1... | collective-permute-start | bytes 49160 | tf_op jit(solution)/shard_map/ppermute | solution.py:285
  225.6 11.5 %collective-permute-start.24 = (f32[16,256]{1,0:T(8,128)S(1)}, f32[16,256]{1,0:T(8,128)S(1)}, u32[]{:S(2)}, u32[]{:S(2)}) collective-permute-start(f32[16,256]{1,0:T(8,128)S(1)} %get-tuple-element.111.refs_1_), channel_id=1, source_target_pairs={{0,1},{1,2},{2,3},{3,4},{4,5},{5,6},{6,7},{7,8},{8,9},{9,10},{10,1... | collective-permute-start | bytes 49160 | tf_op jit(solution)/shard_map/ppermute | solution.py:284
  229.6 6.7 %collective-permute-start.27 = (f32[16,128]{1,0:T(8,128)S(1)}, f32[16,128]{1,0:T(8,128)S(1)}, u32[]{:S(2)}, u32[]{:S(2)}) collective-permute-start(f32[16,128]{1,0:T(8,128)S(1)} %get-tuple-element.112.refs_2_), channel_id=1, source_target_pairs={{16,0},{32,16},{48,32},{64,48},{80,64},{96,80},{112,96},{128,112},... | collective-permute-start | bytes 24584 | tf_op jit(solution)/shard_map/ppermute | solution.py:285
  231.9 5.2 %collective-permute-start.26 = (f32[16,128]{1,0:T(8,128)S(1)}, f32[16,128]{1,0:T(8,128)S(1)}, u32[]{:S(2)}, u32[]{:S(2)}) collective-permute-start(f32[16,128]{1,0:T(8,128)S(1)} %get-tuple-element.113.refs_3_), channel_id=1, source_target_pairs={{0,16},{16,32},{32,48},{48,64},{64,80},{80,96},{96,112},{112,128},... | collective-permute-start | bytes 24584 | tf_op jit(solution)/shard_map/ppermute | solution.py:284

commit v3 on v2

v3 whole, which is shorter than its diff:
```python
import functools
import jax
import jax.numpy as jnp
from jax import lax
from jax.experimental import pallas as pl
from jax.experimental.pallas import tpu as pltpu
from jax.sharding import PartitionSpec as P

EW = 256
ES = 128
MB = 128
ITERS = 3
LANES = 128
ROWS = 8
LIMIT = 20 << 20

highest = lax.Precision.HIGHEST
epsilon = 1e-06
VMEM = pl.BlockSpec(memory_space=pltpu.VMEM)
SMEM = pl.BlockSpec(memory_space=pltpu.SMEM)


def dot(a, b, dims=((1,), (0,))):
    return lax.dot_general(
        a, b, (dims, ((), ())), precision=highest, preferred_element_type=jnp.float32
    )


def split(value):
    high = value.astype(jnp.bfloat16)
    return high, (value - high.astype(jnp.float32)).astype(jnp.bfloat16)


def narrow_dot(a, b, dims=((1,), (0,))):
    return lax.dot_general(a, b, (dims, ((), ())), preferred_element_type=jnp.float32)


def call(kernel, outs, args, flops=1 << 20, specs=None, scratch=()):
    outs = [jax.ShapeDtypeStruct(shape, dtype) for shape, dtype in outs]
    moved = sum(a.size * a.dtype.itemsize for a in args) + sum(
        o.size * o.dtype.itemsize for o in outs
    )
    return pl.pallas_call(
        kernel,
        out_shape=outs,
        in_specs=specs or [VMEM] * len(args),
        out_specs=[VMEM] * len(outs),
        scratch_shapes=scratch,
        compiler_params=pltpu.CompilerParams(vmem_limit_bytes=LIMIT),
        cost_estimate=pl.CostEstimate(flops=flops, bytes_accessed=moved, transcendentals=0),
    )(*args)


def sides(cells):
    return ((0, EW), (EW, 2 * EW), (2 * EW, 2 * EW + ES), (2 * EW + ES, cells))


def sublane_mask(rows, loads):
    row = lax.broadcasted_iota(jnp.int32, (rows, LANES), 0)
    lane = lax.broadcasted_iota(jnp.int32, (rows, LANES), 1)
    return lax.rem(row, ROWS) == lax.div(lane, loads)


def pack(rows, loads):
    kept = jnp.where(sublane_mask(rows.shape[0], loads), rows, 0.0)
    return jnp.sum(kept.reshape(rows.shape[0] // ROWS, ROWS, LANES), axis=1)


def column_of(row, loads):
    a = lax.broadcasted_iota(jnp.int32, (loads, LANES), 0)
    b = lax.broadcasted_iota(jnp.int32, (loads, LANES), 1)
    return jnp.sum(jnp.where(a == b, row, 0.0), axis=1, keepdims=True)


def row_of(column, loads):
    a = lax.broadcasted_iota(jnp.int32, (loads, LANES), 0)
    b = lax.broadcasted_iota(jnp.int32, (loads, LANES), 1)
    return jnp.sum(jnp.where(a == lax.rem(b, loads), column, 0.0), axis=0, keepdims=True)


def one_hot(map_row, block):
    inside = map_row[:, block * MB : (block + 1) * MB] - block * MB
    spot = lax.broadcasted_iota(jnp.int32, (MB, MB), 0)
    return jnp.where(spot == inside, 1.0, 0.0)


def route_kernel(slot_ref, rows_ref, out_ref, token_ref):
    groups, modes, width = out_ref.shape
    per_tile = LANES // modes
    tiles = width // LANES
    owner = lax.broadcasted_iota(jnp.int32, (modes, LANES), 1) // modes

    def step(group, carry):
        for tile in range(tiles):
            block = jnp.zeros((modes, LANES), jnp.float32)
            for part in range(per_tile):
                slot = slot_ref[(group * tiles + tile) * per_tile + part]
                home = lax.shift_right_logical(slot, per_tile.bit_length() - 1)
                source = rows_ref[:, pl.ds(pl.multiple_of(home * LANES, LANES), LANES)]
                shift = ((part - slot) & (per_tile - 1)) * modes
                block = jnp.where(owner == part, pltpu.roll(source, shift, 1), block)
            out_ref[group, :, tile * LANES : (tile + 1) * LANES] = block
        return carry

    lax.fori_loop(0, groups, step, 0, unroll=2)
    token_ref[...] = jnp.zeros_like(token_ref)


def parities():
    return [lax.axis_index(axis) % 2 == 1 for axis in ("gy", "gx")]


def outgoing(field, refs):
    odd_column, odd_row = parities()
    west, east, south, north = (field[:, a:b] for a, b in sides(field.shape[1]))
    refs[0][...] = jnp.where(odd_column, west, east)
    refs[1][...] = jnp.where(odd_column, east, west)
    if len(refs) > 2:
        refs[2][...] = jnp.where(odd_row, south, north)
        refs[3][...] = jnp.where(odd_row, north, south)


def incoming(first, second, odd):
    return jnp.where(odd, first, second), jnp.where(odd, second, first)


def joined(field, others):
    odd_column, odd_row = parities()
    found = [*incoming(others[0], others[1], odd_column)]
    if len(others) > 2:
        found += incoming(others[2], others[3], odd_row)
    parts = [
        field[:, start:stop] + other for (start, stop), other in zip(sides(field.shape[1]), found)
    ]
    return jnp.concatenate(parts + [field[:, 2 * EW :]] * (len(others) == 2), axis=1)


def prepare_kernel(map_ref, basis_ref, loads_ref, token_ref, frame_ref, field_ref, *edge_refs):
    modes, cells = basis_ref.shape
    loads = loads_ref.shape[0]
    map_row = map_ref[...]
    both = jnp.concatenate([loads_ref[...], basis_ref[...]], axis=0)
    moved = jnp.concatenate(
        [
            dot(both[:, block * MB : (block + 1) * MB], one_hot(map_row, block), ((1,), (1,)))
            for block in range(cells // MB)
        ],
        axis=1,
    )
    high, low = split(moved[loads:])
    frame_ref[:modes, :] = high
    frame_ref[modes:, :] = low
    field_ref[...] = moved[:loads]
    outgoing(moved[:loads], edge_refs[:2])
    odd_row = parities()[1]
    south, north = (moved[:, start:stop] for start, stop in sides(cells)[2:])
    edge_refs[2][...] = jnp.where(odd_row, south, north)
    edge_refs[3][...] = jnp.where(odd_row, north, south)


def reorder_kernel(map_ref, schur_ref, token_ref, high_ref, low_ref):
    cells = schur_ref.shape[0]
    map_row = map_ref[...]
    hots = [one_hot(map_row, block).astype(jnp.bfloat16) for block in range(cells // MB)]
    for i, left in enumerate(hots):
        span_i = slice(i * MB, (i + 1) * MB)
        for part, out_ref in zip(split(schur_ref[span_i, :]), (high_ref, low_ref)):
            rows = narrow_dot(left, part).astype(jnp.bfloat16)
            for j, right in enumerate(hots):
                span = slice(j * MB, (j + 1) * MB)
                out_ref[span_i, span] = narrow_dot(rows[:, span], right, ((1,), (1,))).astype(
                    jnp.bfloat16
                )


def stacked(value):
    return jnp.concatenate(split(value), axis=0)


def coefficients(field, frame):
    loads, modes = field.shape[0], frame.shape[0] // 2
    copies = [jnp.concatenate([part] * (LANES // loads), axis=0) for part in split(field)]
    both = narrow_dot(frame, jnp.concatenate(copies, axis=0), ((1,), (1,)))
    both = both[:, :LANES] + both[:, LANES:]
    return pack(both[:modes] + both[modes:], loads)


def begin_kernel(own_ref, *refs):
    others = [ref[...] for ref in refs[:4]]
    frame_ref, residual_ref, out_ref, south_ref, north_ref = refs[4:]
    loads = own_ref.shape[0]
    south, north = incoming(others[2], others[3], parities()[1])
    south_ref[...] = stacked(south[loads:])
    north_ref[...] = stacked(north[loads:])
    field = joined(own_ref[...], others[:2] + [other[:loads] for other in others[2:]])
    residual_ref[...] = field
    coeffs = coefficients(field, frame_ref[...])
    payload = jnp.concatenate([coeffs, jnp.zeros_like(coeffs)], axis=0)
    out_ref[...] = jnp.broadcast_to(payload[None], out_ref.shape)


def gather_kernel(more, own_ref, *refs):
    others = [ref[...] for ref in refs[:4]]
    residual_ref, refs = refs[4], refs[5:]
    out_ref = refs[-1]
    field = joined(own_ref[...], others)
    loads = field.shape[0]
    if more:
        frame_ref, field_ref = refs[:2]
        field_ref[...] = field
        coeffs = coefficients(field, frame_ref[...])
    else:
        coeffs = jnp.zeros((4, LANES), jnp.float32)
    totals = [
        row_of(jnp.sum(other * field, axis=1, keepdims=True), loads)
        for other in (residual_ref[...], field)
    ]
    payload = jnp.concatenate([coeffs, *totals, jnp.zeros((2, LANES), jnp.float32)], axis=0)
    out_ref[...] = jnp.broadcast_to(payload[None], out_ref.shape)


def expanded(loads, gathered_ref, wide_ref):
    quads = wide_ref.shape[0] // (gathered_ref.shape[0] * ROWS)
    keep = sublane_mask(ROWS, loads)
    for column in range(gathered_ref.shape[0]):
        for quad in range(quads):
            row = gathered_ref[column, quad : quad + 1, :]
            start = (column * quads + quad) * ROWS
            wide_ref[start : start + ROWS, :] = jnp.where(keep, row, 0.0)
    wide = wide_ref[...]
    shift = LANES // 2
    while shift >= loads:
        wide = wide + pltpu.roll(wide, shift, 1)
        shift //= 2
    tail = jnp.sum(gathered_ref[...], axis=0)[quads:, :]
    return jnp.concatenate(split(wide), axis=1), tail


def coarse_kernel(loads, first, *refs):
    if first:
        gathered_ref, matrix_ref, out_ref, high_ref, low_ref, wide_ref = refs
        high, low = split(matrix_ref[...])
        high_ref[...] = high
        low_ref[...] = low
    else:
        gathered_ref, high_ref, low_ref, out_ref, wide_ref = refs
        high, low = high_ref[...], low_ref[...]
    right, tail = expanded(loads, gathered_ref, wide_ref)
    groups = out_ref.shape[0]
    quads = high_ref.shape[0] // (groups * ROWS)
    product = narrow_dot(high, right) + narrow_dot(low, right)
    packed = pack(product[:, :LANES] + product[:, LANES:], loads)
    nothing = jnp.zeros((quads, LANES), jnp.float32)
    blocks = [packed[group * quads : (group + 1) * quads, :] for group in range(groups)]
    blocks = [nothing, *blocks, nothing]
    for group in range(groups):
        out_ref[group] = jnp.concatenate(
            [blocks[group + 1], blocks[group], blocks[group + 2], tail], axis=0
        )


def lift_kernel(iteration, *refs):
    refs = list(refs)
    reduced_ref, frame_ref, south_ref, north_ref, residual_ref = refs[:5]
    refs = refs[5:]
    residual = residual_ref[...]
    loads, cells = residual.shape
    quads = frame_ref.shape[0] // (2 * ROWS)
    sums = jnp.sum(reduced_ref[...], axis=0)
    lifted = sums
    if iteration:
        image_ref, search_ref, lifted_ref = refs[:3]
        refs = refs[3:]
        solution_ref = refs.pop(0) if iteration > 1 else None
        residual_out, solution_out = refs[:2]
        refs = refs[2:]
        stride_row = sums[3 * quads : 3 * quads + 1, :] / (
            sums[3 * quads + 1 : 3 * quads + 2, :] + epsilon
        )
        stride = column_of(stride_row, loads)
        residual = residual - stride * image_ref[...]
        residual_out[...] = residual
        step = stride * search_ref[...]
        solution_out[...] = step if solution_ref is None else solution_ref[...] + step
        lifted = lifted_ref[...] - stride_row * sums
    lifted_out, base_out, edges = refs[0], refs[1], refs[2:]
    lifted_out[...] = lifted
    keep = sublane_mask(ROWS, loads)
    a = lax.broadcasted_iota(jnp.int32, (loads, LANES), 0)
    b = lax.broadcasted_iota(jnp.int32, (loads, LANES), 1)
    fold = jnp.where(a == lax.rem(b, loads), 1.0, 0.0).astype(jnp.bfloat16)

    def spread(part, other_frame):
        rows = lifted[part * quads : (part + 1) * quads, :]
        wide = jnp.concatenate(
            [jnp.where(keep, rows[quad : quad + 1, :], 0.0) for quad in range(quads)], axis=0
        )
        left = jnp.concatenate(
            [
                jnp.concatenate([half, half], axis=1)
                for half in (
                    narrow_dot(fold, piece, ((1,), (1,))).astype(jnp.bfloat16)
                    for piece in split(wide)
                )
            ],
            axis=0,
        )
        both = narrow_dot(left, other_frame)
        return both[:loads] + both[loads:]

    own = spread(0, frame_ref[...])
    outgoing(own, edges)
    base = residual + own
    low, middle = sides(cells)[2]
    base_out[:, :low] = base[:, :low]
    base_out[:, low:middle] = base[:, low:middle] + spread(1, south_ref[...])
    base_out[:, middle:] = base[:, middle:] + spread(2, north_ref[...])


def schur_kernel(base_ref, first_ref, second_ref, high_ref, low_ref, search_ref, image_ref, *edges):
    search = joined(base_ref[...], [first_ref[...], second_ref[...]])
    search_ref[...] = search
    loads = search.shape[0]
    left = stacked(search)
    both = narrow_dot(left, high_ref[...]) + narrow_dot(left, low_ref[...])
    image = both[:loads] + both[loads:]
    image_ref[...] = image
    outgoing(image, edges)


def total_kernel(gathered_ref, out_ref):
    out_ref[...] = jnp.broadcast_to(jnp.sum(gathered_ref[...], axis=0)[None], out_ref.shape)


def finish_kernel(reduced_ref, solution_ref, search_ref, map_ref, out_ref):
    loads, cells = solution_ref.shape
    sums = jnp.sum(reduced_ref[...], axis=0)
    stride = column_of(sums[4:5, :] / (sums[5:6, :] + epsilon), loads)
    result = solution_ref[...] + stride * search_ref[...]
    map_row = map_ref[...]
    for block in range(cells // MB):
        span = slice(block * MB, (block + 1) * MB)
        out_ref[:, span] = dot(result[:, span], one_hot(map_row, block))


def exchange(edges):
    found = []
    for number, edge in enumerate(edges):
        axis, start = ("gy", "gx")[number // 2], number % 2
        pairs = []
        for low in range(start, lax.axis_size(axis) - 1, 2):
            pairs += [(low, low + 1), (low + 1, low)]
        found.append(lax.ppermute(edge, axis, pairs))
    return found


def per_device(schur_blocks, basis, loads, coarse_inverse, iface_map, coarse_slot):
    f32, bf16 = jnp.float32, jnp.bfloat16
    columns = lax.axis_size("gy")
    groups = lax.axis_size("gx")
    count, cells = loads.shape[2:]
    modes = basis.shape[2]
    field = ((count, cells), f32)
    column_edges = [((count, EW), f32)] * 2
    edges_of = column_edges + [((count, ES), f32)] * 2
    packed = ((2 * ROWS, LANES), f32)
    along = ((columns, ROWS, LANES), f32)
    across = ((groups, 2 * ROWS, LANES), f32)

    routed, token = call(
        route_kernel,
        [((groups, modes, columns * modes), f32), ((ROWS, LANES), f32)],
        [coarse_slot, coarse_inverse],
        specs=[SMEM, VMEM],
    )
    matrix = lax.all_to_all(routed, "gx", 0, 0, tiled=True)
    matrix = matrix.reshape(groups * modes, columns * modes)

    frame, own, *edges = call(
        prepare_kernel,
        [((2 * modes, cells), bf16), field]
        + column_edges
        + [((count + modes, ES), f32)] * 2,
        [iface_map[0], basis[0, 0], loads[0, 0], token],
    )
    residual, payload, south, north = call(
        begin_kernel,
        [field, along] + [((2 * modes, ES), bf16)] * 2,
        [own, *exchange(edges), frame],
    )
    schur = call(
        reorder_kernel,
        [((cells, cells), bf16)] * 2,
        [iface_map[0], schur_blocks[0, 0], token],
        flops=1 << 28,
    )
    frames = [frame, south, north]
    split_shape = (matrix.shape, bf16)
    wide = [pltpu.VMEM((columns * modes, LANES), f32)]
    solution = image = search = lifted = None
    for iteration in range(ITERS):
        first = iteration == 0
        if first:
            payload, matrix, *schur = lax.optimization_barrier((payload, matrix, *schur))
        gathered = lax.all_to_all(payload, "gy", 0, 0, tiled=True)
        partial, *parts = call(
            functools.partial(coarse_kernel, count, first),
            [across] + [split_shape] * (2 * first),
            [gathered, matrix] if first else [gathered, *halves],
            flops=1 << 29,
            scratch=wide,
        )
        halves = parts if first else halves
        reduced = lax.all_to_all(partial, "gx", 0, 0, tiled=True)
        known = [image, search, lifted] if iteration else []
        found = call(
            functools.partial(lift_kernel, iteration),
            [field] * (2 if iteration else 0) + [packed, field, *column_edges],
            [reduced, *frames, residual, *known] + ([solution] if iteration > 1 else []),
        )
        if iteration:
            residual, solution, *found = found
        lifted, base, *edges = found
        search, local, *edges = call(
            schur_kernel,
            [field, field, *edges_of],
            [base, *exchange(edges), *schur],
            flops=1 << 27,
        )
        more = iteration < ITERS - 1
        found = call(
            functools.partial(gather_kernel, more),
            [field] * more + [along],
            [local, *exchange(edges), residual] + [frame] * more,
        )
        image, payload = found if more else (None, found[0])
    gathered = lax.all_to_all(payload, "gy", 0, 0, tiled=True)
    (partial,) = call(total_kernel, [((groups, ROWS, LANES), f32)], [gathered])
    reduced = lax.all_to_all(partial, "gx", 0, 0, tiled=True)
    (result,) = call(finish_kernel, [field], [reduced, solution, search, iface_map[0]])
    return result[None, None]


def solution(mesh):
    placed = (
        P("gx", "gy", None, None),
        P("gx", "gy", None, None),
        P("gx", "gy", None, None),
        P(("gx", "gy"), None),
        P("gx", "gy", None),
        P(),
    )
    return jax.shard_map(
        per_device, mesh=mesh, in_specs=placed, out_specs=P("gx", "gy", None, None), check_vma=False
    )
```

time: 275 us -> 255 us (0.927)
  starting transfers between devices: 90.5 us -> 64 us
  waiting for transfers between devices: 16 us -> 27.7 us
  blocking collectives: 142 us -> 138 us
    ppermute x28 -> x22, starting transfers between devices: 79.2 us -> 52.6 us  [exchange(): found.append(lax.ppermute(edge, axis, pairs))]
    ppermute x28 -> x22, waiting for transfers between devices: 11 us -> 24.5 us  [exchange(): found.append(lax.ppermute(edge, axis, pairs))]
    all_to_all x4, blocking collectives: 68.6 us -> 58.6 us  [per_device(): reduced = lax.all_to_all(partial, 'gx', 0, 0, tiled=True)]
    all_to_all x4, blocking collectives: 73.5 us -> 79.7 us  [per_device(): gathered = lax.all_to_all(payload, 'gy', 0, 0, tiled=True)]
  transfers between devices with their start and end apart: 29 -> 23, of which waited for: 8 -> 8; matrix products, arithmetic and copies ran while one was open for 0% -> 0% of each run, Pallas kernels for 2% -> 2%
where the time goes in v3:
time: 255 us; the launch traced here: 254 us
  blocking collectives  138 us (54%)
  starting transfers between devices  64 us (25%)
  waiting for transfers between devices  27.7 us (11%)
  Pallas kernels  19.4 us (8%)
  local copies, waits for them, and re-layouts  3.94 us (2%)
    all_to_all x4, blocking collectives, per_device(): gathered = lax.all_to_all(payload, 'gy', 0, 0, tiled=True)  79.7 us
    all_to_all x4, blocking collectives, per_device(): reduced = lax.all_to_all(partial, 'gx', 0, 0, tiled=True)  58.6 us
    ppermute x22, starting transfers between devices, exchange(): found.append(lax.ppermute(edge, axis, pairs))  52.6 us
    ppermute x22, waiting for transfers between devices, exchange(): found.append(lax.ppermute(edge, axis, pairs))  24.5 us
    pallas_call x18, Pallas kernels, call(): pl.pallas_call(kernel, out_shape=outs, in_specs=specs or [VMEM] * len(arg...  19.4 us
    all_to_all x1, starting transfers between devices, per_device(): matrix = lax.all_to_all(routed, 'gx', 0, 0, tiled=True)  11.3 us
  transfers between devices with their start and end apart: 23, of which 8 were waited for; matrix products, arithmetic and copies ran while one was open for 0% of the time, Pallas kernels for 2%

profile of v3, /device:TPU:1, one launch (start us, length us, event | category | flops | bytes accessed | tf_op | source)
XLA Modules:
  0.0 253.6 jit_solution(11317339407049070430)
XLA Ops:
  0.0 1.6 copy-done.1
  1.6 0.7 copy-done.5
  2.3 5.2 %shard_map.64 = (f32[32,32,512]{2,1,0:T(8,128)}, f32[8,128]{1,0:T(8,128)S(1)}) custom-call(s32[512]{0:T(512)S(1)} %copy-done.5, f32[32,16384]{1,0:T(8,128)S(1)} %copy-done.1), custom_call_target="tpu_custom_call" | custom-call | flops 1048576 | bytes 4200448 | tf_op jit(solution)/shard_map/pallas_call | solution.py:43
  7.5 11.3 %all-to-all-start = ((f32[32,32,512]{2,1,0:T(8,128)}), f32[32,32,512]{2,1,0:T(8,128)}, u32[]{:S(2)}, u32[]{:S(2)}) async-start(f32[32,32,512]{2,1,0:T(8,128)} %get-tuple-element.71), calls=%async_computation | async-start | bytes 4194304 | tf_op jit(solution)/shard_map/all_to_all | solution.py:376
  18.8 0.7 shard_map.65
  19.5 1.9 collective-permute-start
  21.5 0.7 collective-permute-start.1
  22.1 2.3 collective-permute-start.2
  24.5 3.2 %collective-permute-start.3 = (f32[48,128]{1,0:T(8,128)S(1)}, f32[48,128]{1,0:T(8,128)S(1)}, u32[]{:S(2)}, u32[]{:S(2)}) collective-permute-start(f32[48,128]{1,0:T(8,128)S(1)} %get-tuple-element.68), channel_id=1, source_target_pairs={{16,32},{32,16},{48,64},{64,48},{80,96},{96,80},{112,128},{128,112... | collective-permute-start | bytes 73736 | tf_op jit(solution)/shard_map/ppermute | solution.py:353
  27.7 1.7 copy-done
  29.4 2.9 %shard_map.67 = (bf16[768,768]{1,0:T(8,128)(2,1)S(1)}, bf16[768,768]{1,0:T(8,128)(2,1)S(1)}) custom-call(s32[1,768]{1,0:T(1,128)S(1)} %bitcast.10, f32[768,768]{1,0:T(8,128)S(1)} %bitcast.6, f32[8,128]{1,0:T(8,128)S(1)} %get-tuple-element.63.token_ref), custom_call_target="tpu_custom_call" | custom-call | flops 268435456 | bytes 4725760 | tf_op jit(solution)/shard_map/pallas_call | solution.py:43
  32.4 11.4 %collective-permute-done.3.refs_3_ = f32[48,128]{1,0:T(8,128)S(1)} collective-permute-done((f32[48,128]{1,0:T(8,128)S(1)}, f32[48,128]{1,0:T(8,128)S(1)}, u32[]{:S(2)}, u32[]{:S(2)}) %collective-permute-start.3) | collective-permute-done | bytes 24608 | tf_op jit(solution)/shard_map/ppermute | solution.py:353
  44.0 3.2 %all-to-all-done = f32[32,32,512]{2,1,0:T(8,128)} async-done(((f32[32,32,512]{2,1,0:T(8,128)}), f32[32,32,512]{2,1,0:T(8,128)}, u32[]{:S(2)}, u32[]{:S(2)}) %all-to-all-start) | async-done | bytes 2097184 | tf_op jit(solution)/shard_map/all_to_all | solution.py:376
  47.3 23.7 %all_to_all.45.refs_0_ = f32[16,8,128]{2,1,0:T(8,128)S(1)} all-to-all(f32[16,8,128]{2,1,0:T(8,128)S(1)} %get-tuple-element.74), channel_id=1, replica_groups=mesh['gx'=32,'gy'=16] {'gy'}, dimensions={0} | all-to-all | bytes 131072 | tf_op jit(solution)/shard_map/all_to_all | solution.py:405
  70.9 2.6 %shard_map.68 = (f32[32,16,128]{2,1,0:T(8,128)S(1)}, bf16[1024,512]{1,0:T(8,128)(2,1)S(1)}, bf16[1024,512]{1,0:T(8,128)(2,1)S(1)}) custom-call(f32[16,8,128]{2,1,0:T(8,128)S(1)} %all_to_all.45.refs_0_, f32[1024,512]{1,0:T(8,128)} %bitcast.3.refs_1_), custom_call_target="tpu_custom_call" | custom-call | flops 536870912 | bytes 4521984 | tf_op jit(solution)/shard_map/pallas_call | solution.py:43
  73.5 14.6 %all_to_all.46.refs_0_ = f32[32,16,128]{2,1,0:T(8,128)S(1)} all-to-all(f32[32,16,128]{2,1,0:T(8,128)S(1)} %get-tuple-element.76), channel_id=1, replica_groups=mesh['gx'=32,'gy'=16] {'gx'}, dimensions={0} | all-to-all | bytes 524288 | tf_op jit(solution)/shard_map/all_to_all | solution.py:414
  88.1 0.7 shard_map.69
  88.8 2.6 %collective-permute-start.4 = (f32[16,256]{1,0:T(8,128)S(1)}, f32[16,256]{1,0:T(8,128)S(1)}, u32[]{:S(2)}, u32[]{:S(2)}) collective-permute-start(f32[16,256]{1,0:T(8,128)S(1)} %get-tuple-element.81), channel_id=1, source_target_pairs={{0,1},{1,0},{2,3},{3,2},{4,5},{5,4},{6,7},{7,6},{8,9},{9,8},{10,11... | collective-permute-start | bytes 49160 | tf_op jit(solution)/shard_map/ppermute | solution.py:353
  91.4 0.7 collective-permute-start.5
  92.1 1.2 collective-permute-done.4.first_ref
  93.8 5.3 %collective-permute-start.6 = (f32[16,256]{1,0:T(8,128)S(1)}, f32[16,256]{1,0:T(8,128)S(1)}, u32[]{:S(2)}, u32[]{:S(2)}) collective-permute-start(f32[16,256]{1,0:T(8,128)S(1)} %get-tuple-element.86), channel_id=1, source_target_pairs={{0,1},{1,0},{2,3},{3,2},{4,5},{5,4},{6,7},{7,6},{8,9},{9,8},{10,11... | collective-permute-start | bytes 49160 | tf_op jit(solution)/shard_map/ppermute | solution.py:353
  99.1 0.7 collective-permute-start.7
  99.7 3.8 %collective-permute-start.8 = (f32[16,128]{1,0:T(8,128)S(1)}, f32[16,128]{1,0:T(8,128)S(1)}, u32[]{:S(2)}, u32[]{:S(2)}) collective-permute-start(f32[16,128]{1,0:T(8,128)S(1)} %get-tuple-element.88), channel_id=1, source_target_pairs={{0,16},{16,0},{32,48},{48,32},{64,80},{80,64},{96,112},{112,96},{1... | collective-permute-start | bytes 24584 | tf_op jit(solution)/shard_map/ppermute | solution.py:353
  103.6 1.9 collective-permute-start.9
  105.5 3.0 %collective-permute-done.9.refs_3_ = f32[16,128]{1,0:T(8,128)S(1)} collective-permute-done((f32[16,128]{1,0:T(8,128)S(1)}, f32[16,128]{1,0:T(8,128)S(1)}, u32[]{:S(2)}, u32[]{:S(2)}) %collective-permute-start.9) | collective-permute-done | bytes 8224 | tf_op jit(solution)/shard_map/ppermute | solution.py:353
  108.8 18.7 %all_to_all.47.refs_0_ = f32[16,8,128]{2,1,0:T(8,128)S(1)} all-to-all(f32[16,8,128]{2,1,0:T(8,128)S(1)} %get-tuple-element.90), channel_id=1, replica_groups=mesh['gx'=32,'gy'=16] {'gy'}, dimensions={0} | all-to-all | bytes 131072 | tf_op jit(solution)/shard_map/all_to_all | solution.py:405
  127.5 0.9 shard_map.72
  128.5 15.1 %all_to_all.48.refs_0_ = f32[32,16,128]{2,1,0:T(8,128)S(1)} all-to-all(f32[32,16,128]{2,1,0:T(8,128)S(1)} %shard_map.72), channel_id=1, replica_groups=mesh['gx'=32,'gy'=16] {'gx'}, dimensions={0} | all-to-all | bytes 524288 | tf_op jit(solution)/shard_map/all_to_all | solution.py:414
  143.6 0.7 shard_map.73
  144.3 2.4 collective-permute-start.10
  147.4 1.4 collective-permute-done.10.first_ref
  149.3 5.3 %collective-permute-start.12 = (f32[16,256]{1,0:T(8,128)S(1)}, f32[16,256]{1,0:T(8,128)S(1)}, u32[]{:S(2)}, u32[]{:S(2)}) collective-permute-start(f32[16,256]{1,0:T(8,128)S(1)} %get-tuple-element.100), channel_id=1, source_target_pairs={{0,1},{1,0},{2,3},{3,2},{4,5},{5,4},{6,7},{7,6},{8,9},{9,8},{10,11... | collective-permute-start | bytes 49160 | tf_op jit(solution)/shard_map/ppermute | solution.py:353
  155.2 3.8 %collective-permute-start.14 = (f32[16,128]{1,0:T(8,128)S(1)}, f32[16,128]{1,0:T(8,128)S(1)}, u32[]{:S(2)}, u32[]{:S(2)}) collective-permute-start(f32[16,128]{1,0:T(8,128)S(1)} %get-tuple-element.102), channel_id=1, source_target_pairs={{0,16},{16,0},{32,48},{48,32},{64,80},{80,64},{96,112},{112,96},{1... | collective-permute-start | bytes 24584 | tf_op jit(solution)/shard_map/ppermute | solution.py:353
  159.1 1.9 collective-permute-start.15
  161.0 3.0 %collective-permute-done.15.refs_3_ = f32[16,128]{1,0:T(8,128)S(1)} collective-permute-done((f32[16,128]{1,0:T(8,128)S(1)}, f32[16,128]{1,0:T(8,128)S(1)}, u32[]{:S(2)}, u32[]{:S(2)}) %collective-permute-start.15) | collective-permute-done | bytes 8224 | tf_op jit(solution)/shard_map/ppermute | solution.py:353
  164.3 18.7 %all_to_all.49.refs_0_ = f32[16,8,128]{2,1,0:T(8,128)S(1)} all-to-all(f32[16,8,128]{2,1,0:T(8,128)S(1)} %get-tuple-element.105), channel_id=1, replica_groups=mesh['gx'=32,'gy'=16] {'gy'}, dimensions={0} | all-to-all | bytes 131072 | tf_op jit(solution)/shard_map/all_to_all | solution.py:405
  183.0 0.9 shard_map.76
  183.9 15.1 %all_to_all.50.refs_0_ = f32[32,16,128]{2,1,0:T(8,128)S(1)} all-to-all(f32[32,16,128]{2,1,0:T(8,128)S(1)} %shard_map.76), channel_id=1, replica_groups=mesh['gx'=32,'gy'=16] {'gx'}, dimensions={0} | all-to-all | bytes 524288 | tf_op jit(solution)/shard_map/all_to_all | solution.py:414
  199.0 1.1 shard_map.77
  200.1 2.4 collective-permute-start.16
  203.2 1.4 collective-permute-done.16.first_ref
  205.0 5.3 %collective-permute-start.18 = (f32[16,256]{1,0:T(8,128)S(1)}, f32[16,256]{1,0:T(8,128)S(1)}, u32[]{:S(2)}, u32[]{:S(2)}) collective-permute-start(f32[16,256]{1,0:T(8,128)S(1)} %get-tuple-element.114), channel_id=1, source_target_pairs={{0,1},{1,0},{2,3},{3,2},{4,5},{5,4},{6,7},{7,6},{8,9},{9,8},{10,11... | collective-permute-start | bytes 49160 | tf_op jit(solution)/shard_map/ppermute | solution.py:353
  211.0 3.8 %collective-permute-start.20 = (f32[16,128]{1,0:T(8,128)S(1)}, f32[16,128]{1,0:T(8,128)S(1)}, u32[]{:S(2)}, u32[]{:S(2)}) collective-permute-start(f32[16,128]{1,0:T(8,128)S(1)} %get-tuple-element.116), channel_id=1, source_target_pairs={{0,16},{16,0},{32,48},{48,32},{64,80},{80,64},{96,112},{112,96},{1... | collective-permute-start | bytes 24584 | tf_op jit(solution)/shard_map/ppermute | solution.py:353
  214.8 1.9 collective-permute-start.21
  216.8 3.0 %collective-permute-done.21.refs_3_ = f32[16,128]{1,0:T(8,128)S(1)} collective-permute-done((f32[16,128]{1,0:T(8,128)S(1)}, f32[16,128]{1,0:T(8,128)S(1)}, u32[]{:S(2)}, u32[]{:S(2)}) %collective-permute-start.21) | collective-permute-done | bytes 8224 | tf_op jit(solution)/shard_map/ppermute | solution.py:353
  219.9 18.7 %all_to_all.51.gathered_ref = f32[16,8,128]{2,1,0:T(8,128)S(1)} all-to-all(f32[16,8,128]{2,1,0:T(8,128)S(1)} %shard_map.79), channel_id=1, replica_groups=mesh['gx'=32,'gy'=16] {'gy'}, dimensions={0} | all-to-all | bytes 131072 | tf_op jit(solution)/shard_map/all_to_all | solution.py:437
  238.6 13.8 %all_to_all.52.reduced_ref = f32[32,8,128]{2,1,0:T(8,128)S(1)} all-to-all(f32[32,8,128]{2,1,0:T(8,128)S(1)} %shard_map.80), channel_id=1, replica_groups=mesh['gx'=32,'gy'=16] {'gx'}, dimensions={0} | all-to-all | bytes 262144 | tf_op jit(solution)/shard_map/all_to_all | solution.py:439
  252.4 1.2 shard_map.81
  (36 shorter events, 5.2 us)
Async XLA Ops:
  0.0 1.6 copy-start.1
  1.6 0.7 copy-start.5
  7.4 11.3 %copy-start.2 = (f32[1,1,32,768]{3,2,1,0:T(8,128)S(1)}, f32[1,1,32,768]{3,2,1,0:T(8,128)}, u32[]{:S(2)}) copy-start(f32[1,1,32,768]{3,2,1,0:T(8,128)} %param.7) | copy-start | bytes 294916
  7.4 11.3 %copy-start.3 = (f32[1,1,16,768]{3,2,1,0:T(8,128)S(1)}, f32[1,1,16,768]{3,2,1,0:T(8,128)}, u32[]{:S(2)}) copy-start(f32[1,1,16,768]{3,2,1,0:T(8,128)} %param.8) | copy-start | bytes 147460
  7.4 11.3 %copy-start.4 = (s32[1,1,768]{2,1,0:T(1,128)S(1)}, s32[1,1,768]{2,1,0:T(1,128)}, u32[]{:S(2)}) copy-start(s32[1,1,768]{2,1,0:T(1,128)} %param.10) | copy-start | bytes 9220
  7.5 39.8 %all-to-all-start = ((f32[32,32,512]{2,1,0:T(8,128)}), f32[32,32,512]{2,1,0:T(8,128)}, u32[]{:S(2)}, u32[]{:S(2)}) async-start(f32[32,32,512]{2,1,0:T(8,128)} %get-tuple-element.71), calls=%async_computation | async-start | bytes 4194304 | tf_op jit(solution)/shard_map/all_to_all | solution.py:376
  19.5 12.8 %collective-permute-start = (f32[16,256]{1,0:T(8,128)S(1)}, f32[16,256]{1,0:T(8,128)S(1)}, u32[]{:S(2)}, u32[]{:S(2)}) collective-permute-start(f32[16,256]{1,0:T(8,128)S(1)} %get-tuple-element.65), channel_id=1, source_target_pairs={{0,1},{1,0},{2,3},{3,2},{4,5},{5,4},{6,7},{7,6},{8,9},{9,8},{10,11... | collective-permute-start | bytes 49160 | tf_op jit(solution)/shard_map/ppermute | solution.py:353
  21.5 10.9 %collective-permute-start.1 = (f32[16,256]{1,0:T(8,128)S(1)}, f32[16,256]{1,0:T(8,128)S(1)}, u32[]{:S(2)}, u32[]{:S(2)}) collective-permute-start(f32[16,256]{1,0:T(8,128)S(1)} %get-tuple-element.66), channel_id=1, source_target_pairs={{1,2},{2,1},{3,4},{4,3},{5,6},{6,5},{7,8},{8,7},{9,10},{10,9},{11,... | collective-permute-start | bytes 49160 | tf_op jit(solution)/shard_map/ppermute | solution.py:353
  22.1 10.2 %collective-permute-start.2 = (f32[48,128]{1,0:T(8,128)S(1)}, f32[48,128]{1,0:T(8,128)S(1)}, u32[]{:S(2)}, u32[]{:S(2)}) collective-permute-start(f32[48,128]{1,0:T(8,128)S(1)} %get-tuple-element.67), channel_id=1, source_target_pairs={{0,16},{16,0},{32,48},{48,32},{64,80},{80,64},{96,112},{112,96},{1... | collective-permute-start | bytes 73736 | tf_op jit(solution)/shard_map/ppermute | solution.py:353
  24.5 19.2 %collective-permute-start.3 = (f32[48,128]{1,0:T(8,128)S(1)}, f32[48,128]{1,0:T(8,128)S(1)}, u32[]{:S(2)}, u32[]{:S(2)}) collective-permute-start(f32[48,128]{1,0:T(8,128)S(1)} %get-tuple-element.68), channel_id=1, source_target_pairs={{16,32},{32,16},{48,64},{64,48},{80,96},{96,80},{112,128},{128,112... | collective-permute-start | bytes 73736 | tf_op jit(solution)/shard_map/ppermute | solution.py:353
  27.7 1.7 copy-start
  88.8 4.5 %collective-permute-start.4 = (f32[16,256]{1,0:T(8,128)S(1)}, f32[16,256]{1,0:T(8,128)S(1)}, u32[]{:S(2)}, u32[]{:S(2)}) collective-permute-start(f32[16,256]{1,0:T(8,128)S(1)} %get-tuple-element.81), channel_id=1, source_target_pairs={{0,1},{1,0},{2,3},{3,2},{4,5},{5,4},{6,7},{7,6},{8,9},{9,8},{10,11... | collective-permute-start | bytes 49160 | tf_op jit(solution)/shard_map/ppermute | solution.py:353
  91.4 1.9 collective-permute-start.5
  93.8 14.8 %collective-permute-start.6 = (f32[16,256]{1,0:T(8,128)S(1)}, f32[16,256]{1,0:T(8,128)S(1)}, u32[]{:S(2)}, u32[]{:S(2)}) collective-permute-start(f32[16,256]{1,0:T(8,128)S(1)} %get-tuple-element.86), channel_id=1, source_target_pairs={{0,1},{1,0},{2,3},{3,2},{4,5},{5,4},{6,7},{7,6},{8,9},{9,8},{10,11... | collective-permute-start | bytes 49160 | tf_op jit(solution)/shard_map/ppermute | solution.py:353
  99.1 9.5 %collective-permute-start.7 = (f32[16,256]{1,0:T(8,128)S(1)}, f32[16,256]{1,0:T(8,128)S(1)}, u32[]{:S(2)}, u32[]{:S(2)}) collective-permute-start(f32[16,256]{1,0:T(8,128)S(1)} %get-tuple-element.87), channel_id=1, source_target_pairs={{1,2},{2,1},{3,4},{4,3},{5,6},{6,5},{7,8},{8,7},{9,10},{10,9},{11,... | collective-permute-start | bytes 49160 | tf_op jit(solution)/shard_map/ppermute | solution.py:353
  99.7 5.7 %collective-permute-start.8 = (f32[16,128]{1,0:T(8,128)S(1)}, f32[16,128]{1,0:T(8,128)S(1)}, u32[]{:S(2)}, u32[]{:S(2)}) collective-permute-start(f32[16,128]{1,0:T(8,128)S(1)} %get-tuple-element.88), channel_id=1, source_target_pairs={{0,16},{16,0},{32,48},{48,32},{64,80},{80,64},{96,112},{112,96},{1... | collective-permute-start | bytes 24584 | tf_op jit(solution)/shard_map/ppermute | solution.py:353
  103.6 5.0 %collective-permute-start.9 = (f32[16,128]{1,0:T(8,128)S(1)}, f32[16,128]{1,0:T(8,128)S(1)}, u32[]{:S(2)}, u32[]{:S(2)}) collective-permute-start(f32[16,128]{1,0:T(8,128)S(1)} %get-tuple-element.89), channel_id=1, source_target_pairs={{16,32},{32,16},{48,64},{64,48},{80,96},{96,80},{112,128},{128,112... | collective-permute-start | bytes 24584 | tf_op jit(solution)/shard_map/ppermute | solution.py:353
  144.3 4.5 %collective-permute-start.10 = (f32[16,256]{1,0:T(8,128)S(1)}, f32[16,256]{1,0:T(8,128)S(1)}, u32[]{:S(2)}, u32[]{:S(2)}) collective-permute-start(f32[16,256]{1,0:T(8,128)S(1)} %get-tuple-element.97), channel_id=1, source_target_pairs={{0,1},{1,0},{2,3},{3,2},{4,5},{5,4},{6,7},{7,6},{8,9},{9,8},{10,11... | collective-permute-start | bytes 49160 | tf_op jit(solution)/shard_map/ppermute | solution.py:353
  146.7 2.1 collective-permute-start.11
  149.3 14.8 %collective-permute-start.12 = (f32[16,256]{1,0:T(8,128)S(1)}, f32[16,256]{1,0:T(8,128)S(1)}, u32[]{:S(2)}, u32[]{:S(2)}) collective-permute-start(f32[16,256]{1,0:T(8,128)S(1)} %get-tuple-element.100), channel_id=1, source_target_pairs={{0,1},{1,0},{2,3},{3,2},{4,5},{5,4},{6,7},{7,6},{8,9},{9,8},{10,11... | collective-permute-start | bytes 49160 | tf_op jit(solution)/shard_map/ppermute | solution.py:353
  154.6 9.5 %collective-permute-start.13 = (f32[16,256]{1,0:T(8,128)S(1)}, f32[16,256]{1,0:T(8,128)S(1)}, u32[]{:S(2)}, u32[]{:S(2)}) collective-permute-start(f32[16,256]{1,0:T(8,128)S(1)} %get-tuple-element.101), channel_id=1, source_target_pairs={{1,2},{2,1},{3,4},{4,3},{5,6},{6,5},{7,8},{8,7},{9,10},{10,9},{11,... | collective-permute-start | bytes 49160 | tf_op jit(solution)/shard_map/ppermute | solution.py:353
  155.2 5.7 %collective-permute-start.14 = (f32[16,128]{1,0:T(8,128)S(1)}, f32[16,128]{1,0:T(8,128)S(1)}, u32[]{:S(2)}, u32[]{:S(2)}) collective-permute-start(f32[16,128]{1,0:T(8,128)S(1)} %get-tuple-element.102), channel_id=1, source_target_pairs={{0,16},{16,0},{32,48},{48,32},{64,80},{80,64},{96,112},{112,96},{1... | collective-permute-start | bytes 24584 | tf_op jit(solution)/shard_map/ppermute | solution.py:353
  159.1 5.0 %collective-permute-start.15 = (f32[16,128]{1,0:T(8,128)S(1)}, f32[16,128]{1,0:T(8,128)S(1)}, u32[]{:S(2)}, u32[]{:S(2)}) collective-permute-start(f32[16,128]{1,0:T(8,128)S(1)} %get-tuple-element.103), channel_id=1, source_target_pairs={{16,32},{32,16},{48,64},{64,48},{80,96},{96,80},{112,128},{128,112... | collective-permute-start | bytes 24584 | tf_op jit(solution)/shard_map/ppermute | solution.py:353
  200.1 4.5 %collective-permute-start.16 = (f32[16,256]{1,0:T(8,128)S(1)}, f32[16,256]{1,0:T(8,128)S(1)}, u32[]{:S(2)}, u32[]{:S(2)}) collective-permute-start(f32[16,256]{1,0:T(8,128)S(1)} %get-tuple-element.111), channel_id=1, source_target_pairs={{0,1},{1,0},{2,3},{3,2},{4,5},{5,4},{6,7},{7,6},{8,9},{9,8},{10,11... | collective-permute-start | bytes 49160 | tf_op jit(solution)/shard_map/ppermute | solution.py:353
  202.5 2.1 collective-permute-start.17
  205.0 14.8 %collective-permute-start.18 = (f32[16,256]{1,0:T(8,128)S(1)}, f32[16,256]{1,0:T(8,128)S(1)}, u32[]{:S(2)}, u32[]{:S(2)}) collective-permute-start(f32[16,256]{1,0:T(8,128)S(1)} %get-tuple-element.114), channel_id=1, source_target_pairs={{0,1},{1,0},{2,3},{3,2},{4,5},{5,4},{6,7},{7,6},{8,9},{9,8},{10,11... | collective-permute-start | bytes 49160 | tf_op jit(solution)/shard_map/ppermute | solution.py:353
  210.3 9.5 %collective-permute-start.19 = (f32[16,256]{1,0:T(8,128)S(1)}, f32[16,256]{1,0:T(8,128)S(1)}, u32[]{:S(2)}, u32[]{:S(2)}) collective-permute-start(f32[16,256]{1,0:T(8,128)S(1)} %get-tuple-element.115), channel_id=1, source_target_pairs={{1,2},{2,1},{3,4},{4,3},{5,6},{6,5},{7,8},{8,7},{9,10},{10,9},{11,... | collective-permute-start | bytes 49160 | tf_op jit(solution)/shard_map/ppermute | solution.py:353
  211.0 5.7 %collective-permute-start.20 = (f32[16,128]{1,0:T(8,128)S(1)}, f32[16,128]{1,0:T(8,128)S(1)}, u32[]{:S(2)}, u32[]{:S(2)}) collective-permute-start(f32[16,128]{1,0:T(8,128)S(1)} %get-tuple-element.116), channel_id=1, source_target_pairs={{0,16},{16,0},{32,48},{48,32},{64,80},{80,64},{96,112},{112,96},{1... | collective-permute-start | bytes 24584 | tf_op jit(solution)/shard_map/ppermute | solution.py:353
  214.8 5.0 %collective-permute-start.21 = (f32[16,128]{1,0:T(8,128)S(1)}, f32[16,128]{1,0:T(8,128)S(1)}, u32[]{:S(2)}, u32[]{:S(2)}) collective-permute-start(f32[16,128]{1,0:T(8,128)S(1)} %get-tuple-element.117), channel_id=1, source_target_pairs={{16,32},{32,16},{48,64},{64,48},{80,96},{96,80},{112,128},{128,112... | collective-permute-start | bytes 24584 | tf_op jit(solution)/shard_map/ppermute | solution.py:353

commit v4 on v3

--- a/solution.py
+++ b/solution.py
@@ -113,22 +113,24 @@
 def outgoing(field, refs):
     odd_column, odd_row = parities()
     west, east, south, north = (field[:, a:b] for a, b in sides(field.shape[1]))
-    refs[0][...] = jnp.where(odd_column, west, east)
-    refs[1][...] = jnp.where(odd_column, east, west)
     if len(refs) > 2:
-        refs[2][...] = jnp.where(odd_row, south, north)
-        refs[3][...] = jnp.where(odd_row, north, south)
-
-
-def incoming(first, second, odd):
-    return jnp.where(odd, first, second), jnp.where(odd, second, first)
+        refs[0][...] = jnp.where(odd_row, north, south)
+        refs[3][...] = jnp.where(odd_row, south, north)
+        refs = refs[1:3]
+    refs[0][...] = jnp.where(odd_column, east, west)
+    refs[1][...] = jnp.where(odd_column, west, east)
+
+
+def incoming(far, near, odd):
+    return jnp.where(odd, near, far), jnp.where(odd, far, near)
 
 
 def joined(field, others):
     odd_column, odd_row = parities()
-    found = [*incoming(others[0], others[1], odd_column)]
+    columns = others[1:3] if len(others) > 2 else others
+    found = [*incoming(columns[0], columns[1], odd_column)]
     if len(others) > 2:
-        found += incoming(others[2], others[3], odd_row)
+        found += incoming(others[0], others[3], odd_row)
     parts = [
         field[:, start:stop] + other for (start, stop), other in zip(sides(field.shape[1]), found)
     ]
@@ -151,11 +153,11 @@
     frame_ref[:modes, :] = high
     frame_ref[modes:, :] = low
     field_ref[...] = moved[:loads]
-    outgoing(moved[:loads], edge_refs[:2])
+    outgoing(moved[:loads], edge_refs[1:3])
     odd_row = parities()[1]
     south, north = (moved[:, start:stop] for start, stop in sides(cells)[2:])
-    edge_refs[2][...] = jnp.where(odd_row, south, north)
-    edge_refs[3][...] = jnp.where(odd_row, north, south)
+    edge_refs[0][...] = jnp.where(odd_row, north, south)
+    edge_refs[3][...] = jnp.where(odd_row, south, north)
 
 
 def reorder_kernel(map_ref, schur_ref, token_ref, high_ref, low_ref):
@@ -185,18 +187,23 @@
     return pack(both[:modes] + both[modes:], loads)
 
 
+def flatten(coeffs, totals, out_ref):
+    rows = [coeffs[quad : quad + 1, :] for quad in range(coeffs.shape[0])] + totals
+    row = jnp.concatenate(rows, axis=1)
+    out_ref[...] = jnp.broadcast_to(row[None], out_ref.shape)
+
+
 def begin_kernel(own_ref, *refs):
     others = [ref[...] for ref in refs[:4]]
     frame_ref, residual_ref, out_ref, south_ref, north_ref = refs[4:]
     loads = own_ref.shape[0]
-    south, north = incoming(others[2], others[3], parities()[1])
+    south, north = incoming(others[0], others[3], parities()[1])
     south_ref[...] = stacked(south[loads:])
     north_ref[...] = stacked(north[loads:])
-    field = joined(own_ref[...], others[:2] + [other[:loads] for other in others[2:]])
+    field = joined(own_ref[...], [other[:loads] for other in others])
     residual_ref[...] = field
     coeffs = coefficients(field, frame_ref[...])
-    payload = jnp.concatenate([coeffs, jnp.zeros_like(coeffs)], axis=0)
-    out_ref[...] = jnp.broadcast_to(payload[None], out_ref.shape)
+    flatten(coeffs, [jnp.zeros((1, LANES), jnp.float32)] * 2, out_ref)
 
 
 def gather_kernel(more, own_ref, *refs):
@@ -210,13 +217,12 @@
         field_ref[...] = field
         coeffs = coefficients(field, frame_ref[...])
     else:
-        coeffs = jnp.zeros((4, LANES), jnp.float32)
+        coeffs = jnp.zeros((0, LANES), jnp.float32)
     totals = [
         row_of(jnp.sum(other * field, axis=1, keepdims=True), loads)
         for other in (residual_ref[...], field)
     ]
-    payload = jnp.concatenate([coeffs, *totals, jnp.zeros((2, LANES), jnp.float32)], axis=0)
-    out_ref[...] = jnp.broadcast_to(payload[None], out_ref.shape)
+    flatten(coeffs, totals, out_ref)
 
 
 def expanded(loads, gathered_ref, wide_ref):
@@ -224,7 +230,7 @@
     keep = sublane_mask(ROWS, loads)
     for column in range(gathered_ref.shape[0]):
         for quad in range(quads):
-            row = gathered_ref[column, quad : quad + 1, :]
+            row = gathered_ref[column, :, quad * LANES : (quad + 1) * LANES]
             start = (column * quads + quad) * ROWS
             wide_ref[start : start + ROWS, :] = jnp.where(keep, row, 0.0)
     wide = wide_ref[...]
@@ -232,7 +238,10 @@
     while shift >= loads:
         wide = wide + pltpu.roll(wide, shift, 1)
         shift //= 2
-    tail = jnp.sum(gathered_ref[...], axis=0)[quads:, :]
+    sums = jnp.sum(gathered_ref[:, :, quads * LANES :], axis=0)
+    tail = jnp.concatenate(
+        [sums[:, :LANES], sums[:, LANES:], jnp.zeros((2, LANES), jnp.float32)], axis=0
+    )
     return jnp.concatenate(split(wide), axis=1), tail
 
 
@@ -335,7 +344,7 @@
 def finish_kernel(reduced_ref, solution_ref, search_ref, map_ref, out_ref):
     loads, cells = solution_ref.shape
     sums = jnp.sum(reduced_ref[...], axis=0)
-    stride = column_of(sums[4:5, :] / (sums[5:6, :] + epsilon), loads)
+    stride = column_of(sums[:, :LANES] / (sums[:, LANES:] + epsilon), loads)
     result = solution_ref[...] + stride * search_ref[...]
     map_row = map_ref[...]
     for block in range(cells // MB):
@@ -344,9 +353,10 @@
 
 
 def exchange(edges):
+    swaps = (("gx", 1), ("gy", 1), ("gy", 0), ("gx", 0))
     found = []
-    for number, edge in enumerate(edges):
-        axis, start = ("gy", "gx")[number // 2], number % 2
+    chosen = swaps if len(edges) > 2 else swaps[1:3]
+    for edge, (axis, start) in zip(edges, chosen):
         pairs = []
         for low in range(start, lax.axis_size(axis) - 1, 2):
             pairs += [(low, low + 1), (low + 1, low)]
@@ -362,9 +372,12 @@
     modes = basis.shape[2]
     field = ((count, cells), f32)
     column_edges = [((count, EW), f32)] * 2
-    edges_of = column_edges + [((count, ES), f32)] * 2
+    row_edge = ((count, ES), f32)
+    edges_of = [row_edge, *column_edges, row_edge]
+    wide_edge = ((count + modes, ES), f32)
     packed = ((2 * ROWS, LANES), f32)
-    along = ((columns, ROWS, LANES), f32)
+    along = ((columns, 1, (modes // ROWS + 2) * LANES), f32)
+    along_last = ((columns, 1, 2 * LANES), f32)
     across = ((groups, 2 * ROWS, LANES), f32)
 
     routed, token = call(
@@ -378,9 +391,7 @@
 
     frame, own, *edges = call(
         prepare_kernel,
-        [((2 * modes, cells), bf16), field]
-        + column_edges
-        + [((count + modes, ES), f32)] * 2,
+        [((2 * modes, cells), bf16), field, wide_edge, *column_edges, wide_edge],
         [iface_map[0], basis[0, 0], loads[0, 0], token],
     )
     residual, payload, south, north = call(
@@ -430,12 +441,12 @@
         more = iteration < ITERS - 1
         found = call(
             functools.partial(gather_kernel, more),
-            [field] * more + [along],
+            [field, along] if more else [along_last],
             [local, *exchange(edges), residual] + [frame] * more,
         )
         image, payload = found if more else (None, found[0])
     gathered = lax.all_to_all(payload, "gy", 0, 0, tiled=True)
-    (partial,) = call(total_kernel, [((groups, ROWS, LANES), f32)], [gathered])
+    (partial,) = call(total_kernel, [((groups, 1, 2 * LANES), f32)], [gathered])
     reduced = lax.all_to_all(partial, "gx", 0, 0, tiled=True)
     (result,) = call(finish_kernel, [field], [reduced, solution, search, iface_map[0]])
     return result[None, None]

time: 255 us -> 249 us (0.976)
  waiting for transfers between devices: 27.7 us -> 18.9 us
  starting transfers between devices: 64 us -> 72.6 us
  blocking collectives: 138 us -> 132 us
    ppermute x22, waiting for transfers between devices: 24.5 us -> 15.7 us  [exchange(): found.append(lax.ppermute(edge, axis, pairs))]
    all_to_all x4, blocking collectives: 79.7 us -> 71 us  [per_device(): gathered = lax.all_to_all(payload, 'gy', 0, 0, tiled=True)]
    ppermute x22, starting transfers between devices: 52.6 us -> 61.2 us  [exchange(): found.append(lax.ppermute(edge, axis, pairs))]
    all_to_all x4, blocking collectives: 58.6 us -> 61.3 us  [per_device(): reduced = lax.all_to_all(partial, 'gx', 0, 0, tiled=True)]
where the time goes in v4:
time: 249 us; the launch traced here: 248 us
  blocking collectives  132 us (53%)
  starting transfers between devices  72.6 us (29%)
  Pallas kernels  19.4 us (8%)
  waiting for transfers between devices  18.9 us (8%)
  local copies, waits for them, and re-layouts  3.94 us (2%)
    all_to_all x4, blocking collectives, per_device(): gathered = lax.all_to_all(payload, 'gy', 0, 0, tiled=True)  71 us
    all_to_all x4, blocking collectives, per_device(): reduced = lax.all_to_all(partial, 'gx', 0, 0, tiled=True)  61.3 us
    ppermute x22, starting transfers between devices, exchange(): found.append(lax.ppermute(edge, axis, pairs))  61.2 us
    pallas_call x18, Pallas kernels, call(): pl.pallas_call(kernel, out_shape=outs, in_specs=specs or [VMEM] * len(arg...  19.4 us
    ppermute x22, waiting for transfers between devices, exchange(): found.append(lax.ppermute(edge, axis, pairs))  15.7 us
    all_to_all x1, starting transfers between devices, per_device(): matrix = lax.all_to_all(routed, 'gx', 0, 0, tiled=True)  11.3 us
  transfers between devices with their start and end apart: 23, of which 8 were waited for; matrix products, arithmetic and copies ran while one was open for 0% of the time, Pallas kernels for 2%

profile of v4, /device:TPU:1, one launch (start us, length us, event | category | flops | bytes accessed | tf_op | source)
XLA Modules:
  0.0 247.5 jit_solution(7692379023576558517)
XLA Ops:
  0.0 1.6 copy-done.1
  1.6 0.7 copy-done.5
  2.3 5.2 %shard_map.64 = (f32[32,32,512]{2,1,0:T(8,128)}, f32[8,128]{1,0:T(8,128)S(1)}) custom-call(s32[512]{0:T(512)S(1)} %copy-done.5, f32[32,16384]{1,0:T(8,128)S(1)} %copy-done.1), custom_call_target="tpu_custom_call" | custom-call | flops 1048576 | bytes 4200448 | tf_op jit(solution)/shard_map/pallas_call | solution.py:43
  7.5 11.3 %all-to-all-start = ((f32[32,32,512]{2,1,0:T(8,128)}), f32[32,32,512]{2,1,0:T(8,128)}, u32[]{:S(2)}, u32[]{:S(2)}) async-start(f32[32,32,512]{2,1,0:T(8,128)} %get-tuple-element.71), calls=%async_computation | async-start | bytes 4194304 | tf_op jit(solution)/shard_map/all_to_all | solution.py:389
  18.8 0.7 shard_map.65
  20.2 3.9 %collective-permute-start.2 = (f32[16,256]{1,0:T(8,128)S(1)}, f32[16,256]{1,0:T(8,128)S(1)}, u32[]{:S(2)}, u32[]{:S(2)}) collective-permute-start(f32[16,256]{1,0:T(8,128)S(1)} %get-tuple-element.67), channel_id=1, source_target_pairs={{0,1},{1,0},{2,3},{3,2},{4,5},{5,4},{6,7},{7,6},{8,9},{9,8},{10,11... | collective-permute-start | bytes 49160 | tf_op jit(solution)/shard_map/ppermute | solution.py:363
  24.1 4.1 %collective-permute-start = (f32[48,128]{1,0:T(8,128)S(1)}, f32[48,128]{1,0:T(8,128)S(1)}, u32[]{:S(2)}, u32[]{:S(2)}) collective-permute-start(f32[48,128]{1,0:T(8,128)S(1)} %get-tuple-element.65), channel_id=1, source_target_pairs={{16,32},{32,16},{48,64},{64,48},{80,96},{96,80},{112,128},{128,112... | collective-permute-start | bytes 73736 | tf_op jit(solution)/shard_map/ppermute | solution.py:363
  28.2 1.9 collective-permute-start.3
  30.2 1.7 copy-done
  31.8 2.9 %shard_map.67 = (bf16[768,768]{1,0:T(8,128)(2,1)S(1)}, bf16[768,768]{1,0:T(8,128)(2,1)S(1)}) custom-call(s32[1,768]{1,0:T(1,128)S(1)} %bitcast.10, f32[768,768]{1,0:T(8,128)S(1)} %bitcast.6, f32[8,128]{1,0:T(8,128)S(1)} %get-tuple-element.63.token_ref), custom_call_target="tpu_custom_call" | custom-call | flops 268435456 | bytes 4725760 | tf_op jit(solution)/shard_map/pallas_call | solution.py:43
  34.7 9.0 %collective-permute-done.refs_0_ = f32[48,128]{1,0:T(8,128)S(1)} collective-permute-done((f32[48,128]{1,0:T(8,128)S(1)}, f32[48,128]{1,0:T(8,128)S(1)}, u32[]{:S(2)}, u32[]{:S(2)}) %collective-permute-start) | collective-permute-done | bytes 24608 | tf_op jit(solution)/shard_map/ppermute | solution.py:363
  44.0 3.2 %all-to-all-done = f32[32,32,512]{2,1,0:T(8,128)} async-done(((f32[32,32,512]{2,1,0:T(8,128)}), f32[32,32,512]{2,1,0:T(8,128)}, u32[]{:S(2)}, u32[]{:S(2)}) %all-to-all-start) | async-done | bytes 2097184 | tf_op jit(solution)/shard_map/all_to_all | solution.py:389
  47.3 23.6 %all_to_all.45.refs_0_ = f32[16,1,768]{2,1,0:T(1,128)S(1)} all-to-all(f32[16,1,768]{2,1,0:T(1,128)S(1)} %get-tuple-element.74), channel_id=1, replica_groups=mesh['gx'=32,'gy'=16] {'gy'}, dimensions={0} | all-to-all | bytes 98304 | tf_op jit(solution)/shard_map/all_to_all | solution.py:416
  70.9 2.6 %shard_map.68 = (f32[32,16,128]{2,1,0:T(8,128)S(1)}, bf16[1024,512]{1,0:T(8,128)(2,1)S(1)}, bf16[1024,512]{1,0:T(8,128)(2,1)S(1)}) custom-call(f32[16,1,768]{2,1,0:T(1,128)S(1)} %all_to_all.45.refs_0_, f32[1024,512]{1,0:T(8,128)} %bitcast.3.refs_1_), custom_call_target="tpu_custom_call" | custom-call | flops 536870912 | bytes 4505600 | tf_op jit(solution)/shard_map/pallas_call | solution.py:43
  73.4 14.2 %all_to_all.46.refs_0_ = f32[32,16,128]{2,1,0:T(8,128)S(1)} all-to-all(f32[32,16,128]{2,1,0:T(8,128)S(1)} %get-tuple-element.76), channel_id=1, replica_groups=mesh['gx'=32,'gy'=16] {'gx'}, dimensions={0} | all-to-all | bytes 524288 | tf_op jit(solution)/shard_map/all_to_all | solution.py:425
  87.7 0.7 shard_map.69
  88.4 0.7 collective-permute-start.4
  89.1 4.1 %collective-permute-start.5 = (f32[16,256]{1,0:T(8,128)S(1)}, f32[16,256]{1,0:T(8,128)S(1)}, u32[]{:S(2)}, u32[]{:S(2)}) collective-permute-start(f32[16,256]{1,0:T(8,128)S(1)} %get-tuple-element.82), channel_id=1, source_target_pairs={{0,1},{1,0},{2,3},{3,2},{4,5},{5,4},{6,7},{7,6},{8,9},{9,8},{10,11... | collective-permute-start | bytes 49160 | tf_op jit(solution)/shard_map/ppermute | solution.py:363
  93.3 1.1 collective-permute-done.5.second_ref
  94.8 0.7 collective-permute-start.7
  95.5 5.6 %collective-permute-start.8 = (f32[16,256]{1,0:T(8,128)S(1)}, f32[16,256]{1,0:T(8,128)S(1)}, u32[]{:S(2)}, u32[]{:S(2)}) collective-permute-start(f32[16,256]{1,0:T(8,128)S(1)} %get-tuple-element.88), channel_id=1, source_target_pairs={{0,1},{1,0},{2,3},{3,2},{4,5},{5,4},{6,7},{7,6},{8,9},{9,8},{10,11... | collective-permute-start | bytes 49160 | tf_op jit(solution)/shard_map/ppermute | solution.py:363
  101.1 3.9 %collective-permute-start.6 = (f32[16,128]{1,0:T(8,128)S(1)}, f32[16,128]{1,0:T(8,128)S(1)}, u32[]{:S(2)}, u32[]{:S(2)}) collective-permute-start(f32[16,128]{1,0:T(8,128)S(1)} %get-tuple-element.86), channel_id=1, source_target_pairs={{16,32},{32,16},{48,64},{64,48},{80,96},{96,80},{112,128},{128,112... | collective-permute-start | bytes 24584 | tf_op jit(solution)/shard_map/ppermute | solution.py:363
  105.1 1.9 collective-permute-start.9
  107.0 1.1 collective-permute-done.9.refs_3_
  108.4 15.8 %all_to_all.47.refs_0_ = f32[16,1,768]{2,1,0:T(1,128)S(1)} all-to-all(f32[16,1,768]{2,1,0:T(1,128)S(1)} %get-tuple-element.90), channel_id=1, replica_groups=mesh['gx'=32,'gy'=16] {'gy'}, dimensions={0} | all-to-all | bytes 98304 | tf_op jit(solution)/shard_map/all_to_all | solution.py:416
  124.3 0.9 shard_map.72
  125.2 16.3 %all_to_all.48.refs_0_ = f32[32,16,128]{2,1,0:T(8,128)S(1)} all-to-all(f32[32,16,128]{2,1,0:T(8,128)S(1)} %shard_map.72), channel_id=1, replica_groups=mesh['gx'=32,'gy'=16] {'gx'}, dimensions={0} | all-to-all | bytes 524288 | tf_op jit(solution)/shard_map/all_to_all | solution.py:425
  141.6 0.7 shard_map.73
  142.3 0.7 collective-permute-start.10
  143.0 4.1 %collective-permute-start.11 = (f32[16,256]{1,0:T(8,128)S(1)}, f32[16,256]{1,0:T(8,128)S(1)}, u32[]{:S(2)}, u32[]{:S(2)}) collective-permute-start(f32[16,256]{1,0:T(8,128)S(1)} %get-tuple-element.98), channel_id=1, source_target_pairs={{0,1},{1,0},{2,3},{3,2},{4,5},{5,4},{6,7},{7,6},{8,9},{9,8},{10,11... | collective-permute-start | bytes 49160 | tf_op jit(solution)/shard_map/ppermute | solution.py:363
  147.1 1.1 collective-permute-done.11.second_ref
  149.4 5.6 %collective-permute-start.14 = (f32[16,256]{1,0:T(8,128)S(1)}, f32[16,256]{1,0:T(8,128)S(1)}, u32[]{:S(2)}, u32[]{:S(2)}) collective-permute-start(f32[16,256]{1,0:T(8,128)S(1)} %get-tuple-element.102), channel_id=1, source_target_pairs={{0,1},{1,0},{2,3},{3,2},{4,5},{5,4},{6,7},{7,6},{8,9},{9,8},{10,11... | collective-permute-start | bytes 49160 | tf_op jit(solution)/shard_map/ppermute | solution.py:363
  155.0 3.9 %collective-permute-start.12 = (f32[16,128]{1,0:T(8,128)S(1)}, f32[16,128]{1,0:T(8,128)S(1)}, u32[]{:S(2)}, u32[]{:S(2)}) collective-permute-start(f32[16,128]{1,0:T(8,128)S(1)} %get-tuple-element.100), channel_id=1, source_target_pairs={{16,32},{32,16},{48,64},{64,48},{80,96},{96,80},{112,128},{128,112... | collective-permute-start | bytes 24584 | tf_op jit(solution)/shard_map/ppermute | solution.py:363
  158.9 1.9 collective-permute-start.15
  160.8 1.1 collective-permute-done.15.refs_3_
  162.3 15.9 %all_to_all.49.refs_0_ = f32[16,1,768]{2,1,0:T(1,128)S(1)} all-to-all(f32[16,1,768]{2,1,0:T(1,128)S(1)} %get-tuple-element.105), channel_id=1, replica_groups=mesh['gx'=32,'gy'=16] {'gy'}, dimensions={0} | all-to-all | bytes 98304 | tf_op jit(solution)/shard_map/all_to_all | solution.py:416
  178.1 0.9 shard_map.76
  179.1 16.3 %all_to_all.50.refs_0_ = f32[32,16,128]{2,1,0:T(8,128)S(1)} all-to-all(f32[32,16,128]{2,1,0:T(8,128)S(1)} %shard_map.76), channel_id=1, replica_groups=mesh['gx'=32,'gy'=16] {'gx'}, dimensions={0} | all-to-all | bytes 524288 | tf_op jit(solution)/shard_map/all_to_all | solution.py:425
  195.4 1.1 shard_map.77
  197.2 4.1 %collective-permute-start.17 = (f32[16,256]{1,0:T(8,128)S(1)}, f32[16,256]{1,0:T(8,128)S(1)}, u32[]{:S(2)}, u32[]{:S(2)}) collective-permute-start(f32[16,256]{1,0:T(8,128)S(1)} %get-tuple-element.112), channel_id=1, source_target_pairs={{0,1},{1,0},{2,3},{3,2},{4,5},{5,4},{6,7},{7,6},{8,9},{9,8},{10,11... | collective-permute-start | bytes 49160 | tf_op jit(solution)/shard_map/ppermute | solution.py:363
  201.3 1.1 collective-permute-done.17.second_ref
  203.5 5.6 %collective-permute-start.20 = (f32[16,256]{1,0:T(8,128)S(1)}, f32[16,256]{1,0:T(8,128)S(1)}, u32[]{:S(2)}, u32[]{:S(2)}) collective-permute-start(f32[16,256]{1,0:T(8,128)S(1)} %get-tuple-element.116), channel_id=1, source_target_pairs={{0,1},{1,0},{2,3},{3,2},{4,5},{5,4},{6,7},{7,6},{8,9},{9,8},{10,11... | collective-permute-start | bytes 49160 | tf_op jit(solution)/shard_map/ppermute | solution.py:363
  209.1 3.9 %collective-permute-start.18 = (f32[16,128]{1,0:T(8,128)S(1)}, f32[16,128]{1,0:T(8,128)S(1)}, u32[]{:S(2)}, u32[]{:S(2)}) collective-permute-start(f32[16,128]{1,0:T(8,128)S(1)} %get-tuple-element.114), channel_id=1, source_target_pairs={{16,32},{32,16},{48,64},{64,48},{80,96},{96,80},{112,128},{128,112... | collective-permute-start | bytes 24584 | tf_op jit(solution)/shard_map/ppermute | solution.py:363
  213.1 1.9 collective-permute-start.21
  215.0 1.1 collective-permute-done.21.refs_3_
  216.2 15.7 %all_to_all.51.gathered_ref = f32[16,1,256]{2,1,0:T(1,128)S(1)} all-to-all(f32[16,1,256]{2,1,0:T(1,128)S(1)} %shard_map.79), channel_id=1, replica_groups=mesh['gx'=32,'gy'=16] {'gy'}, dimensions={0} | all-to-all | bytes 32768 | tf_op jit(solution)/shard_map/all_to_all | solution.py:448
  232.0 14.4 %all_to_all.52.reduced_ref = f32[32,1,256]{2,1,0:T(1,128)S(1)} all-to-all(f32[32,1,256]{2,1,0:T(1,128)S(1)} %shard_map.80), channel_id=1, replica_groups=mesh['gx'=32,'gy'=16] {'gx'}, dimensions={0} | all-to-all | bytes 65536 | tf_op jit(solution)/shard_map/all_to_all | solution.py:450
  246.4 1.2 shard_map.81
  (36 shorter events, 5.2 us)
Async XLA Ops:
  0.0 1.6 copy-start.1
  1.6 0.7 copy-start.5
  7.4 11.3 %copy-start.2 = (f32[1,1,32,768]{3,2,1,0:T(8,128)S(1)}, f32[1,1,32,768]{3,2,1,0:T(8,128)}, u32[]{:S(2)}) copy-start(f32[1,1,32,768]{3,2,1,0:T(8,128)} %param.7) | copy-start | bytes 294916
  7.4 11.3 %copy-start.3 = (f32[1,1,16,768]{3,2,1,0:T(8,128)S(1)}, f32[1,1,16,768]{3,2,1,0:T(8,128)}, u32[]{:S(2)}) copy-start(f32[1,1,16,768]{3,2,1,0:T(8,128)} %param.8) | copy-start | bytes 147460
  7.4 11.3 %copy-start.4 = (s32[1,1,768]{2,1,0:T(1,128)S(1)}, s32[1,1,768]{2,1,0:T(1,128)}, u32[]{:S(2)}) copy-start(s32[1,1,768]{2,1,0:T(1,128)} %param.10) | copy-start | bytes 9220
  7.5 39.8 %all-to-all-start = ((f32[32,32,512]{2,1,0:T(8,128)}), f32[32,32,512]{2,1,0:T(8,128)}, u32[]{:S(2)}, u32[]{:S(2)}) async-start(f32[32,32,512]{2,1,0:T(8,128)} %get-tuple-element.71), calls=%async_computation | async-start | bytes 4194304 | tf_op jit(solution)/shard_map/all_to_all | solution.py:389
  19.5 15.2 %collective-permute-start.1 = (f32[16,256]{1,0:T(8,128)S(1)}, f32[16,256]{1,0:T(8,128)S(1)}, u32[]{:S(2)}, u32[]{:S(2)}) collective-permute-start(f32[16,256]{1,0:T(8,128)S(1)} %get-tuple-element.66), channel_id=1, source_target_pairs={{1,2},{2,1},{3,4},{4,3},{5,6},{6,5},{7,8},{8,7},{9,10},{10,9},{11,... | collective-permute-start | bytes 49160 | tf_op jit(solution)/shard_map/ppermute | solution.py:363
  20.2 14.5 %collective-permute-start.2 = (f32[16,256]{1,0:T(8,128)S(1)}, f32[16,256]{1,0:T(8,128)S(1)}, u32[]{:S(2)}, u32[]{:S(2)}) collective-permute-start(f32[16,256]{1,0:T(8,128)S(1)} %get-tuple-element.67), channel_id=1, source_target_pairs={{0,1},{1,0},{2,3},{3,2},{4,5},{5,4},{6,7},{7,6},{8,9},{9,8},{10,11... | collective-permute-start | bytes 49160 | tf_op jit(solution)/shard_map/ppermute | solution.py:363
  24.1 19.6 %collective-permute-start = (f32[48,128]{1,0:T(8,128)S(1)}, f32[48,128]{1,0:T(8,128)S(1)}, u32[]{:S(2)}, u32[]{:S(2)}) collective-permute-start(f32[48,128]{1,0:T(8,128)S(1)} %get-tuple-element.65), channel_id=1, source_target_pairs={{16,32},{32,16},{48,64},{64,48},{80,96},{96,80},{112,128},{128,112... | collective-permute-start | bytes 73736 | tf_op jit(solution)/shard_map/ppermute | solution.py:363
  28.2 15.5 %collective-permute-start.3 = (f32[48,128]{1,0:T(8,128)S(1)}, f32[48,128]{1,0:T(8,128)S(1)}, u32[]{:S(2)}, u32[]{:S(2)}) collective-permute-start(f32[48,128]{1,0:T(8,128)S(1)} %get-tuple-element.68), channel_id=1, source_target_pairs={{0,16},{16,0},{32,48},{48,32},{64,80},{80,64},{96,112},{112,96},{1... | collective-permute-start | bytes 73736 | tf_op jit(solution)/shard_map/ppermute | solution.py:363
  30.1 1.7 copy-start
  88.4 4.8 %collective-permute-start.4 = (f32[16,256]{1,0:T(8,128)S(1)}, f32[16,256]{1,0:T(8,128)S(1)}, u32[]{:S(2)}, u32[]{:S(2)}) collective-permute-start(f32[16,256]{1,0:T(8,128)S(1)} %get-tuple-element.81), channel_id=1, source_target_pairs={{1,2},{2,1},{3,4},{4,3},{5,6},{6,5},{7,8},{8,7},{9,10},{10,9},{11,... | collective-permute-start | bytes 49160 | tf_op jit(solution)/shard_map/ppermute | solution.py:363
  89.1 5.3 %collective-permute-start.5 = (f32[16,256]{1,0:T(8,128)S(1)}, f32[16,256]{1,0:T(8,128)S(1)}, u32[]{:S(2)}, u32[]{:S(2)}) collective-permute-start(f32[16,256]{1,0:T(8,128)S(1)} %get-tuple-element.82), channel_id=1, source_target_pairs={{0,1},{1,0},{2,3},{3,2},{4,5},{5,4},{6,7},{7,6},{8,9},{9,8},{10,11... | collective-permute-start | bytes 49160 | tf_op jit(solution)/shard_map/ppermute | solution.py:363
  94.8 13.3 %collective-permute-start.7 = (f32[16,256]{1,0:T(8,128)S(1)}, f32[16,256]{1,0:T(8,128)S(1)}, u32[]{:S(2)}, u32[]{:S(2)}) collective-permute-start(f32[16,256]{1,0:T(8,128)S(1)} %get-tuple-element.87), channel_id=1, source_target_pairs={{1,2},{2,1},{3,4},{4,3},{5,6},{6,5},{7,8},{8,7},{9,10},{10,9},{11,... | collective-permute-start | bytes 49160 | tf_op jit(solution)/shard_map/ppermute | solution.py:363
  95.5 12.6 %collective-permute-start.8 = (f32[16,256]{1,0:T(8,128)S(1)}, f32[16,256]{1,0:T(8,128)S(1)}, u32[]{:S(2)}, u32[]{:S(2)}) collective-permute-start(f32[16,256]{1,0:T(8,128)S(1)} %get-tuple-element.88), channel_id=1, source_target_pairs={{0,1},{1,0},{2,3},{3,2},{4,5},{5,4},{6,7},{7,6},{8,9},{9,8},{10,11... | collective-permute-start | bytes 49160 | tf_op jit(solution)/shard_map/ppermute | solution.py:363
  101.1 5.9 %collective-permute-start.6 = (f32[16,128]{1,0:T(8,128)S(1)}, f32[16,128]{1,0:T(8,128)S(1)}, u32[]{:S(2)}, u32[]{:S(2)}) collective-permute-start(f32[16,128]{1,0:T(8,128)S(1)} %get-tuple-element.86), channel_id=1, source_target_pairs={{16,32},{32,16},{48,64},{64,48},{80,96},{96,80},{112,128},{128,112... | collective-permute-start | bytes 24584 | tf_op jit(solution)/shard_map/ppermute | solution.py:363
  105.1 3.1 %collective-permute-start.9 = (f32[16,128]{1,0:T(8,128)S(1)}, f32[16,128]{1,0:T(8,128)S(1)}, u32[]{:S(2)}, u32[]{:S(2)}) collective-permute-start(f32[16,128]{1,0:T(8,128)S(1)} %get-tuple-element.89), channel_id=1, source_target_pairs={{0,16},{16,0},{32,48},{48,32},{64,80},{80,64},{96,112},{112,96},{1... | collective-permute-start | bytes 24584 | tf_op jit(solution)/shard_map/ppermute | solution.py:363
  142.3 4.8 %collective-permute-start.10 = (f32[16,256]{1,0:T(8,128)S(1)}, f32[16,256]{1,0:T(8,128)S(1)}, u32[]{:S(2)}, u32[]{:S(2)}) collective-permute-start(f32[16,256]{1,0:T(8,128)S(1)} %get-tuple-element.97), channel_id=1, source_target_pairs={{1,2},{2,1},{3,4},{4,3},{5,6},{6,5},{7,8},{8,7},{9,10},{10,9},{11,... | collective-permute-start | bytes 49160 | tf_op jit(solution)/shard_map/ppermute | solution.py:363
  143.0 5.2 %collective-permute-start.11 = (f32[16,256]{1,0:T(8,128)S(1)}, f32[16,256]{1,0:T(8,128)S(1)}, u32[]{:S(2)}, u32[]{:S(2)}) collective-permute-start(f32[16,256]{1,0:T(8,128)S(1)} %get-tuple-element.98), channel_id=1, source_target_pairs={{0,1},{1,0},{2,3},{3,2},{4,5},{5,4},{6,7},{7,6},{8,9},{9,8},{10,11... | collective-permute-start | bytes 49160 | tf_op jit(solution)/shard_map/ppermute | solution.py:363
  148.7 13.3 %collective-permute-start.13 = (f32[16,256]{1,0:T(8,128)S(1)}, f32[16,256]{1,0:T(8,128)S(1)}, u32[]{:S(2)}, u32[]{:S(2)}) collective-permute-start(f32[16,256]{1,0:T(8,128)S(1)} %get-tuple-element.101), channel_id=1, source_target_pairs={{1,2},{2,1},{3,4},{4,3},{5,6},{6,5},{7,8},{8,7},{9,10},{10,9},{11,... | collective-permute-start | bytes 49160 | tf_op jit(solution)/shard_map/ppermute | solution.py:363
  149.4 12.6 %collective-permute-start.14 = (f32[16,256]{1,0:T(8,128)S(1)}, f32[16,256]{1,0:T(8,128)S(1)}, u32[]{:S(2)}, u32[]{:S(2)}) collective-permute-start(f32[16,256]{1,0:T(8,128)S(1)} %get-tuple-element.102), channel_id=1, source_target_pairs={{0,1},{1,0},{2,3},{3,2},{4,5},{5,4},{6,7},{7,6},{8,9},{9,8},{10,11... | collective-permute-start | bytes 49160 | tf_op jit(solution)/shard_map/ppermute | solution.py:363
  155.0 5.9 %collective-permute-start.12 = (f32[16,128]{1,0:T(8,128)S(1)}, f32[16,128]{1,0:T(8,128)S(1)}, u32[]{:S(2)}, u32[]{:S(2)}) collective-permute-start(f32[16,128]{1,0:T(8,128)S(1)} %get-tuple-element.100), channel_id=1, source_target_pairs={{16,32},{32,16},{48,64},{64,48},{80,96},{96,80},{112,128},{128,112... | collective-permute-start | bytes 24584 | tf_op jit(solution)/shard_map/ppermute | solution.py:363
  158.9 3.1 %collective-permute-start.15 = (f32[16,128]{1,0:T(8,128)S(1)}, f32[16,128]{1,0:T(8,128)S(1)}, u32[]{:S(2)}, u32[]{:S(2)}) collective-permute-start(f32[16,128]{1,0:T(8,128)S(1)} %get-tuple-element.103), channel_id=1, source_target_pairs={{0,16},{16,0},{32,48},{48,32},{64,80},{80,64},{96,112},{112,96},{1... | collective-permute-start | bytes 24584 | tf_op jit(solution)/shard_map/ppermute | solution.py:363
  196.5 4.8 %collective-permute-start.16 = (f32[16,256]{1,0:T(8,128)S(1)}, f32[16,256]{1,0:T(8,128)S(1)}, u32[]{:S(2)}, u32[]{:S(2)}) collective-permute-start(f32[16,256]{1,0:T(8,128)S(1)} %get-tuple-element.111), channel_id=1, source_target_pairs={{1,2},{2,1},{3,4},{4,3},{5,6},{6,5},{7,8},{8,7},{9,10},{10,9},{11,... | collective-permute-start | bytes 49160 | tf_op jit(solution)/shard_map/ppermute | solution.py:363
  197.2 5.2 %collective-permute-start.17 = (f32[16,256]{1,0:T(8,128)S(1)}, f32[16,256]{1,0:T(8,128)S(1)}, u32[]{:S(2)}, u32[]{:S(2)}) collective-permute-start(f32[16,256]{1,0:T(8,128)S(1)} %get-tuple-element.112), channel_id=1, source_target_pairs={{0,1},{1,0},{2,3},{3,2},{4,5},{5,4},{6,7},{7,6},{8,9},{9,8},{10,11... | collective-permute-start | bytes 49160 | tf_op jit(solution)/shard_map/ppermute | solution.py:363
  202.9 13.3 %collective-permute-start.19 = (f32[16,256]{1,0:T(8,128)S(1)}, f32[16,256]{1,0:T(8,128)S(1)}, u32[]{:S(2)}, u32[]{:S(2)}) collective-permute-start(f32[16,256]{1,0:T(8,128)S(1)} %get-tuple-element.115), channel_id=1, source_target_pairs={{1,2},{2,1},{3,4},{4,3},{5,6},{6,5},{7,8},{8,7},{9,10},{10,9},{11,... | collective-permute-start | bytes 49160 | tf_op jit(solution)/shard_map/ppermute | solution.py:363
  203.5 12.6 %collective-permute-start.20 = (f32[16,256]{1,0:T(8,128)S(1)}, f32[16,256]{1,0:T(8,128)S(1)}, u32[]{:S(2)}, u32[]{:S(2)}) collective-permute-start(f32[16,256]{1,0:T(8,128)S(1)} %get-tuple-element.116), channel_id=1, source_target_pairs={{0,1},{1,0},{2,3},{3,2},{4,5},{5,4},{6,7},{7,6},{8,9},{9,8},{10,11... | collective-permute-start | bytes 49160 | tf_op jit(solution)/shard_map/ppermute | solution.py:363
  209.1 5.9 %collective-permute-start.18 = (f32[16,128]{1,0:T(8,128)S(1)}, f32[16,128]{1,0:T(8,128)S(1)}, u32[]{:S(2)}, u32[]{:S(2)}) collective-permute-start(f32[16,128]{1,0:T(8,128)S(1)} %get-tuple-element.114), channel_id=1, source_target_pairs={{16,32},{32,16},{48,64},{64,48},{80,96},{96,80},{112,128},{128,112... | collective-permute-start | bytes 24584 | tf_op jit(solution)/shard_map/ppermute | solution.py:363
  213.1 3.1 %collective-permute-start.21 = (f32[16,128]{1,0:T(8,128)S(1)}, f32[16,128]{1,0:T(8,128)S(1)}, u32[]{:S(2)}, u32[]{:S(2)}) collective-permute-start(f32[16,128]{1,0:T(8,128)S(1)} %get-tuple-element.117), channel_id=1, source_target_pairs={{0,16},{16,0},{32,48},{48,32},{64,80},{80,64},{96,112},{112,96},{1... | collective-permute-start | bytes 24584 | tf_op jit(solution)/shard_map/ppermute | solution.py:363
